TPU v7x, 128 devices: a whole 4x4x4 slice. The times are simulated.
128 devices in a mesh: section: 8 (over x, core), ctx: 16 (over z, y).
Axes of the slice: x: 4, y: 4, z: 4, core: 2. Of those that a mesh axis runs over, the one named last changes fastest.
Arguments:
- carried_stream: float32 [8, 2048, 4096], P('section', 'ctx'), may hold values from -6 to 6
- arrival_queue: bfloat16 [2, 2048, 4096], P(None, 'ctx'), may hold values from -6 to 6
- scaling_factors: float32 [8, 4096], P('section'), may hold values from 0.25 to 1.75
- lookup_projection: bfloat16 [8, 4096, 512], P('section', 'ctx'), may hold values from -22 to 22
- content_projection: bfloat16 [8, 4096, 512], P('section', 'ctx'), may hold values from -0.1875 to 0.1875
- packed_span_lengths: int32 [10, 8], replicated, may hold values from 1 to 1024, 2048 in all within a row
- entry_permutation: int32 [2], replicated, may hold values from 0 to 1, each once
Outputs:
- produced: bfloat16 [2, 8, 2048, 4096], P(None, 'section', 'ctx')
Inputs may be any that keep to these rules, and one draw needn't show every extreme that they name: `packed_span_lengths`: each row holds positive lengths summing to 2048, the largest exactly 1024. `entry_permutation`: a permutation of 0 to 1.
All inputs are finite; a program needn't handle non-finite values.
Results may differ from a plain program's by a relative error of at most 0.0082.
The roundings to bfloat16 on the way count: a program that leaves them out, or rounds other values in their place, can miss the bound.
Values may be sent and summed in bfloat16 or wider, within the bound.
No kernel may reach another device: no remote copies, remote signals or barrier semaphores. Data moves between devices by JAX's collectives and lax.ppermute only.
A program may use at most 128 MiB of HBM per device.

v0:
```python
import jax
import jax.numpy as jnp
from jax import lax
from jax.sharding import PartitionSpec as P

HEAD_SIZE = 128
QUERY_HEADS = 32
KEY_VALUE_HEADS = 4
W = 2


EPSILON = 1e-05
MASK_FLOOR = -1e30


def shifted(value, axis, steps):
    count = lax.axis_size(axis)
    initial, last = (max(0, -steps), min(count, count - steps))
    return lax.ppermute(value, axis, [(source, source + steps) for source in range(initial, last)])


def segment_ids(lengths, positions):
    ends = jnp.cumsum(lengths)
    return jnp.sum((positions[:, None] >= ends[None, :]).astype(jnp.int32), axis=1)


def accumulate(carry, query_rows_set, key_portion, value_portion, allowed):
    highest, totals, mixed = carry
    item_count = key_portion.shape[0]
    scores = jnp.einsum(
        "tgjd,sgd->gjts",
        query_rows_set,
        key_portion.reshape(item_count, KEY_VALUE_HEADS, HEAD_SIZE),
        preferred_element_type=jnp.float32,
    ) * HEAD_SIZE ** (-0.5)
    scores = jnp.where(allowed[None, None], scores, MASK_FLOOR)
    new_high = jnp.maximum(highest, jnp.max(scores, axis=-1))
    weights = jnp.where(allowed[None, None], jnp.exp(scores - new_high[..., None]), 0.0)
    totals = jnp.sum(weights, axis=-1)
    mixed = jnp.einsum(
        "gjts,sgd->gjtd",
        weights,
        value_portion.reshape(item_count, KEY_VALUE_HEADS, HEAD_SIZE).astype(jnp.float32),
        precision=lax.Precision.HIGHEST,
    )
    return (new_high, totals, mixed)


def shards(
    carried_stream,
    arrival_queue,
    scaling_factors,
    lookup_projection,
    content_projection,
    packed_span_lengths,
    entry_permutation,
):
    skip_channel = carried_stream[0]
    gain = scaling_factors[0]
    local_rows = skip_channel.shape[0]
    phase_count = lax.axis_size("section")
    phase_index = lax.axis_index("section")
    context_index = lax.axis_index("ctx")
    key_rows = lookup_projection[0]
    value_rows = content_projection[0]
    key_full, value_full = (
        lax.all_gather(key_rows, "ctx", axis=0, tiled=True),
        lax.all_gather(value_rows, "ctx", axis=0, tiled=True),
    )
    query_positions = context_index * local_rows + jnp.arange(local_rows, dtype=jnp.int32)
    head_groups = QUERY_HEADS // KEY_VALUE_HEADS
    produced = []
    for tick in range(W):
        if tick > 0:
            arrived = shifted(skip_channel, "section", 1)
            chosen = lax.dynamic_index_in_dim(entry_permutation, tick - 1, 0, keepdims=False)
            first_input = lax.dynamic_index_in_dim(arrival_queue, chosen, 0, keepdims=False).astype(
                jnp.float32
            )
            skip_channel = jnp.where(phase_index == 0, first_input, arrived)
        slot_index = jnp.clip(tick - phase_index - 1, 0, W - 1)
        entered_sequence = phase_count + lax.dynamic_index_in_dim(
            entry_permutation, slot_index, 0, keepdims=False
        )
        sequence = jnp.where(phase_index >= tick, phase_index - tick, entered_sequence)
        lengths = lax.dynamic_index_in_dim(packed_span_lengths, sequence, 0, keepdims=False)
        query_segments = segment_ids(lengths, query_positions)
        mean_square = jnp.mean(skip_channel * skip_channel, axis=-1, keepdims=True)
        normalized_input = (skip_channel * lax.rsqrt(mean_square + EPSILON) * gain).astype(
            jnp.bfloat16
        )
        keys_here = jnp.dot(normalized_input, key_full, preferred_element_type=jnp.float32).astype(
            jnp.bfloat16
        )
        values_here = jnp.dot(
            normalized_input, value_full, preferred_element_type=jnp.float32
        ).astype(jnp.bfloat16)
        query_rows_set = normalized_input.reshape(
            local_rows, KEY_VALUE_HEADS, head_groups, HEAD_SIZE
        )
        start_state = (
            jnp.full((KEY_VALUE_HEADS, head_groups, local_rows), MASK_FLOOR, jnp.float32),
            jnp.zeros((KEY_VALUE_HEADS, head_groups, local_rows), jnp.float32),
            jnp.zeros((KEY_VALUE_HEADS, head_groups, local_rows, HEAD_SIZE), jnp.float32),
        )
        key_portion = lax.all_gather(keys_here, "ctx", axis=0, tiled=True)
        value_portion = lax.all_gather(values_here, "ctx", axis=0, tiled=True)
        item_count = key_portion.shape[0]
        key_positions = jnp.arange(item_count, dtype=jnp.int32)
        key_segments = segment_ids(lengths, key_positions)
        allowed = (query_positions[:, None] >= key_positions[None, :]) & (
            query_segments[:, None] == key_segments[None, :]
        )
        highest, totals, mixed = accumulate(
            start_state, query_rows_set, key_portion, value_portion, allowed
        )
        attended = (
            (mixed / totals[..., None])
            .transpose(2, 0, 1, 3)
            .reshape(local_rows, QUERY_HEADS * HEAD_SIZE)
        )
        skip_channel = skip_channel + attended
        produced.append(skip_channel.astype(jnp.bfloat16))
    return jnp.stack(produced)[:, None]


def solution(mesh):
    placed = (
        P("section", "ctx", None),
        P(None, "ctx", None),
        P("section", None),
        P("section", "ctx", None),
        P("section", "ctx", None),
        P(),
        P(),
    )
    return jax.shard_map(
        shards,
        mesh=mesh,
        in_specs=placed,
        out_specs=P(None, "section", "ctx", None),
        check_vma=False,
    )
```

profile of v0, /device:TPU:2, one launch (start us, length us, event | category | flops | bytes accessed | tf_op | source)
XLA Modules:
  0.0 415.5 jit_solution(1464353220016827104)
XLA Ops:
  6.5 0.7 all-gather.17.cloned.1.call-update
  7.3 0.7 all-gather.19.cloned.1.call-update
  8.0 0.0 all-gather.9.cloned.1.call-start
  8.1 1.8 fusion.28
  9.9 53.7 %all-gather.17.cloned.1.call-done = bf16[1,4096,512]{2,1,0:T(8,128)(2,1)} async-done(((bf16[1,256,512]{2,1,0:T(8,128)(2,1)}), bf16[1,4096,512]{2,1,0:T(8,128)(2,1)}) %all-gather.17.cloned.1.call-update) | async-done | bytes 4194320 | tf_op jit(solution)/shard_map/all_gather | solution.py:67
  63.6 3.6 fusion.33
  67.2 0.0 all-gather.11.cloned.1.call-start
  67.3 0.6 fusion.60
  69.1 0.2 dynamic-slice_reduce_fusion
  69.3 0.2 reduce-window.16
  69.5 0.2 reduce-window.17
  69.7 1.7 copy.42
  71.4 0.1 convert_reduce_fusion
  71.5 0.1 convert_reduce_fusion.2
  71.6 1.2 fusion.50
  72.8 44.1 %all-gather.19.cloned.1.call-done = bf16[1,4096,512]{2,1,0:T(8,128)(2,1)} async-done(((bf16[1,256,512]{2,1,0:T(8,128)(2,1)}), bf16[1,4096,512]{2,1,0:T(8,128)(2,1)}) %all-gather.19.cloned.1.call-update) | async-done | bytes 4194320 | tf_op jit(solution)/shard_map/all_gather | solution.py:68
  117.0 3.6 fusion.39
  120.6 0.2 all-gather.13.cloned.1.call-start
  120.8 43.2 %all-gather.9.cloned.1.call-done = bf16[2048,512]{1,0:T(8,128)(2,1)} async-done(((bf16[128,512]{1,0:T(8,128)(2,1)}), bf16[2048,512]{1,0:T(8,128)(2,1)}) %all-gather.9.cloned.1.call-update) | async-done | bytes 2097168 | tf_op jit(solution)/shard_map/all_gather | solution.py:106
  164.0 3.9 reshape.212
  168.0 16.5 %fusion = (f32[4,8,128]{2,1,0:T(8,128)S(1)}, f32[4,2048,128,8]{2,1,3,0:T(8,128)}) fusion(pred[128,2048]{0,1:T(8,128)(4,1)S(1)} %get-tuple-element.10, f32[128,4,8,128]{3,2,1,0:T(8,128)} %bitcast.108, f32[4,8,128]{2,1,0:T(8,128)S(1)} %bitcast.119, f32[128]{0:T(128)S(1)} %add_rsqrt_fusion.1, bf16[2048,4,128,1]{2,1,0,3:T(4,128)(2,1)} %bitcast.109), kind=kOutput, calls=%fused_computation.4 | convolution fusion | flops 2174218240 | bytes 38044160 | tf_op jit(solution)/shard_map/tgjd,sgd->gjts/dot_general | solution.py:30
  184.5 14.9 %fusion.2 = f32[4,8,128]{2,1,0:T(8,128)S(1)} fusion(f32[4,2048,128,8]{2,1,3,0:T(8,128)} %get-tuple-element.15, f32[4,8,128]{2,1,0:T(8,128)S(1)} %broadcast_maximum_fusion.1, pred[128,2048]{0,1:T(8,128)(4,1)S(1)} %get-tuple-element.10), kind=kLoop, calls=%fused_computation.6 | loop fusion | flops 41938944 | bytes 33849344 | tf_op jit(solution)/shard_map/reduce_sum | solution.py:39
  199.4 11.2 %all-gather.11.cloned.1.call-done = bf16[2048,512]{1,0:T(8,128)(2,1)} async-done(((bf16[128,512]{1,0:T(8,128)(2,1)}), bf16[2048,512]{1,0:T(8,128)(2,1)}) %all-gather.11.cloned.1.call-update) | async-done | bytes 2097168 | tf_op jit(solution)/shard_map/all_gather | solution.py:107
  210.6 3.9 copy.38
  214.5 29.3 %bitcast_divide_fusion.1 = f32[128,4,8,128]{0,3,2,1:T(8,128)} fusion(bf16[2048,4,128,1]{0,2,3,1:T(8,128)(2,1)} %bitcast.114, f32[4,2048,128,8]{2,1,3,0:T(8,128)} %get-tuple-element.15, f32[4,8,128]{2,1,0:T(8,128)S(1)} %broadcast_maximum_fusion.1, pred[128,2048]{0,1:T(8,128)(4,1)S(1)} %get-tuple-element.10, f32[128,4,8]{0,2,1:T(8,128)S(1)} %bitcast.121), kind=kOutput, calls=%fused_computation.33 | convolution fusion | flops 12918980608 | bytes 38043648 | tf_op jit(solution)/shard_map/gjts,sgd->gjtd/dot_general | solution.py:40
  243.8 2.9 copy.24
  246.7 3.1 bitcast_add_fusion
  249.8 1.9 collective-permute-start
  253.7 23.8 %collective-permute-done = f32[128,4096]{1,0:T(8,128)} collective-permute-done((f32[128,4096]{1,0:T(8,128)}, f32[128,4096]{1,0:T(8,128)}, u32[]{:S(2)}, u32[]{:S(2)}) %collective-permute-start) | collective-permute-done | bytes 2097184 | tf_op jit(solution)/shard_map/ppermute | solution.py:19
  277.5 2.2 multiply_reduce_fusion
  279.7 2.1 multiply_convert_fusion
  281.9 0.7 copy-done.2
  282.5 1.4 fusion.36
  283.9 0.3 all-gather.15.cloned.1.call-start
  284.2 2.9 copy.23
  287.1 2.9 add_convert_fusion.1
  290.0 1.2 copy.43
  291.2 1.4 fusion.42
  292.6 36.0 %all-gather.13.cloned.1.call-done = bf16[2048,512]{1,0:T(8,128)(2,1)} async-done(((bf16[128,512]{1,0:T(8,128)(2,1)}), bf16[2048,512]{1,0:T(8,128)(2,1)}) %all-gather.13.cloned.1.call-update) | async-done | bytes 2097168 | tf_op jit(solution)/shard_map/all_gather | solution.py:106
  328.6 2.5 reshape.218
  331.2 13.6 %fusion.1 = (f32[4,8,128]{2,1,0:T(8,128)S(1)}, f32[4,2048,128,8]{2,1,3,0:T(8,128)}) fusion(pred[128,2048]{0,1:T(8,128)(4,1)S(1)} %get-tuple-element.9, bf16[128,4,8,128]{3,2,1,0:T(8,128)(2,1)S(1)} %bitcast.113, bf16[2048,4,128,1]{2,1,0,3:T(4,128)(2,1)S(1)} %bitcast.110), kind=kOutput, calls=%fused_computation.5 | convolution fusion | flops 2172645376 | bytes 36978688 | tf_op jit(solution)/shard_map/tgjd,sgd->gjts/dot_general | solution.py:30
  344.8 14.9 %fusion.4 = f32[4,8,128]{2,1,0:T(8,128)S(1)} fusion(f32[4,2048,128,8]{2,1,3,0:T(8,128)} %get-tuple-element.17, f32[4,8,128]{2,1,0:T(8,128)S(1)} %broadcast_maximum_fusion, pred[128,2048]{0,1:T(8,128)(4,1)S(1)} %get-tuple-element.9), kind=kLoop, calls=%fused_computation.8 | loop fusion | flops 41938944 | bytes 33849344 | tf_op jit(solution)/shard_map/reduce_sum | solution.py:39
  359.7 15.5 %all-gather.15.cloned.1.call-done = bf16[2048,512]{1,0:T(8,128)(2,1)} async-done(((bf16[128,512]{1,0:T(8,128)(2,1)}), bf16[2048,512]{1,0:T(8,128)(2,1)}) %all-gather.15.cloned.1.call-update) | async-done | bytes 2097168 | tf_op jit(solution)/shard_map/all_gather | solution.py:107
  375.2 2.9 copy.41
  378.1 24.9 %bitcast_divide_fusion = f32[128,4,8,128]{0,3,2,1:T(8,128)} fusion(bf16[2048,4,128,1]{0,2,3,1:T(8,128)(2,1)S(1)} %bitcast.115, f32[4,2048,128,8]{2,1,3,0:T(8,128)} %get-tuple-element.17, f32[4,8,128]{2,1,0:T(8,128)S(1)} %broadcast_maximum_fusion, pred[128,2048]{0,1:T(8,128)(4,1)S(1)} %get-tuple-element.9, f32[128,4,8]{0,2,1:T(8,128)S(1)} %bitcast.122), kind=kOutput, calls=%fused_computation.30 | convolution fusion | flops 12918980608 | bytes 38043648 | tf_op jit(solution)/shard_map/gjts,sgd->gjtd/dot_general | solution.py:40
  403.0 1.9 copy.29
  404.9 2.3 fusion.45
  407.2 1.5 maximum_bitcast_fusion
  (28 shorter events, 0.2 us)
Async XLA Ops:
  6.5 57.0 %copy-start = (f32[1,128,4096]{2,1,0:T(8,128)S(1)}, f32[1,128,4096]{2,1,0:T(8,128)}, u32[]{:S(2)}) copy-start(f32[1,128,4096]{2,1,0:T(8,128)} %param.7) | copy-start | bytes 6291460
  6.5 57.0 %copy-start.6 = (f32[1,4096]{1,0:T(1,128)S(1)}, f32[1,4096]{1,0:T(1,128)}, u32[]{:S(2)}) copy-start(f32[1,4096]{1,0:T(1,128)} %param.9) | copy-start | bytes 49156
  6.5 57.0 %all-gather.17.cloned.1.call-start = ((), (), s32[]{:S(2)}) async-start(), calls=%async_computation.4 | async-start | bytes 4456448 | tf_op jit(solution)/shard_map/all_gather | solution.py:67
  7.3 109.7 %all-gather.19.cloned.1.call-start = ((), (), s32[]{:S(2)}) async-start(), calls=%async_computation.5 | async-start | bytes 4456448 | tf_op jit(solution)/shard_map/all_gather | solution.py:68
  8.0 156.0 %all-gather.9.cloned.1.call-start = ((), (), s32[]{:S(2)}) async-start(), calls=%async_computation | async-start | bytes 2228224 | tf_op jit(solution)/shard_map/all_gather | solution.py:106
  63.6 3.7 copy-start.8
  63.6 5.5 %copy-start.7 = (s32[10,8]{0,1:T(8,128)S(1)}, s32[10,8]{0,1:T(8,128)}, u32[]{:S(2)}) copy-start(s32[10,8]{0,1:T(8,128)} %param.12) | copy-start | bytes 964
  67.2 143.4 %all-gather.11.cloned.1.call-start = ((), (), s32[]{:S(2)}) async-start(), calls=%async_computation.1 | async-start | bytes 2228224 | tf_op jit(solution)/shard_map/all_gather | solution.py:107
  120.6 208.0 %all-gather.13.cloned.1.call-start = ((), (), s32[]{:S(2)}) async-start(), calls=%async_computation.2 | async-start | bytes 2228224 | tf_op jit(solution)/shard_map/all_gather | solution.py:106
  249.8 27.7 %collective-permute-start = (f32[128,4096]{1,0:T(8,128)}, f32[128,4096]{1,0:T(8,128)}, u32[]{:S(2)}, u32[]{:S(2)}) collective-permute-start(f32[128,4096]{1,0:T(8,128)} %bitcast_add_fusion), channel_id=1, source_target_pairs={{0,16},{16,32},{32,48},{48,64},{64,80},{80,96},{96,112},{1,17},{17... | collective-permute-start | bytes 6291464 | tf_op jit(solution)/shard_map/ppermute | solution.py:19
  253.6 26.1 %copy-start.3 = (bf16[2,128,4096]{2,1,0:T(8,128)(2,1)S(1)}, bf16[2,128,4096]{2,1,0:T(8,128)(2,1)}, u32[]{:S(2)}) copy-start(bf16[2,128,4096]{2,1,0:T(8,128)(2,1)} %param.8) | copy-start | bytes 6291460
  279.7 2.8 copy-start.2
  283.9 91.3 %all-gather.15.cloned.1.call-start = ((), (), s32[]{:S(2)}) async-start(), calls=%async_computation.3 | async-start | bytes 2228224 | tf_op jit(solution)/shard_map/all_gather | solution.py:107
  287.1 4.1 copy-start.1
  292.6 38.6 %copy-start.4 = (bf16[16,8,32,128]{3,2,1,0:T(8,128)(2,1)S(1)}, bf16[16,8,32,128]{3,2,1,0:T(8,128)(2,1)}, u32[]{:S(2)}) copy-start(bf16[16,8,32,128]{3,2,1,0:T(8,128)(2,1)} %copy.43) | copy-start | bytes 3145732
  404.9 2.3 copy-start.5
Sparse Core Ops, SparseCore 0:
  9.5 54.0 all-gather.16
  65.7 51.2 all-gather.18
  119.1 44.8 all-gather.8
  166.0 44.5 all-gather.10
  284.0 44.5 all-gather.12
  330.6 44.5 all-gather.14
where the time goes:
time: 416 us
  waiting for transfers between devices  229 us (55%)
  matrix products  94.2 us (23%)
  other arithmetic  47.6 us (11%)
  local copies, waits for them, and re-layouts  25.4 us (6%)
  between operations  16.8 us (4%)
    all_gather x2, waiting for transfers between devices, shards(): key_portion = lax.all_gather(keys_here, 'ctx', axis=0, tiled=True)  79.2 us
    dot_general x2, matrix products, accumulate(): jnp.einsum('gjts,sgd->gjtd', weights, value_portion.reshape(item_count, K...  54.2 us
    all_gather x1, waiting for transfers between devices, shards(): lax.all_gather(key_rows, 'ctx', axis=0, tiled=True)  53.7 us
    all_gather x1, waiting for transfers between devices, shards(): lax.all_gather(value_rows, 'ctx', axis=0, tiled=True)  44.1 us
    dot_general x2, matrix products, accumulate(): jnp.einsum('tgjd,sgd->gjts', query_rows_set, key_portion.reshape(item_cou...  30.1 us
    reduce_sum x2, other arithmetic, accumulate(): totals = jnp.sum(weights, axis=-1)  29.8 us
    all_gather x2, waiting for transfers between devices, shards(): value_portion = lax.all_gather(values_here, 'ctx', axis=0, tiled=True)  26.7 us
    ppermute x1, waiting for transfers between devices, shifted(): lax.ppermute(value, axis, [(source, source + steps) for source in range(i...  23.8 us
  transfers between devices with their start and end apart: 7, of which 7 were waited for; matrix products, arithmetic and copies ran while one was open for 21% of the time, Pallas kernels for 0%

commit v1 on v0

v1 whole, which is shorter than its diff:
```python
import functools

import jax
import jax.numpy as jnp
from jax import lax
from jax.experimental import pallas as pl
from jax.experimental.pallas import tpu as pltpu
from jax.sharding import PartitionSpec as P

HEAD_SIZE = 128
QUERY_HEADS = 32
KEY_VALUE_HEADS = 4
HEAD_GROUPS = QUERY_HEADS // KEY_VALUE_HEADS
GROUP_WIDTH = HEAD_GROUPS * HEAD_SIZE
KV_WIDTH = KEY_VALUE_HEADS * HEAD_SIZE
W = 2
EPSILON = 1e-05
MASK_FLOOR = -1e30
SIDE = 4
ROWS = 2
SCALE = HEAD_SIZE ** (-0.5)
LOG2E = 1.4426950408889634


def moved(block, dz, dy):
    pairs = [
        (z * SIDE + y, ((z + dz) % SIDE) * SIDE + (y + dy) % SIDE)
        for z in range(SIDE)
        for y in range(SIDE)
    ]
    return lax.ppermute(block, "ctx", pairs)


def swapped(block, first):
    pairs = []
    for z in range(SIDE):
        for y in (first, first + 2):
            a, b = z * SIDE + y % SIDE, z * SIDE + (y + 1) % SIDE
            pairs += [(a, b), (b, a)]
    return lax.ppermute(block, "ctx", pairs)


def window_blocks(own, z, y):
    tokens = own.shape[0]
    up1 = moved(own, 1, 0)
    up2 = moved(up1, 1, 0)
    left1, right1 = moved(up1, 0, 1), moved(up1, 0, -1)
    to_right = jnp.where(y == SIDE - 1, up2, own)
    to_left = jnp.where(y == 0, own, up2)
    left2, right2 = moved(to_right, 0, 1), moved(to_left, 0, -1)
    far1 = swapped(jnp.where(y % 2 == 1, left1, right1), 1)
    far2 = swapped(jnp.where(y % 2 == 1, right2, left2), 0)
    yl, yr, yf = (y + 3) % SIDE, (y + 1) % SIDE, (y + 2) % SIDE

    def near(column):
        return jnp.where(column < y, z, z - ROWS) * SIDE + column

    order = jnp.stack(
        [
            z * SIDE + y,
            (z - 1) * SIDE + y,
            (z - 2) * SIDE + y,
            (z - 1) * SIDE + yl,
            (z - 1) * SIDE + yr,
            near(yl),
            near(yr),
            (z - 1) * SIDE + yf,
            near(yf),
        ]
    )
    return [own, up1, up2, left1, right1, left2, right2, far1, far2], order * tokens


def attention_body(n_blocks, last_tick, bases, last, q, x, starts, *refs):
    keys = refs[:n_blocks]
    values = refs[n_blocks : 2 * n_blocks]
    refs = refs[2 * n_blocks :]
    if last_tick:
        (produced,) = refs
    else:
        first, gain, produced, stream, normed, squares = refs
    g = pl.program_id(0)
    tokens = q.shape[0]
    own = bases[0]
    column = lax.broadcasted_iota(jnp.int32, (tokens, tokens), 1)
    row = lax.broadcasted_iota(jnp.int32, (tokens, tokens), 0)
    low = jnp.broadcast_to(starts[...], (tokens, tokens))
    bias = []
    for b in range(n_blocks):
        position = column + bases[b]
        allowed = (position >= low) & (position <= row + own)
        bias.append(jnp.where(allowed, 0.0, MASK_FLOOR))
    bias = jnp.concatenate(bias, axis=1)
    k = jnp.concatenate([r[...] for r in keys], axis=0)
    v = jnp.concatenate([r[...] for r in values], axis=0)
    v = jnp.concatenate([v, jnp.ones_like(v)], axis=1)
    partial = jnp.zeros((tokens, HEAD_SIZE), jnp.float32)
    for h in range(0, HEAD_GROUPS, 2):
        qs = [q[:, (h + j) * HEAD_SIZE : (h + j + 1) * HEAD_SIZE] for j in range(2)]
        s = lax.dot_general(
            jnp.concatenate(qs, axis=0),
            k,
            (((1,), (1,)), ((), ())),
            preferred_element_type=jnp.float32,
        )
        s = s + jnp.concatenate([bias, bias], axis=0)
        high = jnp.max(s, axis=1, keepdims=True)
        p = jnp.exp2((s - high) * (SCALE * LOG2E)).astype(jnp.bfloat16)
        mixed = jnp.dot(p, v, preferred_element_type=jnp.float32)
        out = mixed[:, :HEAD_SIZE] / mixed[:, HEAD_SIZE:]
        for j in range(2):
            where = slice((h + j) * HEAD_SIZE, (h + j + 1) * HEAD_SIZE)
            new = x[:, where] + out[j * tokens : (j + 1) * tokens]
            produced[:, where] = new.astype(jnp.bfloat16)
            if not last_tick:
                at = pl.ds(pl.multiple_of(g * GROUP_WIDTH, GROUP_WIDTH) + (h + j) * HEAD_SIZE, HEAD_SIZE)
                stream[:, at] = new
    if last_tick:
        return

    @pl.when(g == KEY_VALUE_HEADS - 1)
    def _():
        @pl.when(last[0] == 1)
        def _():
            stream[...] = first[...].astype(jnp.float32)

        total = jnp.zeros((tokens, 128), jnp.float32)
        for c in range(0, stream.shape[1], 128):
            piece = stream[:, c : c + 128]
            total = total + piece * piece
        mean = jnp.sum(total, axis=1, keepdims=True) * (1.0 / stream.shape[1])
        factor = lax.rsqrt(mean + EPSILON)
        for c in range(0, stream.shape[1], 128):
            at = slice(c, c + 128)
            normed[:, at] = (stream[:, at] * factor * gain[:, at]).astype(jnp.bfloat16)


def attention(blocks, bases, q, x, starts, following=None):
    tokens, width = q.shape
    n_blocks = len(blocks)
    last_tick = following is None
    flag = jnp.zeros((1,), jnp.int32) if last_tick else following[0]
    whole = lambda g, *_: (0, 0)
    by_group = pl.BlockSpec((tokens, GROUP_WIDTH), lambda g, *_: (0, g))
    in_specs = [by_group, by_group, pl.BlockSpec((tokens, 1), whole)]
    in_specs += [pl.BlockSpec((tokens, HEAD_SIZE), lambda g, *_: (0, g))] * n_blocks
    in_specs += [
        pl.BlockSpec((tokens, HEAD_SIZE), lambda g, *_: (0, KEY_VALUE_HEADS + g))
    ] * n_blocks
    out_specs = [by_group]
    out_shape = [jax.ShapeDtypeStruct((tokens, width), jnp.bfloat16)]
    operands = [q, x, starts, *blocks, *blocks]
    scratch = []
    if not last_tick:
        in_specs += [pl.BlockSpec((tokens, width), whole), pl.BlockSpec((1, width), whole)]
        operands += [following[1], following[2]]
        out_specs += [pl.BlockSpec((tokens, width), whole)] * 2
        out_shape += [
            jax.ShapeDtypeStruct((tokens, width), jnp.float32),
            jax.ShapeDtypeStruct((tokens, width), jnp.bfloat16),
        ]
        scratch = [pltpu.VMEM((8, 128), jnp.float32)]
    return pl.pallas_call(
        functools.partial(attention_body, n_blocks, last_tick),
        grid_spec=pltpu.PrefetchScalarGridSpec(
            num_scalar_prefetch=2,
            grid=(KEY_VALUE_HEADS,),
            in_specs=in_specs,
            out_specs=out_specs,
            scratch_shapes=scratch,
        ),
        out_shape=out_shape,
        compiler_params=pltpu.CompilerParams(vmem_limit_bytes=48 << 20),
        cost_estimate=pl.CostEstimate(
            flops=4 * tokens * n_blocks * tokens * width,
            transcendentals=tokens * n_blocks * tokens * QUERY_HEADS,
            bytes_accessed=tokens * width * 12 + n_blocks * tokens * 2 * KV_WIDTH * 2,
        ),
        name="attention",
    )(bases, flag, *operands)


def document_starts(lengths, positions):
    count = lengths.shape[0]
    upto = jnp.arange(count)[:, None] >= jnp.arange(count)[None, :]
    ends = jnp.sum(jnp.where(upto, lengths[None, :], 0), axis=1)
    return jnp.max(jnp.where(positions[:, None] >= ends[None, :], ends[None, :], 0), axis=1, keepdims=True)


def shards(carried, arrivals, gains, key_rows, value_rows, lengths, permutation):
    stream = carried[0]
    gain = gains[0:1]
    tokens = stream.shape[0]
    phases = lax.axis_size("section")
    phase = lax.axis_index("section")
    context = lax.axis_index("ctx")
    z, y = context // SIDE, context % SIDE
    onward = [(s, (s + 1) % phases) for s in range(phases)]
    back = [(t, s) for s, t in onward]

    weights = jnp.concatenate([key_rows[0], value_rows[0]], axis=1)
    weights = lax.all_gather(weights, "ctx", axis=0, tiled=True)

    next_gain = lax.ppermute(gain, "section", back)
    chosen = permutation[0]
    first = lax.dynamic_index_in_dim(arrivals, chosen, 0, keepdims=False)
    positions = context * tokens + jnp.arange(tokens, dtype=jnp.int32)
    sequences = [phase, jnp.where(phase == 0, phases + chosen, phase - 1)]
    starts = [
        document_starts(lax.dynamic_index_in_dim(lengths, s, 0, keepdims=False), positions)
        for s in sequences
    ]
    is_last = (phase == phases - 1).astype(jnp.int32).reshape(1)

    mean = jnp.mean(stream * stream, axis=-1, keepdims=True)
    normed = (stream * lax.rsqrt(mean + EPSILON) * gain).astype(jnp.bfloat16)
    own = jnp.dot(normed, weights, preferred_element_type=jnp.float32).astype(jnp.bfloat16)
    blocks, bases = window_blocks(own, z, y)
    early, stream, normed = attention(
        blocks, bases, normed, stream, starts[0], (is_last, first, next_gain)
    )
    normed = lax.ppermute(normed, "section", onward)
    stream = lax.ppermute(stream, "section", onward)
    own = jnp.dot(normed, weights, preferred_element_type=jnp.float32).astype(jnp.bfloat16)
    blocks, bases = window_blocks(own, z, y)
    (late,) = attention(blocks, bases, normed, stream, starts[1])
    return jnp.stack([early, late])[:, None]


def solution(mesh):
    placed = (
        P("section", "ctx", None),
        P(None, "ctx", None),
        P("section", None),
        P("section", "ctx", None),
        P("section", "ctx", None),
        P(),
        P(),
    )
    return jax.shard_map(
        shards,
        mesh=mesh,
        in_specs=placed,
        out_specs=P(None, "section", "ctx", None),
        check_vma=False,
    )
```

time: 416 us -> 217 us (0.52)
  waiting for transfers between devices: 229 us -> 125 us
  matrix products: 94.2 us -> 5.98 us
  other arithmetic: 47.6 us -> 11.9 us
  Pallas kernels: 0 us -> 24 us
  starting transfers between devices: 2.52 us -> 23.6 us
  local copies, waits for them, and re-layouts: 25.4 us -> 11.4 us
    all_gather x6 -> x1, waiting for transfers between devices: 204 us -> 71.6 us  [shards(): weights = lax.all_gather(weights, 'ctx', axis=0, tiled=True)]
    dot_general x8 -> x2, matrix products: 94.2 us -> 5.98 us  [shards(): jnp.dot(normed, weights, preferred_element_type=jnp.float32)]
    reduce_sum x6 -> x2, other arithmetic: 34 us -> 2.12 us  [the longest x1 1.97 us: shards(): mean = jnp.mean(stream * stream, axis=-1, keepdims=True)]
    ppermute x1 -> x19, waiting for transfers between devices: 23.8 us -> 53 us  [the longest x12 30.7 us: moved(): return lax.ppermute(block, 'ctx', pairs)]
    pallas_call x0 -> x2, Pallas kernels: none -> 24 us  [attention(): pl.pallas_call(functools.partial(attention_body, n_blocks, last_tick), gr...]
    ppermute x1 -> x19, starting transfers between devices: 1.91 us -> 23.6 us  [the longest x12 15.6 us: moved(): return lax.ppermute(block, 'ctx', pairs)]
    reshape x7 -> x0, local copies, waits for them, and re-layouts: 21 us -> none  [the longest x3 7.68 us: shards(): attended = (mixed / totals[..., None]).transpose(2, 0, 1, 3).reshape(loca...]
    unnamed x20 -> x44, local copies, waits for them, and re-layouts: 3.59 us -> 9.78 us
  transfers between devices with their start and end apart: 7 -> 20, of which waited for: 7 -> 12; matrix products, arithmetic and copies ran while one was open for 21% -> 5% of each run, Pallas kernels for 0% -> 0%
where the time goes in v1:
time: 217 us; the launch traced here: 215 us
  waiting for transfers between devices  125 us (58%)
  Pallas kernels  24 us (11%)
  starting transfers between devices  23.6 us (11%)
  between operations  13.7 us (6%)
  other arithmetic  11.9 us (5%)
  local copies, waits for them, and re-layouts  11.4 us (5%)
  matrix products  5.98 us (3%)
    all_gather x1, waiting for transfers between devices, shards(): weights = lax.all_gather(weights, 'ctx', axis=0, tiled=True)  71.6 us
    ppermute x12, waiting for transfers between devices, moved(): return lax.ppermute(block, 'ctx', pairs)  30.7 us
    pallas_call x2, Pallas kernels, attention(): pl.pallas_call(functools.partial(attention_body, n_blocks, last_tick), gr...  24 us
    ppermute x12, starting transfers between devices, moved(): return lax.ppermute(block, 'ctx', pairs)  15.6 us
    ppermute x1, waiting for transfers between devices, shards(): normed = lax.ppermute(normed, 'section', onward)  12.6 us
    unnamed x44, local copies, waits for them, and re-layouts  9.78 us
    ppermute x4, waiting for transfers between devices, swapped(): return lax.ppermute(block, 'ctx', pairs)  9.63 us
    ppermute x4, starting transfers between devices, swapped(): return lax.ppermute(block, 'ctx', pairs)  6.42 us
  transfers between devices with their start and end apart: 20, of which 12 were waited for; matrix products, arithmetic and copies ran while one was open for 5% of the time, Pallas kernels for 0%

profile of v1, /device:TPU:2, one launch (start us, length us, event | category | flops | bytes accessed | tf_op | source)
XLA Modules:
  0.0 215.2 jit_solution(6963209964096226030)
XLA Ops:
  6.5 2.0 pad_maximum_fusion
  8.6 2.0 multiply_reduce_fusion
  11.1 71.6 %all-gather.2.cloned.1.call-done = bf16[4096,1024]{1,0:T(8,128)(2,1)} async-done(((bf16[256,1024]{1,0:T(8,128)(2,1)}), bf16[4096,1024]{1,0:T(8,128)(2,1)}) %all-gather.2.cloned.1.call-update) | async-done | bytes 8388624 | tf_op jit(solution)/shard_map/all_gather | solution.py:202
  82.8 4.6 %convolution_convert_fusion.1.refs_0_.refs_9_ = bf16[128,1024]{1,0:T(8,128)(2,1)S(1)} fusion(bf16[128,4096]{1,0:T(8,128)(2,1)S(1)} %multiply_convert_fusion.q, bf16[4096,1024]{1,0:T(8,128)(2,1)} %all-gather.2.cloned.1.call-done), kind=kOutput, calls=%fused_computation.4 | convolution fusion | flops 1073872896 | bytes 9699328 | tf_op jit(solution)/shard_map/dot_general | solution.py:217
  87.4 1.4 collective-permute-start
  89.0 7.8 %collective-permute-done.refs_1_.refs_10_ = bf16[128,1024]{1,0:T(8,128)(2,1)} collective-permute-done((bf16[128,1024]{1,0:T(8,128)(2,1)S(1)}, bf16[128,1024]{1,0:T(8,128)(2,1)}, u32[]{:S(2)}, u32[]{:S(2)}) %collective-permute-start) | collective-permute-done | bytes 262176 | tf_op jit(solution)/shard_map/ppermute | solution.py:31
  97.0 1.1 dynamic-slice_bitcast_fusion.refs_18_
  98.1 1.4 collective-permute-start.2
  99.5 1.9 collective-permute-start.3
  101.4 4.1 %collective-permute-done.1.refs_2_.refs_11_ = bf16[128,1024]{1,0:T(8,128)(2,1)S(1)} collective-permute-done((bf16[128,1024]{1,0:T(8,128)(2,1)}, bf16[128,1024]{1,0:T(8,128)(2,1)S(1)}, u32[]{:S(2)}, u32[]{:S(2)}) %collective-permute-start.1) | collective-permute-done | bytes 262176 | tf_op jit(solution)/shard_map/ppermute | solution.py:31
  105.4 0.9 broadcast_select_fusion.5
  107.0 1.5 collective-permute-start.4
  108.5 1.8 collective-permute-start.5
  110.2 1.7 broadcast_select_fusion.3
  111.9 1.4 collective-permute-start.6
  113.4 2.7 %collective-permute-done.4.refs_5_.refs_14_ = bf16[128,1024]{1,0:T(8,128)(2,1)} collective-permute-done((bf16[128,1024]{1,0:T(8,128)(2,1)}, bf16[128,1024]{1,0:T(8,128)(2,1)}, u32[]{:S(2)}, u32[]{:S(2)}) %collective-permute-start.4) | collective-permute-done | bytes 262176 | tf_op jit(solution)/shard_map/ppermute | solution.py:31
  116.1 0.9 collective-permute-done.5.refs_6_.refs_15_
  117.0 1.7 broadcast_select_fusion.2
  118.6 2.0 collective-permute-start.7
  121.3 4.0 %collective-permute-done.7.refs_8_.refs_17_ = bf16[128,1024]{1,0:T(8,128)(2,1)} collective-permute-done((bf16[128,1024]{1,0:T(8,128)(2,1)}, bf16[128,1024]{1,0:T(8,128)(2,1)}, u32[]{:S(2)}, u32[]{:S(2)}) %collective-permute-start.7) | collective-permute-done | bytes 262176 | tf_op jit(solution)/shard_map/ppermute | solution.py:40
  125.3 0.9 copy-done.2
  126.3 13.2 %attention.2 = (bf16[128,4096]{1,0:T(8,128)(2,1)S(1)}, f32[128,4096]{1,0:T(8,128)}, bf16[128,4096]{1,0:T(8,128)(2,1)S(1)}) custom-call(s32[9]{0:T(128)S(1)} %broadcast_multiply_fusion.bases, s32[1]{0:T(128)} %bitcast.9.last, bf16[128,4096]{1,0:T(8,128)(2,1)S(1)} %multiply_convert_fusion.q, f32[128,4096]{1,0:T(8,128)} %bitcast.34, s32[128,1]{1,0:T(8,128)S(1)} %copy.11.starts, ...), custom_call_target="tpu_custom_call" | custom-call | flops 2415919104 | bytes 8650752 | tf_op jit(solution)/shard_map/attention/pallas_call | solution.py:163
  139.5 1.6 collective-permute-start.10
  141.1 12.6 %collective-permute-done.9.q = bf16[128,4096]{1,0:T(8,128)(2,1)S(1)} collective-permute-done((bf16[128,4096]{1,0:T(8,128)(2,1)S(1)}, bf16[128,4096]{1,0:T(8,128)(2,1)S(1)}, u32[]{:S(2)}, u32[]{:S(2)}) %collective-permute-start.9) | collective-permute-done | bytes 1048608 | tf_op jit(solution)/shard_map/ppermute | solution.py:222
  153.7 1.3 convolution_convert_fusion.refs_0_.refs_9_
  155.2 8.5 %collective-permute-done.11.refs_1_.refs_10_ = bf16[128,1024]{1,0:T(8,128)(2,1)S(1)} collective-permute-done((bf16[128,1024]{1,0:T(8,128)(2,1)S(1)}, bf16[128,1024]{1,0:T(8,128)(2,1)S(1)}, u32[]{:S(2)}, u32[]{:S(2)}) %collective-permute-start.11) | collective-permute-done | bytes 262176 | tf_op jit(solution)/shard_map/ppermute | solution.py:31
  163.7 2.0 collective-permute-start.13
  165.7 1.8 collective-permute-start.14
  167.5 3.8 %collective-permute-done.12.refs_2_.refs_11_ = bf16[128,1024]{1,0:T(8,128)(2,1)S(1)} collective-permute-done((bf16[128,1024]{1,0:T(8,128)(2,1)S(1)}, bf16[128,1024]{1,0:T(8,128)(2,1)S(1)}, u32[]{:S(2)}, u32[]{:S(2)}) %collective-permute-start.12) | collective-permute-done | bytes 262176 | tf_op jit(solution)/shard_map/ppermute | solution.py:31
  171.3 0.7 copy-done.3
  172.0 2.0 collective-permute-start.15
  174.1 1.7 collective-permute-start.16
  175.8 0.8 broadcast_select_fusion.1
  176.6 0.7 copy-done.5
  177.3 2.0 collective-permute-start.17
  179.3 2.9 %collective-permute-done.15.refs_5_.refs_14_ = bf16[128,1024]{1,0:T(8,128)(2,1)S(1)} collective-permute-done((bf16[128,1024]{1,0:T(8,128)(2,1)S(1)}, bf16[128,1024]{1,0:T(8,128)(2,1)S(1)}, u32[]{:S(2)}, u32[]{:S(2)}) %collective-permute-start.15) | collective-permute-done | bytes 262176 | tf_op jit(solution)/shard_map/ppermute | solution.py:31
  182.2 0.8 broadcast_select_fusion
  183.7 1.0 collective-permute-start.18
  184.8 1.0 collective-permute-done.17.refs_7_.refs_16_
  185.8 4.6 %collective-permute-done.18.refs_8_.refs_17_ = bf16[128,1024]{1,0:T(8,128)(2,1)} collective-permute-done((bf16[128,1024]{1,0:T(8,128)(2,1)}, bf16[128,1024]{1,0:T(8,128)(2,1)}, u32[]{:S(2)}, u32[]{:S(2)}) %collective-permute-start.18) | collective-permute-done | bytes 262176 | tf_op jit(solution)/shard_map/ppermute | solution.py:40
  190.4 0.9 copy-done.4
  191.4 0.9 copy-done.6
  192.3 0.9 copy-done.8
  193.3 0.9 copy-done.10
  194.2 0.9 copy-done.12
  195.2 0.9 copy-done.14
  196.1 10.8 %attention.3 = bf16[128,4096]{1,0:T(8,128)(2,1)S(1)} custom-call(s32[9]{0:T(128)S(1)} %broadcast_multiply_fusion.bases, s32[1]{0:T(128)} %constant.101.clone.1.last, bf16[128,4096]{1,0:T(8,128)(2,1)S(1)} %collective-permute-done.9.q, f32[128,4096]{1,0:T(8,128)} %collective-permute-done.10.x, s32[128,1]{1,0:T(8,128)S(1)} %copy.12.starts, ...), custom_call_target="tpu_custom_call" | custom-call | flops 2415919104 | bytes 8650752 | tf_op jit(solution)/shard_map/attention/pallas_call | solution.py:163
  206.9 1.5 maximum_bitcast_fusion
  (61 shorter events, 3.1 us)
Async XLA Ops:
  6.5 90.4 %copy-start = (bf16[2,128,4096]{2,1,0:T(8,128)(2,1)S(1)}, bf16[2,128,4096]{2,1,0:T(8,128)(2,1)}, u32[]{:S(2)}) copy-start(bf16[2,128,4096]{2,1,0:T(8,128)(2,1)} %param.8) | copy-start | bytes 6291460
  6.5 4.1 %copy-start.19 = (f32[1,4096]{1,0:T(1,128)S(1)}, f32[1,4096]{1,0:T(1,128)}, u32[]{:S(2)}) copy-start(f32[1,4096]{1,0:T(1,128)} %param.9) | copy-start | bytes 49156
  6.5 76.2 %all-gather.2.cloned.1.call-start = ((), (), s32[]{:S(2)}) async-start(), calls=%async_computation | async-start | bytes 8912896 | tf_op jit(solution)/shard_map/all_gather | solution.py:202
  8.6 2.2 %copy-start.18 = (f32[1,128,4096]{2,1,0:T(8,128)S(1)}, f32[1,128,4096]{2,1,0:T(8,128)}, u32[]{:S(2)}) copy-start(f32[1,128,4096]{2,1,0:T(8,128)} %param.7) | copy-start | bytes 6291460
  11.1 77.7 %copy-start.21 = (s32[2]{0:T(128)S(1)}, s32[2]{0:T(128)}, u32[]{:S(2)}) copy-start(s32[2]{0:T(128)} %param.13) | copy-start | bytes 28
  87.4 9.4 %collective-permute-start = (bf16[128,1024]{1,0:T(8,128)(2,1)S(1)}, bf16[128,1024]{1,0:T(8,128)(2,1)}, u32[]{:S(2)}, u32[]{:S(2)}) collective-permute-start(bf16[128,1024]{1,0:T(8,128)(2,1)S(1)} %convolution_convert_fusion.1.refs_0_.refs_9_), channel_id=1, source_target_pairs={{0,4},{1,5},{2,6},{3,7},{4,8},{5,9},{6,10},{7,11},{8,12},{9,13},{1... | collective-permute-start | bytes 786440 | tf_op jit(solution)/shard_map/ppermute | solution.py:31
  88.8 32.4 %collective-permute-start.8 = (f32[1,4096]{1,0:T(1,128)S(1)}, f32[1,4096]{1,0:T(1,128)S(1)}, u32[]{:S(2)}, u32[]{:S(2)}) collective-permute-start(f32[1,4096]{1,0:T(1,128)S(1)} %copy-done.19), channel_id=1, source_target_pairs={{16,0},{32,16},{48,32},{64,48},{80,64},{96,80},{112,96},{0,112},{1... | collective-permute-start | bytes 49160 | tf_op jit(solution)/shard_map/ppermute | solution.py:204
  89.0 31.6 %copy-start.20 = (s32[10,8]{0,1:T(8,128)S(1)}, s32[10,8]{0,1:T(8,128)}, u32[]{:S(2)}) copy-start(s32[10,8]{0,1:T(8,128)} %param.12) | copy-start | bytes 964
  96.8 8.6 %collective-permute-start.1 = (bf16[128,1024]{1,0:T(8,128)(2,1)}, bf16[128,1024]{1,0:T(8,128)(2,1)S(1)}, u32[]{:S(2)}, u32[]{:S(2)}) collective-permute-start(bf16[128,1024]{1,0:T(8,128)(2,1)} %collective-permute-done.refs_1_.refs_10_), channel_id=1, source_target_pairs={{0,4},{1,5},{2,6},{3,7},{4,8},{5,9},{6,10},{7,11},{8,12},{9,13},{1... | collective-permute-start | bytes 786440 | tf_op jit(solution)/shard_map/ppermute | solution.py:31
  98.1 12.1 %collective-permute-start.2 = (bf16[128,1024]{1,0:T(8,128)(2,1)}, bf16[128,1024]{1,0:T(8,128)(2,1)}, u32[]{:S(2)}, u32[]{:S(2)}) collective-permute-start(bf16[128,1024]{1,0:T(8,128)(2,1)} %collective-permute-done.refs_1_.refs_10_), channel_id=1, source_target_pairs={{0,1},{1,2},{2,3},{3,0},{4,5},{5,6},{6,7},{7,4},{8,9},{9,10},{10,1... | collective-permute-start | bytes 786440 | tf_op jit(solution)/shard_map/ppermute | solution.py:31
  99.5 10.8 %collective-permute-start.3 = (bf16[128,1024]{1,0:T(8,128)(2,1)}, bf16[128,1024]{1,0:T(8,128)(2,1)}, u32[]{:S(2)}, u32[]{:S(2)}) collective-permute-start(bf16[128,1024]{1,0:T(8,128)(2,1)} %collective-permute-done.refs_1_.refs_10_), channel_id=1, source_target_pairs={{0,3},{1,0},{2,1},{3,2},{4,7},{5,4},{6,5},{7,6},{8,11},{9,8},{10,9... | collective-permute-start | bytes 786440 | tf_op jit(solution)/shard_map/ppermute | solution.py:31
  106.3 0.7 copy-start.1
  107.0 9.1 %collective-permute-start.4 = (bf16[128,1024]{1,0:T(8,128)(2,1)}, bf16[128,1024]{1,0:T(8,128)(2,1)}, u32[]{:S(2)}, u32[]{:S(2)}) collective-permute-start(bf16[128,1024]{1,0:T(8,128)(2,1)} %get-tuple-element.18), channel_id=1, source_target_pairs={{0,1},{1,2},{2,3},{3,0},{4,5},{5,6},{6,7},{7,4},{8,9},{9,10},{10,1... | collective-permute-start | bytes 786440 | tf_op jit(solution)/shard_map/ppermute | solution.py:31
  108.5 8.5 %collective-permute-start.5 = (bf16[128,1024]{1,0:T(8,128)(2,1)}, bf16[128,1024]{1,0:T(8,128)(2,1)}, u32[]{:S(2)}, u32[]{:S(2)}) collective-permute-start(bf16[128,1024]{1,0:T(8,128)(2,1)} %get-tuple-element.17), channel_id=1, source_target_pairs={{0,3},{1,0},{2,1},{3,2},{4,7},{5,4},{6,5},{7,6},{8,11},{9,8},{10,9... | collective-permute-start | bytes 786440 | tf_op jit(solution)/shard_map/ppermute | solution.py:31
  111.9 9.3 %collective-permute-start.6 = (bf16[128,1024]{1,0:T(8,128)(2,1)}, bf16[128,1024]{1,0:T(8,128)(2,1)}, u32[]{:S(2)}, u32[]{:S(2)}) collective-permute-start(bf16[128,1024]{1,0:T(8,128)(2,1)} %broadcast_select_fusion.3), channel_id=1, source_target_pairs={{1,2},{2,1},{3,0},{0,3},{5,6},{6,5},{7,4},{4,7},{9,10},{10,9},{11,... | collective-permute-start | bytes 786440 | tf_op jit(solution)/shard_map/ppermute | solution.py:40
  118.6 6.7 %collective-permute-start.7 = (bf16[128,1024]{1,0:T(8,128)(2,1)}, bf16[128,1024]{1,0:T(8,128)(2,1)}, u32[]{:S(2)}, u32[]{:S(2)}) collective-permute-start(bf16[128,1024]{1,0:T(8,128)(2,1)} %broadcast_select_fusion.2), channel_id=1, source_target_pairs={{0,1},{1,0},{2,3},{3,2},{4,5},{5,4},{6,7},{7,6},{8,9},{9,8},{10,11... | collective-permute-start | bytes 786440 | tf_op jit(solution)/shard_map/ppermute | solution.py:40
  125.3 1.0 copy-start.2
  126.3 27.4 %copy-start.17 = (bf16[4096,1024]{1,0:T(8,128)(2,1)S(1)}, bf16[4096,1024]{1,0:T(8,128)(2,1)}, u32[]{:S(2)}) copy-start(bf16[4096,1024]{1,0:T(8,128)(2,1)} %all-gather.2.cloned.1.call-done) | copy-start | bytes 25165828
  139.5 15.6 %copy-start.15 = (bf16[128,4096]{1,0:T(8,128)(2,1)}, bf16[128,4096]{1,0:T(8,128)(2,1)S(1)}, u32[]{:S(2)}) copy-start(bf16[128,4096]{1,0:T(8,128)(2,1)S(1)} %get-tuple-element.8) | copy-start | bytes 3145732
  139.5 14.2 %collective-permute-start.9 = (bf16[128,4096]{1,0:T(8,128)(2,1)S(1)}, bf16[128,4096]{1,0:T(8,128)(2,1)S(1)}, u32[]{:S(2)}, u32[]{:S(2)}) collective-permute-start(bf16[128,4096]{1,0:T(8,128)(2,1)S(1)} %get-tuple-element.9), channel_id=1, source_target_pairs={{0,16},{16,32},{32,48},{48,64},{64,80},{80,96},{96,112},{112,0},{1... | collective-permute-start | bytes 3145736 | tf_op jit(solution)/shard_map/ppermute | solution.py:222
  139.5 46.3 %collective-permute-start.10 = (f32[128,4096]{1,0:T(8,128)}, f32[128,4096]{1,0:T(8,128)}, u32[]{:S(2)}, u32[]{:S(2)}) collective-permute-start(f32[128,4096]{1,0:T(8,128)} %get-tuple-element.10), channel_id=1, source_target_pairs={{0,16},{16,32},{32,48},{48,64},{64,80},{80,96},{96,112},{112,0},{1... | collective-permute-start | bytes 6291464 | tf_op jit(solution)/shard_map/ppermute | solution.py:223
  155.1 8.6 %collective-permute-start.11 = (bf16[128,1024]{1,0:T(8,128)(2,1)S(1)}, bf16[128,1024]{1,0:T(8,128)(2,1)S(1)}, u32[]{:S(2)}, u32[]{:S(2)}) collective-permute-start(bf16[128,1024]{1,0:T(8,128)(2,1)S(1)} %convolution_convert_fusion.refs_0_.refs_9_), channel_id=1, source_target_pairs={{0,4},{1,5},{2,6},{3,7},{4,8},{5,9},{6,10},{7,11},{8,12},{9,13},{1... | collective-permute-start | bytes 786440 | tf_op jit(solution)/shard_map/ppermute | solution.py:31
  163.7 21.0 %copy-start.13 = (bf16[128,1024]{1,0:T(8,128)(2,1)}, bf16[128,1024]{1,0:T(8,128)(2,1)S(1)}, u32[]{:S(2)}) copy-start(bf16[128,1024]{1,0:T(8,128)(2,1)S(1)} %collective-permute-done.11.refs_1_.refs_10_) | copy-start | bytes 786436
  163.7 7.6 %collective-permute-start.12 = (bf16[128,1024]{1,0:T(8,128)(2,1)S(1)}, bf16[128,1024]{1,0:T(8,128)(2,1)S(1)}, u32[]{:S(2)}, u32[]{:S(2)}) collective-permute-start(bf16[128,1024]{1,0:T(8,128)(2,1)S(1)} %collective-permute-done.11.refs_1_.refs_10_), channel_id=1, source_target_pairs={{0,4},{1,5},{2,6},{3,7},{4,8},{5,9},{6,10},{7,11},{8,12},{9,13},{1... | collective-permute-start | bytes 786440 | tf_op jit(solution)/shard_map/ppermute | solution.py:31
  163.7 12.1 %collective-permute-start.13 = (bf16[128,1024]{1,0:T(8,128)(2,1)S(1)}, bf16[128,1024]{1,0:T(8,128)(2,1)S(1)}, u32[]{:S(2)}, u32[]{:S(2)}) collective-permute-start(bf16[128,1024]{1,0:T(8,128)(2,1)S(1)} %collective-permute-done.11.refs_1_.refs_10_), channel_id=1, source_target_pairs={{0,1},{1,2},{2,3},{3,0},{4,5},{5,6},{6,7},{7,4},{8,9},{9,10},{10,1... | collective-permute-start | bytes 786440 | tf_op jit(solution)/shard_map/ppermute | solution.py:31
  165.7 10.1 %collective-permute-start.14 = (bf16[128,1024]{1,0:T(8,128)(2,1)S(1)}, bf16[128,1024]{1,0:T(8,128)(2,1)S(1)}, u32[]{:S(2)}, u32[]{:S(2)}) collective-permute-start(bf16[128,1024]{1,0:T(8,128)(2,1)S(1)} %collective-permute-done.11.refs_1_.refs_10_), channel_id=1, source_target_pairs={{0,3},{1,0},{2,1},{3,2},{4,7},{5,4},{6,5},{7,6},{8,11},{9,8},{10,9... | collective-permute-start | bytes 786440 | tf_op jit(solution)/shard_map/ppermute | solution.py:31
  171.3 0.7 copy-start.3
  172.0 10.1 %collective-permute-start.15 = (bf16[128,1024]{1,0:T(8,128)(2,1)S(1)}, bf16[128,1024]{1,0:T(8,128)(2,1)S(1)}, u32[]{:S(2)}, u32[]{:S(2)}) collective-permute-start(bf16[128,1024]{1,0:T(8,128)(2,1)S(1)} %get-tuple-element.16), channel_id=1, source_target_pairs={{0,1},{1,2},{2,3},{3,0},{4,5},{5,6},{6,7},{7,4},{8,9},{9,10},{10,1... | collective-permute-start | bytes 786440 | tf_op jit(solution)/shard_map/ppermute | solution.py:31
  174.1 8.1 %collective-permute-start.16 = (bf16[128,1024]{1,0:T(8,128)(2,1)S(1)}, bf16[128,1024]{1,0:T(8,128)(2,1)S(1)}, u32[]{:S(2)}, u32[]{:S(2)}) collective-permute-start(bf16[128,1024]{1,0:T(8,128)(2,1)S(1)} %get-tuple-element.15), channel_id=1, source_target_pairs={{0,3},{1,0},{2,1},{3,2},{4,7},{5,4},{6,5},{7,6},{8,11},{9,8},{10,9... | collective-permute-start | bytes 786440 | tf_op jit(solution)/shard_map/ppermute | solution.py:31
  175.8 0.8 copy-start.7
  176.6 0.7 copy-start.5
  177.3 8.5 %collective-permute-start.17 = (bf16[128,1024]{1,0:T(8,128)(2,1)}, bf16[128,1024]{1,0:T(8,128)(2,1)}, u32[]{:S(2)}, u32[]{:S(2)}) collective-permute-start(bf16[128,1024]{1,0:T(8,128)(2,1)} %broadcast_select_fusion.1), channel_id=1, source_target_pairs={{1,2},{2,1},{3,0},{0,3},{5,6},{6,5},{7,4},{4,7},{9,10},{10,9},{11,... | collective-permute-start | bytes 786440 | tf_op jit(solution)/shard_map/ppermute | solution.py:40
  182.2 0.8 copy-start.11
  183.0 0.7 copy-start.9
  183.7 6.7 %collective-permute-start.18 = (bf16[128,1024]{1,0:T(8,128)(2,1)}, bf16[128,1024]{1,0:T(8,128)(2,1)}, u32[]{:S(2)}, u32[]{:S(2)}) collective-permute-start(bf16[128,1024]{1,0:T(8,128)(2,1)} %broadcast_select_fusion), channel_id=1, source_target_pairs={{0,1},{1,0},{2,3},{3,2},{4,5},{5,4},{6,7},{7,6},{8,9},{9,8},{10,11... | collective-permute-start | bytes 786440 | tf_op jit(solution)/shard_map/ppermute | solution.py:40
  190.4 1.0 copy-start.4
  191.3 0.9 copy-start.6
  192.3 0.9 copy-start.8
  193.2 0.9 copy-start.10
  194.2 0.9 copy-start.12
  195.2 0.9 copy-start.14
  196.1 10.8 %copy-start.16 = (bf16[128,4096]{1,0:T(8,128)(2,1)S(1)}, bf16[128,4096]{1,0:T(8,128)(2,1)}, u32[]{:S(2)}) copy-start(bf16[128,4096]{1,0:T(8,128)(2,1)} %copy-done.15) | copy-start | bytes 3145732
Sparse Core Ops, SparseCore 0:
  9.5 73.2 all-gather.1

commit v2 on v1

v2 whole, which is shorter than its diff:
```python
import functools

import jax
import jax.numpy as jnp
from jax import lax
from jax.experimental import pallas as pl
from jax.experimental.pallas import tpu as pltpu
from jax.sharding import PartitionSpec as P

HEAD_SIZE = 128
QUERY_HEADS = 32
KEY_VALUE_HEADS = 4
HEAD_GROUPS = QUERY_HEADS // KEY_VALUE_HEADS
GROUP_WIDTH = HEAD_GROUPS * HEAD_SIZE
KV_WIDTH = KEY_VALUE_HEADS * HEAD_SIZE
W = 2
EPSILON = 1e-05
MASK_FLOOR = -1e30
SIDE = 4
VMEM = 56 << 20
DEPTH = 256
SCALE = HEAD_SIZE ** (-0.5)
LOG2E = 1.4426950408889634


def moved(block, dz, dy):
    pairs = [
        (z * SIDE + y, ((z + dz) % SIDE) * SIDE + (y + dy) % SIDE)
        for z in range(SIDE)
        for y in range(SIDE)
    ]
    return lax.ppermute(block, "ctx", pairs)


def swapped(block, first, along_z=False):
    pairs = []
    for other in range(SIDE):
        for at in (first, first + 2):
            a, b = at % SIDE, (at + 1) % SIDE
            if along_z:
                a, b = a * SIDE + other, b * SIDE + other
            else:
                a, b = other * SIDE + a, other * SIDE + b
            pairs += [(a, b), (b, a)]
    return lax.ppermute(block, "ctx", pairs)


def tree_gather(own, z, y):
    zp, yp, zm, ym = moved(own, 1, 0), moved(own, 0, 1), moved(own, -1, 0), moved(own, 0, -1)
    got = {(0, 0): own, (1, 0): zp, (0, 1): yp, (3, 0): zm, (0, 3): ym}
    got[0, 2] = swapped(jnp.where(y % 2 == 1, yp, ym), 1)
    got[2, 0] = swapped(jnp.where(z % 2 == 1, zm, zp), 0, True)
    got[1, 1] = moved(zp, 0, 1)
    got[3, 3] = moved(zm, 0, -1)
    got[1, 3] = moved(ym, 1, 0)
    got[3, 1] = moved(yp, -1, 0)
    got[1, 2] = moved(got[0, 2], 1, 0)
    got[3, 2] = moved(got[0, 2], -1, 0)
    got[2, 1] = moved(got[2, 0], 0, 1)
    got[2, 3] = moved(got[2, 0], 0, -1)
    got[2, 2] = moved(got[1, 2], 1, 0)
    order = [((z - dz) % SIDE) * SIDE + (y - dy) % SIDE for dz, dy in got]
    return list(got.values()), jnp.stack(order)


def window_places(y):
    yl, yr, yf = (y + 3) % SIDE, (y + 1) % SIDE, (y + 2) % SIDE
    above = [SIDE + y - c for c in (yl, yr, yf)]
    near = [jnp.where(c < y, 0, 2 * SIDE) + y - c for c in (yl, yr, yf)]
    return jnp.stack([jnp.zeros_like(y), SIDE + 0 * y, 2 * SIDE + 0 * y, *above, *near])


def window_blocks(own, y):
    up1, up2 = moved(own, 1, 0), moved(own, 2, 0)
    above = [moved(up1, 0, 1), moved(up1, 0, -1), moved(up1, 0, 2)]
    to_right = jnp.where(y == SIDE - 1, up2, own)
    to_left = jnp.where(y == 0, own, up2)
    across = jnp.where(y < 2, own, up2)
    near = [moved(to_right, 0, 1), moved(to_left, 0, -1), moved(across, 0, 2)]
    return [own, up1, up2, *above, *near]


def fetched(blocks, into, sems, first=0):
    copies, row = [], 0
    for i, block in enumerate(blocks):
        height = block.shape[0]
        copies.append(pltpu.make_async_copy(block, into.at[pl.ds(row, height)], sems.at[first + i]))
        row += height
    for copy in copies:
        copy.start()
    return copies


def by_head(out, rows, which, beside):
    if not beside:
        out[...] = rows
        return
    for h in range(KEY_VALUE_HEADS):
        at = (2 * h + which) * HEAD_SIZE
        out[:, at : at + HEAD_SIZE] = rows[:, h * HEAD_SIZE : (h + 1) * HEAD_SIZE]


def projection_body(n_keys, with_keys, with_values, order, rows, *refs):
    key_blocks, refs = refs[:n_keys], refs[n_keys:]
    if with_keys:
        keys, refs = refs[0], refs[1:]
    if with_values:
        value_rows, refs = refs[0], refs[1:]
    out, refs = refs[0], list(refs[1:])
    sems = refs.pop()
    width = rows.shape[1]
    count = width // DEPTH
    if n_keys:
        held_keys = refs.pop(0)
        key_copies = fetched(key_blocks, held_keys, sems)
    if with_values:
        held_values = refs.pop(0)
        pieces = [value_rows.at[pl.ds(j * DEPTH, DEPTH)] for j in range(count)]
        value_copies = fetched(pieces, held_values, sems, n_keys)
    if n_keys:
        total = jnp.zeros((rows.shape[0], KV_WIDTH), jnp.float32)
        for j, copy in enumerate(key_copies):
            copy.wait()
            at = pl.ds(pl.multiple_of(order[j] * DEPTH, DEPTH), DEPTH)
            part = held_keys[j * DEPTH : (j + 1) * DEPTH]
            total = total + jnp.dot(rows[:, at], part, preferred_element_type=jnp.float32)
        by_head(out, total.astype(out.dtype), 0, with_values)
    if with_keys:
        by_head(out, keys[...], 0, True)
    if with_values:
        total = jnp.zeros((rows.shape[0], KV_WIDTH), jnp.float32)
        for j, copy in enumerate(value_copies):
            copy.wait()
            at = slice(j * DEPTH, (j + 1) * DEPTH)
            total = total + jnp.dot(rows[:, at], held_values[at], preferred_element_type=jnp.float32)
        by_head(out, total.astype(out.dtype), 1, True)


def projection(rows, order, key_blocks=(), keys=None, values=None):
    tokens, width = rows.shape
    n_keys = len(key_blocks)
    in_vmem, in_hbm = pl.BlockSpec(memory_space=pltpu.VMEM), pl.BlockSpec(memory_space=pl.ANY)
    in_specs = [pl.BlockSpec(memory_space=pltpu.SMEM), in_vmem] + [in_hbm] * n_keys
    operands = [order, rows, *key_blocks]
    held = pltpu.VMEM((width, KV_WIDTH), jnp.bfloat16)
    scratch = [held] if n_keys else []
    n_copies, columns = n_keys, KV_WIDTH
    if keys is not None:
        in_specs, operands = in_specs + [in_vmem], operands + [keys]
    if values is not None:
        in_specs, operands = in_specs + [in_hbm], operands + [values]
        scratch, n_copies, columns = scratch + [held], n_copies + width // DEPTH, 2 * KV_WIDTH
    return pl.pallas_call(
        functools.partial(projection_body, n_keys, keys is not None, values is not None),
        in_specs=in_specs,
        out_specs=in_vmem,
        out_shape=jax.ShapeDtypeStruct((tokens, columns), jnp.bfloat16),
        scratch_shapes=[*scratch, pltpu.SemaphoreType.DMA((n_copies,))],
        compiler_params=pltpu.CompilerParams(vmem_limit_bytes=VMEM),
        cost_estimate=pl.CostEstimate(
            flops=2 * tokens * width * KV_WIDTH * len(scratch),
            transcendentals=0,
            bytes_accessed=len(scratch) * width * KV_WIDTH * 2,
        ),
        name="projection",
    )(*operands)


def attention_body(n_blocks, last_tick, places, last, q, x, starts, *refs):
    blocks, refs = refs[:n_blocks], refs[n_blocks:]
    if last_tick:
        _, produced = refs
    else:
        first, gain, produced, stream, normed, rows = refs
    g = pl.program_id(0)
    tokens = q.shape[0]

    column = lax.broadcasted_iota(jnp.int32, (tokens, tokens), 1)
    row = lax.broadcasted_iota(jnp.int32, (tokens, tokens), 0)
    low = jnp.broadcast_to(starts[...], (tokens, tokens))
    bias = []
    for b in range(n_blocks):
        allowed = column - places[b] * tokens >= low
        if b == 0:
            allowed = allowed & (column <= row)
        bias.append(jnp.where(allowed, 0.0, MASK_FLOOR))
    bias = jnp.concatenate(bias, axis=1)
    bias = jnp.concatenate([bias, bias], axis=0)
    k = jnp.concatenate([block[:, :HEAD_SIZE] for block in blocks], axis=0)
    v = jnp.concatenate([block[:, HEAD_SIZE:] for block in blocks], axis=0)
    v = jnp.concatenate([v, jnp.ones_like(v)], axis=1)
    for h in range(0, HEAD_GROUPS, 2):
        qs = [q[:, (h + j) * HEAD_SIZE : (h + j + 1) * HEAD_SIZE] for j in range(2)]
        s = lax.dot_general(
            jnp.concatenate(qs, axis=0),
            k,
            (((1,), (1,)), ((), ())),
            preferred_element_type=jnp.float32,
        )
        s = s + bias
        high = jnp.max(s, axis=1, keepdims=True)
        p = jnp.exp2((s - high) * (SCALE * LOG2E)).astype(jnp.bfloat16)
        mixed = jnp.dot(p, v, preferred_element_type=jnp.float32)
        out = mixed[:, :HEAD_SIZE] / mixed[:, HEAD_SIZE:]
        for j in range(2):
            where = slice((h + j) * HEAD_SIZE, (h + j + 1) * HEAD_SIZE)
            new = x[:, where] + out[j * tokens : (j + 1) * tokens]
            produced[0, :, where] = new.astype(jnp.bfloat16)
            if not last_tick:
                new = jnp.where(last[0] == 1, first[:, where].astype(jnp.float32), new)
                stream[:, where] = new
                at = pl.multiple_of(g * GROUP_WIDTH, GROUP_WIDTH) + (h + j) * HEAD_SIZE
                rows[:, pl.ds(at, HEAD_SIZE)] = new
    if last_tick:
        return

    @pl.when(g == KEY_VALUE_HEADS - 1)
    def _():
        total = jnp.zeros((tokens, 128), jnp.float32)
        for c in range(0, rows.shape[1], 128):
            piece = rows[:, c : c + 128]
            total = total + piece * piece
        mean = jnp.sum(total, axis=1, keepdims=True) * (1.0 / rows.shape[1])
        factor = lax.rsqrt(mean + EPSILON)
        for c in range(0, rows.shape[1], 128):
            at = slice(c, c + 128)
            normed[:, at] = (rows[:, at] * factor * gain[:, at]).astype(jnp.bfloat16)


def attention(blocks, places, q, x, starts, tick, onward=None, produced=None):
    tokens, width = q.shape
    n_blocks = len(blocks)
    span = sum(block.shape[0] for block in blocks)
    last_tick = onward is None
    flag = jnp.zeros((1,), jnp.int32) if last_tick else onward[0]
    whole = lambda g, *_: (0, 0)
    by_group = pl.BlockSpec((tokens, GROUP_WIDTH), lambda g, *_: (0, g))
    in_specs = [by_group, by_group, pl.BlockSpec((tokens, 1), whole)]
    in_specs += [pl.BlockSpec((tokens, 2 * HEAD_SIZE), lambda g, *_: (0, g))] * n_blocks
    out_specs = [pl.BlockSpec((1, tokens, GROUP_WIDTH), lambda g, *_: (tick, 0, g))]
    out_shape = [jax.ShapeDtypeStruct((W, tokens, width), jnp.bfloat16)]
    operands = [q, x, starts, *blocks]
    scratch = []
    aliases = {}
    if last_tick:
        aliases = {2 + len(operands): 0}
        in_specs += [pl.BlockSpec(memory_space=pl.ANY)]
        operands += [produced]
    else:
        in_specs += [by_group, pl.BlockSpec((1, width), whole)]
        operands += [onward[1], onward[2]]
        out_specs += [by_group, pl.BlockSpec((tokens, width), whole)]
        out_shape += [
            jax.ShapeDtypeStruct((tokens, width), jnp.float32),
            jax.ShapeDtypeStruct((tokens, width), jnp.bfloat16),
        ]
        scratch += [pltpu.VMEM((tokens, width), jnp.float32)]
    return pl.pallas_call(
        functools.partial(attention_body, n_blocks, last_tick),
        grid_spec=pltpu.PrefetchScalarGridSpec(
            num_scalar_prefetch=2,
            grid=(KEY_VALUE_HEADS,),
            in_specs=in_specs,
            out_specs=out_specs,
            scratch_shapes=scratch,
        ),
        out_shape=out_shape,
        input_output_aliases=aliases,
        compiler_params=pltpu.CompilerParams(vmem_limit_bytes=VMEM),
        cost_estimate=pl.CostEstimate(
            flops=4 * tokens * span * width,
            transcendentals=tokens * span * QUERY_HEADS,
            bytes_accessed=tokens * width * 12 + span * 2 * KV_WIDTH * 2,
        ),
        name="attention",
    )(places, flag, *operands)


def document_starts(lengths, positions):
    count = lengths.shape[0]
    upto = jnp.arange(count)[:, None] >= jnp.arange(count)[None, :]
    ends = jnp.sum(jnp.where(upto, lengths[None, :], 0), axis=1)
    return jnp.max(jnp.where(positions[:, None] >= ends[None, :], ends[None, :], 0), axis=1, keepdims=True)


def shards(carried, arrivals, gains, key_rows, value_rows, lengths, permutation):
    stream = carried[0]
    gain = gains[0:1]
    tokens = stream.shape[0]
    phases = lax.axis_size("section")
    phase = lax.axis_index("section")
    context = lax.axis_index("ctx")
    z, y = context // SIDE, context % SIDE
    onward = [(s, (s + 1) % phases) for s in range(phases)]
    back = [(t, s) for s, t in onward]

    value_weights = lax.all_gather(value_rows[0], "ctx", axis=0, tiled=True)
    key_blocks, order = tree_gather(key_rows[0], z, y)

    next_gain = lax.ppermute(gain, "section", back)
    chosen = permutation[0]
    first = lax.dynamic_index_in_dim(arrivals, chosen, 0, keepdims=False)
    positions = context * tokens + jnp.arange(tokens, dtype=jnp.int32)
    sequences = [phase, jnp.where(phase == 0, phases + chosen, phase - 1)]
    starts = [
        document_starts(lax.dynamic_index_in_dim(lengths, s, 0, keepdims=False), positions) - context * tokens
        for s in sequences
    ]
    is_last = (phase == phases - 1).astype(jnp.int32).reshape(1)

    mean = jnp.mean(stream * stream, axis=-1, keepdims=True)
    normed = (stream * lax.rsqrt(mean + EPSILON) * gain).astype(jnp.bfloat16)
    places = window_places(y)
    keys = projection(normed, order, key_blocks)
    own = projection(normed, order, (), keys, value_weights)
    blocks = window_blocks(own, y)
    produced, stream, normed = attention(
        blocks, places, normed, stream, starts[0], 0, (is_last, first, next_gain)
    )
    normed = lax.ppermute(normed, "section", onward)
    normed, stream = lax.optimization_barrier((normed, stream))
    stream = lax.ppermute(stream, "section", onward)
    own = projection(normed, order, key_blocks, None, value_weights)
    blocks = window_blocks(own, y)
    (produced,) = attention(blocks, places, normed, stream, starts[1], 1, None, produced)
    return produced[:, None]


def solution(mesh):
    placed = (
        P("section", "ctx", None),
        P(None, "ctx", None),
        P("section", None),
        P("section", "ctx", None),
        P("section", "ctx", None),
        P(),
        P(),
    )
    return jax.shard_map(
        shards,
        mesh=mesh,
        in_specs=placed,
        out_specs=P(None, "section", "ctx", None),
        check_vma=False,
    )
```

time: 217 us -> 207 us (0.954)
  waiting for transfers between devices: 125 us -> 92.8 us
  starting transfers between devices: 23.6 us -> 47.2 us
  Pallas kernels: 24 us -> 39.5 us
  matrix products: 5.98 us -> 0 us
  local copies, waits for them, and re-layouts: 11.4 us -> 5.97 us
  other arithmetic: 11.9 us -> 7.08 us
    all_gather x1, waiting for transfers between devices: 71.6 us -> 7.13 us  [shards(): value_weights = lax.all_gather(value_rows[0], 'ctx', axis=0, tiled=True)]
    ppermute x12 -> x29, waiting for transfers between devices: 30.7 us -> 65.9 us  [moved(): return lax.ppermute(block, 'ctx', pairs)]
    ppermute x12 -> x29, starting transfers between devices: 15.6 us -> 42.2 us  [moved(): return lax.ppermute(block, 'ctx', pairs)]
    pallas_call x0 -> x3, Pallas kernels: none -> 14.9 us  [projection(): pl.pallas_call(functools.partial(projection_body, n_keys, keys is not Non...]
    unnamed x44 -> x52, local copies, waits for them, and re-layouts: 9.78 us -> 1.83 us
    dot_general x2 -> x0, matrix products: 5.98 us -> none  [shards(): jnp.dot(normed, weights, preferred_element_type=jnp.float32)]
    ppermute x4 -> x2, waiting for transfers between devices: 9.63 us -> 4.55 us  [swapped(): return lax.ppermute(block, 'ctx', pairs)]
    select_n x6 -> x4, other arithmetic: 5.86 us -> 3.72 us  [the longest x2 2.89 us: window_blocks(): across = jnp.where(y < 2, own, up2)]
  transfers between devices with their start and end apart: 20 -> 35, of which waited for: 12 -> 18; matrix products, arithmetic and copies ran while one was open for 5% -> 5% of each run, Pallas kernels for 0% -> 5%
where the time goes in v2:
time: 207 us
  waiting for transfers between devices  92.8 us (45%)
  starting transfers between devices  47.2 us (23%)
  Pallas kernels  39.5 us (19%)
  between operations  14 us (7%)
  other arithmetic  7.08 us (3%)
  local copies, waits for them, and re-layouts  5.97 us (3%)
    ppermute x29, waiting for transfers between devices, moved(): return lax.ppermute(block, 'ctx', pairs)  65.9 us
    ppermute x29, starting transfers between devices, moved(): return lax.ppermute(block, 'ctx', pairs)  42.2 us
    pallas_call x2, Pallas kernels, attention(): pl.pallas_call(functools.partial(attention_body, n_blocks, last_tick), gr...  24.6 us
    pallas_call x3, Pallas kernels, projection(): pl.pallas_call(functools.partial(projection_body, n_keys, keys is not Non...  14.9 us
    ppermute x1, waiting for transfers between devices, shards(): normed = lax.ppermute(normed, 'section', onward)  14.4 us
    all_gather x1, waiting for transfers between devices, shards(): value_weights = lax.all_gather(value_rows[0], 'ctx', axis=0, tiled=True)  7.13 us
    ppermute x2, starting transfers between devices, swapped(): return lax.ppermute(block, 'ctx', pairs)  5.01 us
    ppermute x2, waiting for transfers between devices, swapped(): return lax.ppermute(block, 'ctx', pairs)  4.55 us
  transfers between devices with their start and end apart: 35, of which 18 were waited for; matrix products, arithmetic and copies ran while one was open for 5% of the time, Pallas kernels for 5%

profile of v2, /device:TPU:2, one launch (start us, length us, event | category | flops | bytes accessed | tf_op | source)
XLA Modules:
  0.0 206.6 jit_solution(16160717845498805662)
XLA Ops:
  7.3 1.6 collective-permute-start.1
  8.9 1.7 collective-permute-start.3
  10.6 1.9 collective-permute-start
  12.5 2.1 %collective-permute-start.2 = (bf16[256,512]{1,0:T(8,128)(2,1)}, bf16[256,512]{1,0:T(8,128)(2,1)S(1)}, u32[]{:S(2)}, u32[]{:S(2)}) collective-permute-start(bf16[256,512]{1,0:T(8,128)(2,1)} %bitcast.46), channel_id=1, source_target_pairs={{0,12},{1,13},{2,14},{3,15},{4,0},{5,1},{6,2},{7,3},{8,4},{9,5},{1... | collective-permute-start | bytes 786440 | tf_op jit(solution)/shard_map/ppermute | solution.py:32
  14.6 2.3 %collective-permute-done.1.refs_2_ = bf16[256,512]{1,0:T(8,128)(2,1)S(1)} collective-permute-done((bf16[256,512]{1,0:T(8,128)(2,1)}, bf16[256,512]{1,0:T(8,128)(2,1)S(1)}, u32[]{:S(2)}, u32[]{:S(2)}) %collective-permute-start.1) | collective-permute-done | bytes 262176 | tf_op jit(solution)/shard_map/ppermute | solution.py:32
  17.7 3.0 %collective-permute-start.4 = (bf16[256,512]{1,0:T(8,128)(2,1)}, bf16[256,512]{1,0:T(8,128)(2,1)S(1)}, u32[]{:S(2)}, u32[]{:S(2)}) collective-permute-start(bf16[256,512]{1,0:T(8,128)(2,1)} %broadcast_select_fusion.7), channel_id=1, source_target_pairs={{1,2},{2,1},{3,0},{0,3},{5,6},{6,5},{7,4},{4,7},{9,10},{10,9},{11,... | collective-permute-start | bytes 786440 | tf_op jit(solution)/shard_map/ppermute | solution.py:45
  20.8 2.0 collective-permute-start.5
  22.8 3.2 %collective-permute-start.7 = (bf16[256,512]{1,0:T(8,128)(2,1)S(1)}, bf16[256,512]{1,0:T(8,128)(2,1)S(1)}, u32[]{:S(2)}, u32[]{:S(2)}) collective-permute-start(bf16[256,512]{1,0:T(8,128)(2,1)S(1)} %collective-permute-done.2.refs_3_), channel_id=1, source_target_pairs={{0,3},{1,0},{2,1},{3,2},{4,7},{5,4},{6,5},{7,6},{8,11},{9,8},{10,9... | collective-permute-start | bytes 786440 | tf_op jit(solution)/shard_map/ppermute | solution.py:32
  26.1 4.5 %collective-permute-done.4.refs_5_ = bf16[256,512]{1,0:T(8,128)(2,1)S(1)} collective-permute-done((bf16[256,512]{1,0:T(8,128)(2,1)}, bf16[256,512]{1,0:T(8,128)(2,1)S(1)}, u32[]{:S(2)}, u32[]{:S(2)}) %collective-permute-start.4) | collective-permute-done | bytes 262176 | tf_op jit(solution)/shard_map/ppermute | solution.py:45
  30.7 2.3 %collective-permute-start.10 = (bf16[256,512]{1,0:T(8,128)(2,1)S(1)}, bf16[256,512]{1,0:T(8,128)(2,1)}, u32[]{:S(2)}, u32[]{:S(2)}) collective-permute-start(bf16[256,512]{1,0:T(8,128)(2,1)S(1)} %collective-permute-done.4.refs_5_), channel_id=1, source_target_pairs={{0,4},{1,5},{2,6},{3,7},{4,8},{5,9},{6,10},{7,11},{8,12},{9,13},{1... | collective-permute-start | bytes 786440 | tf_op jit(solution)/shard_map/ppermute | solution.py:32
  32.9 1.8 multiply_reduce_fusion
  34.8 2.7 %collective-permute-start.9 = (bf16[256,512]{1,0:T(8,128)(2,1)S(1)}, bf16[256,512]{1,0:T(8,128)(2,1)}, u32[]{:S(2)}, u32[]{:S(2)}) collective-permute-start(bf16[256,512]{1,0:T(8,128)(2,1)S(1)} %collective-permute-done.1.refs_2_), channel_id=1, source_target_pairs={{0,12},{1,13},{2,14},{3,15},{4,0},{5,1},{6,2},{7,3},{8,4},{9,5},{1... | collective-permute-start | bytes 786440 | tf_op jit(solution)/shard_map/ppermute | solution.py:32
  37.9 2.8 %collective-permute-start.13 = (bf16[256,512]{1,0:T(8,128)(2,1)}, bf16[256,512]{1,0:T(8,128)(2,1)}, u32[]{:S(2)}, u32[]{:S(2)}) collective-permute-start(bf16[256,512]{1,0:T(8,128)(2,1)} %collective-permute-done.5.refs_6_), channel_id=1, source_target_pairs={{0,3},{1,0},{2,1},{3,2},{4,7},{5,4},{6,5},{7,6},{8,11},{9,8},{10,9... | collective-permute-start | bytes 786440 | tf_op jit(solution)/shard_map/ppermute | solution.py:32
  40.7 2.7 %collective-permute-start.11 = (bf16[256,512]{1,0:T(8,128)(2,1)S(1)}, bf16[256,512]{1,0:T(8,128)(2,1)}, u32[]{:S(2)}, u32[]{:S(2)}) collective-permute-start(bf16[256,512]{1,0:T(8,128)(2,1)S(1)} %collective-permute-done.4.refs_5_), channel_id=1, source_target_pairs={{0,12},{1,13},{2,14},{3,15},{4,0},{5,1},{6,2},{7,3},{8,4},{9,5},{1... | collective-permute-start | bytes 786440 | tf_op jit(solution)/shard_map/ppermute | solution.py:32
  43.4 1.6 collective-permute-start.14
  45.1 1.3 multiply_convert_fusion.rows.q
  47.2 5.2 %collective-permute-done.11.refs_12_ = bf16[256,512]{1,0:T(8,128)(2,1)} collective-permute-done((bf16[256,512]{1,0:T(8,128)(2,1)S(1)}, bf16[256,512]{1,0:T(8,128)(2,1)}, u32[]{:S(2)}, u32[]{:S(2)}) %collective-permute-start.11) | collective-permute-done | bytes 262176 | tf_op jit(solution)/shard_map/ppermute | solution.py:32
  52.3 6.1 %collective-permute-done.14.refs_15_ = bf16[256,512]{1,0:T(8,128)(2,1)} collective-permute-done((bf16[256,512]{1,0:T(8,128)(2,1)}, bf16[256,512]{1,0:T(8,128)(2,1)}, u32[]{:S(2)}, u32[]{:S(2)}) %collective-permute-start.14) | collective-permute-done | bytes 262176 | tf_op jit(solution)/shard_map/ppermute | solution.py:32
  58.4 4.5 %projection.3.refs_0_ = bf16[128,512]{1,0:T(8,128)(2,1)} custom-call(s32[16]{0:T(128)} %stack.95.order, bf16[128,4096]{1,0:T(8,128)(2,1)} %multiply_convert_fusion.rows.q, bf16[256,512]{1,0:T(8,128)(2,1)} %bitcast.47, bf16[256,512]{1,0:T(8,128)(2,1)} %copy-done.5, bf16[256,512]{1,0:T(8,128)(2,1)} %copy-done.3, bf16[256,512]{1,0:T(8,128)(2,1)} %copy-done.6, ...), custom_call_target="tpu_custom_call" | custom-call | flops 536870912 | bytes 4194304 | tf_op jit(solution)/shard_map/projection/pallas_call | solution.py:153
  62.9 7.1 %all-gather.3.cloned.1.call-done = bf16[1,4096,512]{2,1,0:T(8,128)(2,1)} async-done(((bf16[1,256,512]{2,1,0:T(8,128)(2,1)}), bf16[1,4096,512]{2,1,0:T(8,128)(2,1)}) %all-gather.3.cloned.1.call-update) | async-done | bytes 4194320 | tf_op jit(solution)/shard_map/all_gather | solution.py:297
  70.0 4.5 %projection.4.refs_0_ = bf16[128,1024]{1,0:T(8,128)(2,1)} custom-call(s32[16]{0:T(128)} %stack.95.order, bf16[128,4096]{1,0:T(8,128)(2,1)} %multiply_convert_fusion.rows.q, bf16[128,512]{1,0:T(8,128)(2,1)} %projection.3.refs_0_, bf16[4096,512]{1,0:T(8,128)(2,1)} %bitcast.40), custom_call_target="tpu_custom_call" | custom-call | flops 536870912 | bytes 4194304 | tf_op jit(solution)/shard_map/projection/pallas_call | solution.py:153
  75.7 2.0 collective-permute-start.15
  77.7 7.8 %collective-permute-done.16.refs_2_ = bf16[128,1024]{1,0:T(8,128)(2,1)S(1)} collective-permute-done((bf16[128,1024]{1,0:T(8,128)(2,1)}, bf16[128,1024]{1,0:T(8,128)(2,1)S(1)}, u32[]{:S(2)}, u32[]{:S(2)}) %collective-permute-start.16) | collective-permute-done | bytes 262176 | tf_op jit(solution)/shard_map/ppermute | solution.py:32
  85.5 1.1 broadcast_select_fusion.1
  88.4 3.2 %collective-permute-start.21 = (bf16[128,1024]{1,0:T(8,128)(2,1)S(1)}, bf16[128,1024]{1,0:T(8,128)(2,1)S(1)}, u32[]{:S(2)}, u32[]{:S(2)}) collective-permute-start(bf16[128,1024]{1,0:T(8,128)(2,1)S(1)} %get-tuple-element.23), channel_id=1, source_target_pairs={{0,3},{1,0},{2,1},{3,2},{4,7},{5,4},{6,5},{7,6},{8,11},{9,8},{10,9... | collective-permute-start | bytes 786440 | tf_op jit(solution)/shard_map/ppermute | solution.py:32
  92.4 2.4 %collective-permute-start.18 = (bf16[128,1024]{1,0:T(8,128)(2,1)}, bf16[128,1024]{1,0:T(8,128)(2,1)S(1)}, u32[]{:S(2)}, u32[]{:S(2)}) collective-permute-start(bf16[128,1024]{1,0:T(8,128)(2,1)} %collective-permute-done.15.refs_1_), channel_id=1, source_target_pairs={{0,3},{1,0},{2,1},{3,2},{4,7},{5,4},{6,5},{7,6},{8,11},{9,8},{10,9... | collective-permute-start | bytes 786440 | tf_op jit(solution)/shard_map/ppermute | solution.py:32
  94.8 4.5 %collective-permute-done.20.refs_6_ = bf16[128,1024]{1,0:T(8,128)(2,1)} collective-permute-done((bf16[128,1024]{1,0:T(8,128)(2,1)S(1)}, bf16[128,1024]{1,0:T(8,128)(2,1)}, u32[]{:S(2)}, u32[]{:S(2)}) %collective-permute-start.20) | collective-permute-done | bytes 262176 | tf_op jit(solution)/shard_map/ppermute | solution.py:32
  99.4 1.1 dynamic-slice_bitcast_fusion.refs_9_
  100.5 3.0 %collective-permute-done.21.refs_7_ = bf16[128,1024]{1,0:T(8,128)(2,1)S(1)} collective-permute-done((bf16[128,1024]{1,0:T(8,128)(2,1)S(1)}, bf16[128,1024]{1,0:T(8,128)(2,1)S(1)}, u32[]{:S(2)}, u32[]{:S(2)}) %collective-permute-start.21) | collective-permute-done | bytes 262176 | tf_op jit(solution)/shard_map/ppermute | solution.py:32
  103.5 7.7 %collective-permute-done.17.refs_3_ = bf16[128,1024]{1,0:T(8,128)(2,1)S(1)} collective-permute-done((bf16[128,1024]{1,0:T(8,128)(2,1)}, bf16[128,1024]{1,0:T(8,128)(2,1)S(1)}, u32[]{:S(2)}, u32[]{:S(2)}) %collective-permute-start.17) | collective-permute-done | bytes 262176 | tf_op jit(solution)/shard_map/ppermute | solution.py:32
  111.2 1.0 collective-permute-done.18.refs_4_
  113.0 12.9 %attention.2 = (bf16[2,128,4096]{2,1,0:T(8,128)(2,1)}, f32[128,4096]{1,0:T(8,128)}, bf16[128,4096]{1,0:T(8,128)(2,1)}) custom-call(s32[9]{0:T(128)} %stack.78.places, s32[1]{0:T(128)} %bitcast.6.last, bf16[128,4096]{1,0:T(8,128)(2,1)} %multiply_convert_fusion.rows.q, f32[128,4096]{1,0:T(8,128)} %bitcast.42, s32[128,1]{1,0:T(8,128)} %copy.12.starts, ...), custom_call_target="tpu_custom_call" | custom-call | flops 2415919104 | bytes 8650752 | tf_op jit(solution)/shard_map/attention/pallas_call | solution.py:258
  126.0 14.4 %collective-permute-done.24.rows.q = bf16[128,4096]{1,0:T(8,128)(2,1)S(1)} collective-permute-done((bf16[128,4096]{1,0:T(8,128)(2,1)}, bf16[128,4096]{1,0:T(8,128)(2,1)S(1)}, u32[]{:S(2)}, u32[]{:S(2)}) %collective-permute-start.24) | collective-permute-done | bytes 1048608 | tf_op jit(solution)/shard_map/ppermute | solution.py:320
  141.4 6.0 %projection.5.refs_0_ = bf16[128,1024]{1,0:T(8,128)(2,1)} custom-call(s32[16]{0:T(128)} %stack.95.order, bf16[128,4096]{1,0:T(8,128)(2,1)} %copy-done.2, bf16[256,512]{1,0:T(8,128)(2,1)} %bitcast.48, bf16[256,512]{1,0:T(8,128)(2,1)} %copy-done.5, bf16[256,512]{1,0:T(8,128)(2,1)} %copy-done.3, bf16[256,512]{1,0:T(8,128)(2,1)} %copy-done.6, ...), custom_call_target="tpu_custom_call" | custom-call | flops 1073741824 | bytes 8388608 | tf_op jit(solution)/shard_map/projection/pallas_call | solution.py:153
  148.1 1.9 collective-permute-start.26
  150.0 8.4 %collective-permute-done.27.refs_2_ = bf16[128,1024]{1,0:T(8,128)(2,1)S(1)} collective-permute-done((bf16[128,1024]{1,0:T(8,128)(2,1)}, bf16[128,1024]{1,0:T(8,128)(2,1)S(1)}, u32[]{:S(2)}, u32[]{:S(2)}) %collective-permute-start.27) | collective-permute-done | bytes 262176 | tf_op jit(solution)/shard_map/ppermute | solution.py:32
  158.4 1.8 broadcast_select_fusion
  160.2 1.4 collective-permute-start.31
  161.6 2.2 %collective-permute-start.32 = (bf16[128,1024]{1,0:T(8,128)(2,1)S(1)}, bf16[128,1024]{1,0:T(8,128)(2,1)S(1)}, u32[]{:S(2)}, u32[]{:S(2)}) collective-permute-start(bf16[128,1024]{1,0:T(8,128)(2,1)S(1)} %get-tuple-element.20), channel_id=1, source_target_pairs={{0,3},{1,0},{2,1},{3,2},{4,7},{5,4},{6,5},{7,6},{8,11},{9,8},{10,9... | collective-permute-start | bytes 786440 | tf_op jit(solution)/shard_map/ppermute | solution.py:32
  163.8 1.5 collective-permute-start.33
  165.2 1.4 collective-permute-start.28
  166.6 5.7 %collective-permute-done.31.refs_6_ = bf16[128,1024]{1,0:T(8,128)(2,1)S(1)} collective-permute-done((bf16[128,1024]{1,0:T(8,128)(2,1)S(1)}, bf16[128,1024]{1,0:T(8,128)(2,1)S(1)}, u32[]{:S(2)}, u32[]{:S(2)}) %collective-permute-start.31) | collective-permute-done | bytes 262176 | tf_op jit(solution)/shard_map/ppermute | solution.py:32
  173.0 2.0 collective-permute-done.32.refs_7_
  175.8 2.3 %collective-permute-done.33.refs_8_ = bf16[128,1024]{1,0:T(8,128)(2,1)S(1)} collective-permute-done((bf16[128,1024]{1,0:T(8,128)(2,1)}, bf16[128,1024]{1,0:T(8,128)(2,1)S(1)}, u32[]{:S(2)}, u32[]{:S(2)}) %collective-permute-start.33) | collective-permute-done | bytes 262176 | tf_op jit(solution)/shard_map/ppermute | solution.py:32
  178.1 3.3 %collective-permute-done.28.refs_3_ = bf16[128,1024]{1,0:T(8,128)(2,1)} collective-permute-done((bf16[128,1024]{1,0:T(8,128)(2,1)S(1)}, bf16[128,1024]{1,0:T(8,128)(2,1)}, u32[]{:S(2)}, u32[]{:S(2)}) %collective-permute-start.28) | collective-permute-done | bytes 262176 | tf_op jit(solution)/shard_map/ppermute | solution.py:32
  181.4 4.6 %collective-permute-done.29.refs_4_ = bf16[128,1024]{1,0:T(8,128)(2,1)} collective-permute-done((bf16[128,1024]{1,0:T(8,128)(2,1)S(1)}, bf16[128,1024]{1,0:T(8,128)(2,1)}, u32[]{:S(2)}, u32[]{:S(2)}) %collective-permute-start.29) | collective-permute-done | bytes 262176 | tf_op jit(solution)/shard_map/ppermute | solution.py:32
  185.9 2.0 collective-permute-done.30.refs_5_
  188.0 11.7 %attention.3 = bf16[2,128,4096]{2,1,0:T(8,128)(2,1)} custom-call(s32[9]{0:T(128)} %stack.78.places, s32[1]{0:T(128)} %constant.161.clone.1.last, bf16[128,4096]{1,0:T(8,128)(2,1)} %copy-done.2, f32[128,4096]{1,0:T(8,128)} %collective-permute-done.25.x, s32[128,1]{1,0:T(8,128)} %copy.13.starts, ...), custom_call_target="tpu_custom_call", output_to_operand_aliasing={{}: (14, {})} | custom-call | flops 2415919104 | bytes 8650752 | tf_op jit(solution)/shard_map/attention/pallas_call | solution.py:258
  (98 shorter events, 10.3 us)
Async XLA Ops:
  6.5 92.8 %copy-start = (bf16[2,128,4096]{2,1,0:T(8,128)(2,1)S(1)}, bf16[2,128,4096]{2,1,0:T(8,128)(2,1)}, u32[]{:S(2)}) copy-start(bf16[2,128,4096]{2,1,0:T(8,128)(2,1)} %param.8) | copy-start | bytes 6291460
  6.5 38.5 %copy-start.17 = (f32[1,4096]{1,0:T(1,128)S(1)}, f32[1,4096]{1,0:T(1,128)}, u32[]{:S(2)}) copy-start(f32[1,4096]{1,0:T(1,128)} %param.9) | copy-start | bytes 49156
  6.5 63.5 %all-gather.3.cloned.1.call-start = ((), (), s32[]{:S(2)}) async-start(), calls=%async_computation | async-start | bytes 4456448 | tf_op jit(solution)/shard_map/all_gather | solution.py:297
  7.3 9.6 %collective-permute-start.1 = (bf16[256,512]{1,0:T(8,128)(2,1)}, bf16[256,512]{1,0:T(8,128)(2,1)S(1)}, u32[]{:S(2)}, u32[]{:S(2)}) collective-permute-start(bf16[256,512]{1,0:T(8,128)(2,1)} %bitcast.43), channel_id=1, source_target_pairs={{0,1},{1,2},{2,3},{3,0},{4,5},{5,6},{6,7},{7,4},{8,9},{9,10},{10,1... | collective-permute-start | bytes 786440 | tf_op jit(solution)/shard_map/ppermute | solution.py:32
  8.9 8.0 %collective-permute-start.3 = (bf16[256,512]{1,0:T(8,128)(2,1)}, bf16[256,512]{1,0:T(8,128)(2,1)S(1)}, u32[]{:S(2)}, u32[]{:S(2)}) collective-permute-start(bf16[256,512]{1,0:T(8,128)(2,1)} %bitcast.44), channel_id=1, source_target_pairs={{0,3},{1,0},{2,1},{3,2},{4,7},{5,4},{6,5},{7,6},{8,11},{9,8},{10,9... | collective-permute-start | bytes 786440 | tf_op jit(solution)/shard_map/ppermute | solution.py:32
  10.6 10.2 %collective-permute-start = (bf16[256,512]{1,0:T(8,128)(2,1)}, bf16[256,512]{1,0:T(8,128)(2,1)S(1)}, u32[]{:S(2)}, u32[]{:S(2)}) collective-permute-start(bf16[256,512]{1,0:T(8,128)(2,1)} %bitcast.45), channel_id=1, source_target_pairs={{0,4},{1,5},{2,6},{3,7},{4,8},{5,9},{6,10},{7,11},{8,12},{9,13},{1... | collective-permute-start | bytes 786440 | tf_op jit(solution)/shard_map/ppermute | solution.py:32
  12.5 8.3 %collective-permute-start.2 = (bf16[256,512]{1,0:T(8,128)(2,1)}, bf16[256,512]{1,0:T(8,128)(2,1)S(1)}, u32[]{:S(2)}, u32[]{:S(2)}) collective-permute-start(bf16[256,512]{1,0:T(8,128)(2,1)} %bitcast.46), channel_id=1, source_target_pairs={{0,12},{1,13},{2,14},{3,15},{4,0},{5,1},{6,2},{7,3},{8,4},{9,5},{1... | collective-permute-start | bytes 786440 | tf_op jit(solution)/shard_map/ppermute | solution.py:32
  16.9 29.5 %copy-start.3 = (bf16[256,512]{1,0:T(8,128)(2,1)}, bf16[256,512]{1,0:T(8,128)(2,1)S(1)}, u32[]{:S(2)}) copy-start(bf16[256,512]{1,0:T(8,128)(2,1)S(1)} %collective-permute-done.1.refs_2_) | copy-start | bytes 786436
  16.9 29.5 %copy-start.4 = (bf16[256,512]{1,0:T(8,128)(2,1)}, bf16[256,512]{1,0:T(8,128)(2,1)S(1)}, u32[]{:S(2)}) copy-start(bf16[256,512]{1,0:T(8,128)(2,1)S(1)} %collective-permute-done.3.refs_4_) | copy-start | bytes 786436
  17.7 13.0 %collective-permute-start.4 = (bf16[256,512]{1,0:T(8,128)(2,1)}, bf16[256,512]{1,0:T(8,128)(2,1)S(1)}, u32[]{:S(2)}, u32[]{:S(2)}) collective-permute-start(bf16[256,512]{1,0:T(8,128)(2,1)} %broadcast_select_fusion.7), channel_id=1, source_target_pairs={{1,2},{2,1},{3,0},{0,3},{5,6},{6,5},{7,4},{4,7},{9,10},{10,9},{11,... | collective-permute-start | bytes 786440 | tf_op jit(solution)/shard_map/ppermute | solution.py:45
  20.7 24.4 %copy-start.1 = (f32[1,128,4096]{2,1,0:T(8,128)S(1)}, f32[1,128,4096]{2,1,0:T(8,128)}, u32[]{:S(2)}) copy-start(f32[1,128,4096]{2,1,0:T(8,128)} %param.7) | copy-start | bytes 6291460
  20.7 25.6 %copy-start.5 = (bf16[256,512]{1,0:T(8,128)(2,1)}, bf16[256,512]{1,0:T(8,128)(2,1)S(1)}, u32[]{:S(2)}) copy-start(bf16[256,512]{1,0:T(8,128)(2,1)S(1)} %collective-permute-done.refs_1_) | copy-start | bytes 786436
  20.7 25.6 %copy-start.6 = (bf16[256,512]{1,0:T(8,128)(2,1)}, bf16[256,512]{1,0:T(8,128)(2,1)S(1)}, u32[]{:S(2)}) copy-start(bf16[256,512]{1,0:T(8,128)(2,1)S(1)} %collective-permute-done.2.refs_3_) | copy-start | bytes 786436
  20.8 14.0 %collective-permute-start.5 = (bf16[256,512]{1,0:T(8,128)(2,1)S(1)}, bf16[256,512]{1,0:T(8,128)(2,1)}, u32[]{:S(2)}, u32[]{:S(2)}) collective-permute-start(bf16[256,512]{1,0:T(8,128)(2,1)S(1)} %broadcast_select_fusion.6), channel_id=1, source_target_pairs={{0,4},{4,0},{8,12},{12,8},{1,5},{5,1},{9,13},{13,9},{2,6},{6,2},{1... | collective-permute-start | bytes 786440 | tf_op jit(solution)/shard_map/ppermute | solution.py:45
  22.8 14.7 %collective-permute-start.6 = (bf16[256,512]{1,0:T(8,128)(2,1)S(1)}, bf16[256,512]{1,0:T(8,128)(2,1)S(1)}, u32[]{:S(2)}, u32[]{:S(2)}) collective-permute-start(bf16[256,512]{1,0:T(8,128)(2,1)S(1)} %collective-permute-done.refs_1_), channel_id=1, source_target_pairs={{0,1},{1,2},{2,3},{3,0},{4,5},{5,6},{6,7},{7,4},{8,9},{9,10},{10,1... | collective-permute-start | bytes 786440 | tf_op jit(solution)/shard_map/ppermute | solution.py:32
  22.8 15.1 %collective-permute-start.7 = (bf16[256,512]{1,0:T(8,128)(2,1)S(1)}, bf16[256,512]{1,0:T(8,128)(2,1)S(1)}, u32[]{:S(2)}, u32[]{:S(2)}) collective-permute-start(bf16[256,512]{1,0:T(8,128)(2,1)S(1)} %collective-permute-done.2.refs_3_), channel_id=1, source_target_pairs={{0,3},{1,0},{2,1},{3,2},{4,7},{5,4},{6,5},{7,6},{8,11},{9,8},{10,9... | collective-permute-start | bytes 786440 | tf_op jit(solution)/shard_map/ppermute | solution.py:32
  26.0 14.7 %collective-permute-start.8 = (bf16[256,512]{1,0:T(8,128)(2,1)S(1)}, bf16[256,512]{1,0:T(8,128)(2,1)S(1)}, u32[]{:S(2)}, u32[]{:S(2)}) collective-permute-start(bf16[256,512]{1,0:T(8,128)(2,1)S(1)} %collective-permute-done.3.refs_4_), channel_id=1, source_target_pairs={{0,4},{1,5},{2,6},{3,7},{4,8},{5,9},{6,10},{7,11},{8,12},{9,13},{1... | collective-permute-start | bytes 786440 | tf_op jit(solution)/shard_map/ppermute | solution.py:32
  30.7 15.7 %copy-start.7 = (bf16[256,512]{1,0:T(8,128)(2,1)}, bf16[256,512]{1,0:T(8,128)(2,1)S(1)}, u32[]{:S(2)}) copy-start(bf16[256,512]{1,0:T(8,128)(2,1)S(1)} %collective-permute-done.4.refs_5_) | copy-start | bytes 786436
  30.7 12.8 %collective-permute-start.10 = (bf16[256,512]{1,0:T(8,128)(2,1)S(1)}, bf16[256,512]{1,0:T(8,128)(2,1)}, u32[]{:S(2)}, u32[]{:S(2)}) collective-permute-start(bf16[256,512]{1,0:T(8,128)(2,1)S(1)} %collective-permute-done.4.refs_5_), channel_id=1, source_target_pairs={{0,4},{1,5},{2,6},{3,7},{4,8},{5,9},{6,10},{7,11},{8,12},{9,13},{1... | collective-permute-start | bytes 786440 | tf_op jit(solution)/shard_map/ppermute | solution.py:32
  34.8 12.4 %collective-permute-start.9 = (bf16[256,512]{1,0:T(8,128)(2,1)S(1)}, bf16[256,512]{1,0:T(8,128)(2,1)}, u32[]{:S(2)}, u32[]{:S(2)}) collective-permute-start(bf16[256,512]{1,0:T(8,128)(2,1)S(1)} %collective-permute-done.1.refs_2_), channel_id=1, source_target_pairs={{0,12},{1,13},{2,14},{3,15},{4,0},{5,1},{6,2},{7,3},{8,4},{9,5},{1... | collective-permute-start | bytes 786440 | tf_op jit(solution)/shard_map/ppermute | solution.py:32
  37.5 9.7 %collective-permute-start.12 = (bf16[256,512]{1,0:T(8,128)(2,1)}, bf16[256,512]{1,0:T(8,128)(2,1)}, u32[]{:S(2)}, u32[]{:S(2)}) collective-permute-start(bf16[256,512]{1,0:T(8,128)(2,1)} %collective-permute-done.5.refs_6_), channel_id=1, source_target_pairs={{0,1},{1,2},{2,3},{3,0},{4,5},{5,6},{6,7},{7,4},{8,9},{9,10},{10,1... | collective-permute-start | bytes 786440 | tf_op jit(solution)/shard_map/ppermute | solution.py:32
  37.9 9.3 %collective-permute-start.13 = (bf16[256,512]{1,0:T(8,128)(2,1)}, bf16[256,512]{1,0:T(8,128)(2,1)}, u32[]{:S(2)}, u32[]{:S(2)}) collective-permute-start(bf16[256,512]{1,0:T(8,128)(2,1)} %collective-permute-done.5.refs_6_), channel_id=1, source_target_pairs={{0,3},{1,0},{2,1},{3,2},{4,7},{5,4},{6,5},{7,6},{8,11},{9,8},{10,9... | collective-permute-start | bytes 786440 | tf_op jit(solution)/shard_map/ppermute | solution.py:32
  40.7 11.6 %collective-permute-start.11 = (bf16[256,512]{1,0:T(8,128)(2,1)S(1)}, bf16[256,512]{1,0:T(8,128)(2,1)}, u32[]{:S(2)}, u32[]{:S(2)}) collective-permute-start(bf16[256,512]{1,0:T(8,128)(2,1)S(1)} %collective-permute-done.4.refs_5_), channel_id=1, source_target_pairs={{0,12},{1,13},{2,14},{3,15},{4,0},{5,1},{6,2},{7,3},{8,4},{9,5},{1... | collective-permute-start | bytes 786440 | tf_op jit(solution)/shard_map/ppermute | solution.py:32
  43.4 15.0 %collective-permute-start.14 = (bf16[256,512]{1,0:T(8,128)(2,1)}, bf16[256,512]{1,0:T(8,128)(2,1)}, u32[]{:S(2)}, u32[]{:S(2)}) collective-permute-start(bf16[256,512]{1,0:T(8,128)(2,1)} %collective-permute-done.10.refs_11_), channel_id=1, source_target_pairs={{0,4},{1,5},{2,6},{3,7},{4,8},{5,9},{6,10},{7,11},{8,12},{9,13},{1... | collective-permute-start | bytes 786440 | tf_op jit(solution)/shard_map/ppermute | solution.py:32
  74.5 11.0 %collective-permute-start.16 = (bf16[128,1024]{1,0:T(8,128)(2,1)}, bf16[128,1024]{1,0:T(8,128)(2,1)S(1)}, u32[]{:S(2)}, u32[]{:S(2)}) collective-permute-start(bf16[128,1024]{1,0:T(8,128)(2,1)} %projection.4.refs_0_), channel_id=1, source_target_pairs={{0,8},{1,9},{2,10},{3,11},{4,12},{5,13},{6,14},{7,15},{8,0},{9,1},... | collective-permute-start | bytes 786440 | tf_op jit(solution)/shard_map/ppermute | solution.py:32
  75.2 17.2 %collective-permute-start.23 = (f32[1,4096]{1,0:T(1,128)S(1)}, f32[1,4096]{1,0:T(1,128)S(1)}, u32[]{:S(2)}, u32[]{:S(2)}) collective-permute-start(f32[1,4096]{1,0:T(1,128)S(1)} %copy-done.17), channel_id=1, source_target_pairs={{16,0},{32,16},{48,32},{64,48},{80,64},{96,80},{112,96},{0,112},{1... | collective-permute-start | bytes 49160 | tf_op jit(solution)/shard_map/ppermute | solution.py:300
  75.7 15.9 %collective-permute-start.15 = (bf16[128,1024]{1,0:T(8,128)(2,1)}, bf16[128,1024]{1,0:T(8,128)(2,1)}, u32[]{:S(2)}, u32[]{:S(2)}) collective-permute-start(bf16[128,1024]{1,0:T(8,128)(2,1)} %projection.4.refs_0_), channel_id=1, source_target_pairs={{0,4},{1,5},{2,6},{3,7},{4,8},{5,9},{6,10},{7,11},{8,12},{9,13},{1... | collective-permute-start | bytes 786440 | tf_op jit(solution)/shard_map/ppermute | solution.py:32
  85.5 26.7 %copy-start.16 = (bf16[128,1024]{1,0:T(8,128)(2,1)}, bf16[128,1024]{1,0:T(8,128)(2,1)S(1)}, u32[]{:S(2)}) copy-start(bf16[128,1024]{1,0:T(8,128)(2,1)S(1)} %collective-permute-done.16.refs_2_) | copy-start | bytes 786436
  86.6 12.7 %collective-permute-start.20 = (bf16[128,1024]{1,0:T(8,128)(2,1)S(1)}, bf16[128,1024]{1,0:T(8,128)(2,1)}, u32[]{:S(2)}, u32[]{:S(2)}) collective-permute-start(bf16[128,1024]{1,0:T(8,128)(2,1)S(1)} %get-tuple-element.24), channel_id=1, source_target_pairs={{0,1},{1,2},{2,3},{3,0},{4,5},{5,6},{6,7},{7,4},{8,9},{9,10},{10,1... | collective-permute-start | bytes 786440 | tf_op jit(solution)/shard_map/ppermute | solution.py:32
  88.4 15.2 %collective-permute-start.21 = (bf16[128,1024]{1,0:T(8,128)(2,1)S(1)}, bf16[128,1024]{1,0:T(8,128)(2,1)S(1)}, u32[]{:S(2)}, u32[]{:S(2)}) collective-permute-start(bf16[128,1024]{1,0:T(8,128)(2,1)S(1)} %get-tuple-element.23), channel_id=1, source_target_pairs={{0,3},{1,0},{2,1},{3,2},{4,7},{5,4},{6,5},{7,6},{8,11},{9,8},{10,9... | collective-permute-start | bytes 786440 | tf_op jit(solution)/shard_map/ppermute | solution.py:32
  91.6 12.0 %collective-permute-start.22 = (bf16[128,1024]{1,0:T(8,128)(2,1)S(1)}, bf16[128,1024]{1,0:T(8,128)(2,1)S(1)}, u32[]{:S(2)}, u32[]{:S(2)}) collective-permute-start(bf16[128,1024]{1,0:T(8,128)(2,1)S(1)} %get-tuple-element.22), channel_id=1, source_target_pairs={{0,2},{1,3},{2,0},{3,1},{4,6},{5,7},{6,4},{7,5},{8,10},{9,11},{10,... | collective-permute-start | bytes 786440 | tf_op jit(solution)/shard_map/ppermute | solution.py:32
  91.6 19.6 %collective-permute-start.17 = (bf16[128,1024]{1,0:T(8,128)(2,1)}, bf16[128,1024]{1,0:T(8,128)(2,1)S(1)}, u32[]{:S(2)}, u32[]{:S(2)}) collective-permute-start(bf16[128,1024]{1,0:T(8,128)(2,1)} %collective-permute-done.15.refs_1_), channel_id=1, source_target_pairs={{0,1},{1,2},{2,3},{3,0},{4,5},{5,6},{6,7},{7,4},{8,9},{9,10},{10,1... | collective-permute-start | bytes 786440 | tf_op jit(solution)/shard_map/ppermute | solution.py:32
  92.4 19.8 %copy-start.25 = (f32[1,4096]{1,0:T(1,128)}, f32[1,4096]{1,0:T(1,128)S(1)}, u32[]{:S(2)}) copy-start(f32[1,4096]{1,0:T(1,128)S(1)} %collective-permute-done.23.refs_10_) | copy-start | bytes 49156
  92.4 19.8 %collective-permute-start.18 = (bf16[128,1024]{1,0:T(8,128)(2,1)}, bf16[128,1024]{1,0:T(8,128)(2,1)S(1)}, u32[]{:S(2)}, u32[]{:S(2)}) collective-permute-start(bf16[128,1024]{1,0:T(8,128)(2,1)} %collective-permute-done.15.refs_1_), channel_id=1, source_target_pairs={{0,3},{1,0},{2,1},{3,2},{4,7},{5,4},{6,5},{7,6},{8,11},{9,8},{10,9... | collective-permute-start | bytes 786440 | tf_op jit(solution)/shard_map/ppermute | solution.py:32
  99.4 12.8 %collective-permute-start.19 = (bf16[128,1024]{1,0:T(8,128)(2,1)}, bf16[128,1024]{1,0:T(8,128)(2,1)S(1)}, u32[]{:S(2)}, u32[]{:S(2)}) collective-permute-start(bf16[128,1024]{1,0:T(8,128)(2,1)} %collective-permute-done.15.refs_1_), channel_id=1, source_target_pairs={{0,2},{1,3},{2,0},{3,1},{4,6},{5,7},{6,4},{7,5},{8,10},{9,11},{10,... | collective-permute-start | bytes 786440 | tf_op jit(solution)/shard_map/ppermute | solution.py:32
  126.0 14.4 %collective-permute-start.24 = (bf16[128,4096]{1,0:T(8,128)(2,1)}, bf16[128,4096]{1,0:T(8,128)(2,1)S(1)}, u32[]{:S(2)}, u32[]{:S(2)}) collective-permute-start(bf16[128,4096]{1,0:T(8,128)(2,1)} %get-tuple-element.10), channel_id=1, source_target_pairs={{0,16},{16,32},{32,48},{48,64},{64,80},{80,96},{96,112},{112,0},{1... | collective-permute-start | bytes 3145736 | tf_op jit(solution)/shard_map/ppermute | solution.py:320
  140.4 47.5 %collective-permute-start.25 = (f32[128,4096]{1,0:T(8,128)}, f32[128,4096]{1,0:T(8,128)}, u32[]{:S(2)}, u32[]{:S(2)}) collective-permute-start(f32[128,4096]{1,0:T(8,128)} %get-tuple-element.13), channel_id=1, source_target_pairs={{0,16},{16,32},{32,48},{48,64},{64,80},{80,96},{96,112},{112,0},{1... | collective-permute-start | bytes 6291464 | tf_op jit(solution)/shard_map/ppermute | solution.py:322
  147.4 11.0 %collective-permute-start.27 = (bf16[128,1024]{1,0:T(8,128)(2,1)}, bf16[128,1024]{1,0:T(8,128)(2,1)S(1)}, u32[]{:S(2)}, u32[]{:S(2)}) collective-permute-start(bf16[128,1024]{1,0:T(8,128)(2,1)} %projection.5.refs_0_), channel_id=1, source_target_pairs={{0,8},{1,9},{2,10},{3,11},{4,12},{5,13},{6,14},{7,15},{8,0},{9,1},... | collective-permute-start | bytes 786440 | tf_op jit(solution)/shard_map/ppermute | solution.py:32
  148.1 17.1 %collective-permute-start.26 = (bf16[128,1024]{1,0:T(8,128)(2,1)}, bf16[128,1024]{1,0:T(8,128)(2,1)S(1)}, u32[]{:S(2)}, u32[]{:S(2)}) collective-permute-start(bf16[128,1024]{1,0:T(8,128)(2,1)} %projection.5.refs_0_), channel_id=1, source_target_pairs={{0,4},{1,5},{2,6},{3,7},{4,8},{5,9},{6,10},{7,11},{8,12},{9,13},{1... | collective-permute-start | bytes 786440 | tf_op jit(solution)/shard_map/ppermute | solution.py:32
  158.4 29.6 %copy-start.11 = (bf16[128,1024]{1,0:T(8,128)(2,1)}, bf16[128,1024]{1,0:T(8,128)(2,1)S(1)}, u32[]{:S(2)}) copy-start(bf16[128,1024]{1,0:T(8,128)(2,1)S(1)} %collective-permute-done.27.refs_2_) | copy-start | bytes 786436
  160.2 12.2 %collective-permute-start.31 = (bf16[128,1024]{1,0:T(8,128)(2,1)S(1)}, bf16[128,1024]{1,0:T(8,128)(2,1)S(1)}, u32[]{:S(2)}, u32[]{:S(2)}) collective-permute-start(bf16[128,1024]{1,0:T(8,128)(2,1)S(1)} %get-tuple-element.21), channel_id=1, source_target_pairs={{0,1},{1,2},{2,3},{3,0},{4,5},{5,6},{6,7},{7,4},{8,9},{9,10},{10,1... | collective-permute-start | bytes 786440 | tf_op jit(solution)/shard_map/ppermute | solution.py:32
  161.6 13.5 %collective-permute-start.32 = (bf16[128,1024]{1,0:T(8,128)(2,1)S(1)}, bf16[128,1024]{1,0:T(8,128)(2,1)S(1)}, u32[]{:S(2)}, u32[]{:S(2)}) collective-permute-start(bf16[128,1024]{1,0:T(8,128)(2,1)S(1)} %get-tuple-element.20), channel_id=1, source_target_pairs={{0,3},{1,0},{2,1},{3,2},{4,7},{5,4},{6,5},{7,6},{8,11},{9,8},{10,9... | collective-permute-start | bytes 786440 | tf_op jit(solution)/shard_map/ppermute | solution.py:32
  163.8 14.3 %collective-permute-start.33 = (bf16[128,1024]{1,0:T(8,128)(2,1)}, bf16[128,1024]{1,0:T(8,128)(2,1)S(1)}, u32[]{:S(2)}, u32[]{:S(2)}) collective-permute-start(bf16[128,1024]{1,0:T(8,128)(2,1)} %get-tuple-element.19), channel_id=1, source_target_pairs={{0,2},{1,3},{2,0},{3,1},{4,6},{5,7},{6,4},{7,5},{8,10},{9,11},{10,... | collective-permute-start | bytes 786440 | tf_op jit(solution)/shard_map/ppermute | solution.py:32
  165.2 22.7 %copy-start.12 = (bf16[128,1024]{1,0:T(8,128)(2,1)}, bf16[128,1024]{1,0:T(8,128)(2,1)S(1)}, u32[]{:S(2)}) copy-start(bf16[128,1024]{1,0:T(8,128)(2,1)S(1)} %collective-permute-done.26.refs_1_) | copy-start | bytes 786436
  165.2 16.1 %collective-permute-start.28 = (bf16[128,1024]{1,0:T(8,128)(2,1)S(1)}, bf16[128,1024]{1,0:T(8,128)(2,1)}, u32[]{:S(2)}, u32[]{:S(2)}) collective-permute-start(bf16[128,1024]{1,0:T(8,128)(2,1)S(1)} %collective-permute-done.26.refs_1_), channel_id=1, source_target_pairs={{0,1},{1,2},{2,3},{3,0},{4,5},{5,6},{6,7},{7,4},{8,9},{9,10},{10,1... | collective-permute-start | bytes 786440 | tf_op jit(solution)/shard_map/ppermute | solution.py:32
  172.4 15.6 %copy-start.13 = (bf16[128,1024]{1,0:T(8,128)(2,1)}, bf16[128,1024]{1,0:T(8,128)(2,1)S(1)}, u32[]{:S(2)}) copy-start(bf16[128,1024]{1,0:T(8,128)(2,1)S(1)} %collective-permute-done.31.refs_6_) | copy-start | bytes 786436
  172.4 13.5 %collective-permute-start.29 = (bf16[128,1024]{1,0:T(8,128)(2,1)S(1)}, bf16[128,1024]{1,0:T(8,128)(2,1)}, u32[]{:S(2)}, u32[]{:S(2)}) collective-permute-start(bf16[128,1024]{1,0:T(8,128)(2,1)S(1)} %collective-permute-done.26.refs_1_), channel_id=1, source_target_pairs={{0,3},{1,0},{2,1},{3,2},{4,7},{5,4},{6,5},{7,6},{8,11},{9,8},{10,9... | collective-permute-start | bytes 786440 | tf_op jit(solution)/shard_map/ppermute | solution.py:32
  175.0 12.9 %collective-permute-start.30 = (bf16[128,1024]{1,0:T(8,128)(2,1)S(1)}, bf16[128,1024]{1,0:T(8,128)(2,1)}, u32[]{:S(2)}, u32[]{:S(2)}) collective-permute-start(bf16[128,1024]{1,0:T(8,128)(2,1)S(1)} %collective-permute-done.26.refs_1_), channel_id=1, source_target_pairs={{0,2},{1,3},{2,0},{3,1},{4,6},{5,7},{6,4},{7,5},{8,10},{9,11},{10,... | collective-permute-start | bytes 786440 | tf_op jit(solution)/shard_map/ppermute | solution.py:32
  (13 other events, 71.7 us)
Sparse Core Ops, SparseCore 0:
  9.5 60.4 all-gather.2

commit v3 on v2

--- a/solution.py
+++ b/solution.py
@@ -17,7 +17,8 @@
 EPSILON = 1e-05
 MASK_FLOOR = -1e30
 SIDE = 4
-VMEM = 56 << 20
+VMEM = 28 << 20
+TOGETHER = 4
 DEPTH = 256
 SCALE = HEAD_SIZE ** (-0.5)
 LOG2E = 1.4426950408889634
@@ -71,13 +72,14 @@
 
 
 def window_blocks(own, y):
-    up1, up2 = moved(own, 1, 0), moved(own, 2, 0)
+    up1 = moved(own, 1, 0)
+    up2 = moved(up1, 1, 0)
     above = [moved(up1, 0, 1), moved(up1, 0, -1), moved(up1, 0, 2)]
     to_right = jnp.where(y == SIDE - 1, up2, own)
     to_left = jnp.where(y == 0, own, up2)
     across = jnp.where(y < 2, own, up2)
     near = [moved(to_right, 0, 1), moved(to_left, 0, -1), moved(across, 0, 2)]
-    return [own, up1, up2, *above, *near]
+    return [own, up1, up2, *above], near
 
 
 def fetched(blocks, into, sems, first=0):
@@ -166,31 +168,32 @@
     )(*operands)
 
 
-def attention_body(n_blocks, last_tick, places, last, q, x, starts, *refs):
+def attention_body(n_blocks, stage, places, last, q, starts, *refs):
     blocks, refs = refs[:n_blocks], refs[n_blocks:]
-    if last_tick:
-        _, produced = refs
+    if stage == "first":
+        out_mix, out_sum, out_high = refs
+    elif stage == "last":
+        x, mix, sums, highs, _, produced = refs
     else:
-        first, gain, produced, stream, normed, rows = refs
+        x, mix, sums, highs, first, gain, produced, stream, normed, rows = refs
     g = pl.program_id(0)
     tokens = q.shape[0]
-
     column = lax.broadcasted_iota(jnp.int32, (tokens, tokens), 1)
     row = lax.broadcasted_iota(jnp.int32, (tokens, tokens), 0)
     low = jnp.broadcast_to(starts[...], (tokens, tokens))
     bias = []
     for b in range(n_blocks):
         allowed = column - places[b] * tokens >= low
-        if b == 0:
+        if stage == "first" and b == 0:
             allowed = allowed & (column <= row)
         bias.append(jnp.where(allowed, 0.0, MASK_FLOOR))
     bias = jnp.concatenate(bias, axis=1)
-    bias = jnp.concatenate([bias, bias], axis=0)
+    bias = jnp.concatenate([bias] * TOGETHER, axis=0)
     k = jnp.concatenate([block[:, :HEAD_SIZE] for block in blocks], axis=0)
     v = jnp.concatenate([block[:, HEAD_SIZE:] for block in blocks], axis=0)
     v = jnp.concatenate([v, jnp.ones_like(v)], axis=1)
-    for h in range(0, HEAD_GROUPS, 2):
-        qs = [q[:, (h + j) * HEAD_SIZE : (h + j + 1) * HEAD_SIZE] for j in range(2)]
+    for h in range(0, HEAD_GROUPS, TOGETHER):
+        qs = [q[:, (h + j) * HEAD_SIZE : (h + j + 1) * HEAD_SIZE] for j in range(TOGETHER)]
         s = lax.dot_general(
             jnp.concatenate(qs, axis=0),
             k,
@@ -198,20 +201,36 @@
             preferred_element_type=jnp.float32,
         )
         s = s + bias
+        here = slice(h * tokens, (h + TOGETHER) * tokens)
         high = jnp.max(s, axis=1, keepdims=True)
-        p = jnp.exp2((s - high) * (SCALE * LOG2E)).astype(jnp.bfloat16)
+        high = jnp.broadcast_to(high, (high.shape[0], HEAD_SIZE))
+        if stage != "first":
+            before = highs[here]
+            high = jnp.maximum(high, before)
+        p = jnp.concatenate(
+            [
+                jnp.exp2((s[:, c : c + HEAD_SIZE] - high) * (SCALE * LOG2E))
+                for c in range(0, s.shape[1], HEAD_SIZE)
+            ],
+            axis=1,
+        ).astype(jnp.bfloat16)
         mixed = jnp.dot(p, v, preferred_element_type=jnp.float32)
-        out = mixed[:, :HEAD_SIZE] / mixed[:, HEAD_SIZE:]
-        for j in range(2):
+        mixed, total = mixed[:, :HEAD_SIZE], mixed[:, HEAD_SIZE:]
+        if stage == "first":
+            out_mix[here], out_sum[here], out_high[here] = mixed, total, high
+            continue
+        kept = jnp.exp2((before - high) * (SCALE * LOG2E))
+        out = (mixed + mix[here] * kept) / (total + sums[here] * kept)
+        for j in range(TOGETHER):
             where = slice((h + j) * HEAD_SIZE, (h + j + 1) * HEAD_SIZE)
             new = x[:, where] + out[j * tokens : (j + 1) * tokens]
             produced[0, :, where] = new.astype(jnp.bfloat16)
-            if not last_tick:
+            if stage != "last":
                 new = jnp.where(last[0] == 1, first[:, where].astype(jnp.float32), new)
                 stream[:, where] = new
                 at = pl.multiple_of(g * GROUP_WIDTH, GROUP_WIDTH) + (h + j) * HEAD_SIZE
                 rows[:, pl.ds(at, HEAD_SIZE)] = new
-    if last_tick:
+    if stage != "onward":
         return
 
     @pl.when(g == KEY_VALUE_HEADS - 1)
@@ -227,26 +246,34 @@
             normed[:, at] = (rows[:, at] * factor * gain[:, at]).astype(jnp.bfloat16)
 
 
-def attention(blocks, places, q, x, starts, tick, onward=None, produced=None):
+def attention(blocks, places, q, starts, part=None, x=None, onward=None, produced=None):
     tokens, width = q.shape
     n_blocks = len(blocks)
-    span = sum(block.shape[0] for block in blocks)
-    last_tick = onward is None
-    flag = jnp.zeros((1,), jnp.int32) if last_tick else onward[0]
+    span = n_blocks * tokens
+    stage = "first" if part is None else "last" if onward is None else "onward"
+    flag = jnp.zeros((1,), jnp.int32) if onward is None else onward[0]
     whole = lambda g, *_: (0, 0)
     by_group = pl.BlockSpec((tokens, GROUP_WIDTH), lambda g, *_: (0, g))
-    in_specs = [by_group, by_group, pl.BlockSpec((tokens, 1), whole)]
+    by_rows = pl.BlockSpec((HEAD_GROUPS * tokens, HEAD_SIZE), lambda g, *_: (g, 0))
+    in_specs = [by_group, pl.BlockSpec((tokens, 1), whole)]
     in_specs += [pl.BlockSpec((tokens, 2 * HEAD_SIZE), lambda g, *_: (0, g))] * n_blocks
-    out_specs = [pl.BlockSpec((1, tokens, GROUP_WIDTH), lambda g, *_: (tick, 0, g))]
-    out_shape = [jax.ShapeDtypeStruct((W, tokens, width), jnp.bfloat16)]
-    operands = [q, x, starts, *blocks]
+    operands = [q, starts, *blocks]
     scratch = []
     aliases = {}
-    if last_tick:
+    if stage == "first":
+        out_specs = [by_rows] * 3
+        out_shape = [jax.ShapeDtypeStruct((QUERY_HEADS * tokens, HEAD_SIZE), jnp.float32)] * 3
+    else:
+        tick = 0 if stage == "onward" else W - 1
+        in_specs += [by_group] + [by_rows] * 3
+        operands += [x, *part]
+        out_specs = [pl.BlockSpec((1, tokens, GROUP_WIDTH), lambda g, *_: (tick, 0, g))]
+        out_shape = [jax.ShapeDtypeStruct((W, tokens, width), jnp.bfloat16)]
+    if stage == "last":
         aliases = {2 + len(operands): 0}
         in_specs += [pl.BlockSpec(memory_space=pl.ANY)]
         operands += [produced]
-    else:
+    if stage == "onward":
         in_specs += [by_group, pl.BlockSpec((1, width), whole)]
         operands += [onward[1], onward[2]]
         out_specs += [by_group, pl.BlockSpec((tokens, width), whole)]
@@ -256,7 +283,7 @@
         ]
         scratch += [pltpu.VMEM((tokens, width), jnp.float32)]
     return pl.pallas_call(
-        functools.partial(attention_body, n_blocks, last_tick),
+        functools.partial(attention_body, n_blocks, stage),
         grid_spec=pltpu.PrefetchScalarGridSpec(
             num_scalar_prefetch=2,
             grid=(KEY_VALUE_HEADS,),
@@ -313,16 +340,18 @@
     places = window_places(y)
     keys = projection(normed, order, key_blocks)
     own = projection(normed, order, (), keys, value_weights)
-    blocks = window_blocks(own, y)
+    early, late = window_blocks(own, y)
+    part = attention(early, places[: len(early)], normed, starts[0])
     produced, stream, normed = attention(
-        blocks, places, normed, stream, starts[0], 0, (is_last, first, next_gain)
+        late, places[len(early) :], normed, starts[0], part, stream, (is_last, first, next_gain)
     )
     normed = lax.ppermute(normed, "section", onward)
     normed, stream = lax.optimization_barrier((normed, stream))
     stream = lax.ppermute(stream, "section", onward)
     own = projection(normed, order, key_blocks, None, value_weights)
-    blocks = window_blocks(own, y)
-    (produced,) = attention(blocks, places, normed, stream, starts[1], 1, None, produced)
+    early, late = window_blocks(own, y)
+    part = attention(early, places[: len(early)], normed, starts[1])
+    (produced,) = attention(late, places[len(early) :], normed, starts[1], part, stream, None, produced)
     return produced[:, None]
 
 

time: 207 us -> 192 us (0.928); the launches traced: 207 us -> 189 us
  waiting for transfers between devices: 92.8 us -> 69.2 us
  local copies, waits for them, and re-layouts: 5.97 us -> 18.7 us
  starting transfers between devices: 47.2 us -> 42.6 us
    ppermute x29, waiting for transfers between devices: 65.9 us -> 49.1 us  [moved(): return lax.ppermute(block, 'ctx', pairs)]
    unnamed x52 -> x76, local copies, waits for them, and re-layouts: 1.83 us -> 17 us
    all_gather x1, waiting for transfers between devices: 7.13 us -> 0.73 us  [shards(): value_weights = lax.all_gather(value_rows[0], 'ctx', axis=0, tiled=True)]
    pallas_call x3, Pallas kernels: 14.9 us -> 10 us  [projection(): pl.pallas_call(functools.partial(projection_body, n_keys, keys is not Non...]
    pallas_call x2 -> x4, Pallas kernels: 24.6 us -> 29.4 us  [attention(): pl.pallas_call(functools.partial(attention_body, n_blocks, stage), grid_s...]
    ppermute x29, starting transfers between devices: 42.2 us -> 37.7 us  [moved(): return lax.ppermute(block, 'ctx', pairs)]
  transfers between devices with their start and end apart: 35 -> 35, of which waited for: 18 -> 14; matrix products, arithmetic and copies ran while one was open for 5% -> 4% of each run, Pallas kernels for 5% -> 12%
where the time goes in v3:
time: 192 us; the launch traced here: 189 us
  waiting for transfers between devices  69.2 us (36%)
  starting transfers between devices  42.6 us (22%)
  Pallas kernels  39.4 us (21%)
  local copies, waits for them, and re-layouts  18.7 us (10%)
  between operations  14.3 us (7%)
  other arithmetic  5.33 us (3%)
    ppermute x29, waiting for transfers between devices, moved(): return lax.ppermute(block, 'ctx', pairs)  49.1 us
    ppermute x29, starting transfers between devices, moved(): return lax.ppermute(block, 'ctx', pairs)  37.7 us
    pallas_call x4, Pallas kernels, attention(): pl.pallas_call(functools.partial(attention_body, n_blocks, stage), grid_s...  29.4 us
    unnamed x76, local copies, waits for them, and re-layouts  17 us
    ppermute x1, waiting for transfers between devices, shards(): normed = lax.ppermute(normed, 'section', onward)  14.2 us
    pallas_call x3, Pallas kernels, projection(): pl.pallas_call(functools.partial(projection_body, n_keys, keys is not Non...  10 us
    ppermute x2, starting transfers between devices, swapped(): return lax.ppermute(block, 'ctx', pairs)  4.97 us
    ppermute x2, waiting for transfers between devices, swapped(): return lax.ppermute(block, 'ctx', pairs)  4.46 us
  transfers between devices with their start and end apart: 35, of which 14 were waited for; matrix products, arithmetic and copies ran while one was open for 4% of the time, Pallas kernels for 12%

profile of v3, /device:TPU:2, one launch (start us, length us, event | category | flops | bytes accessed | tf_op | source)
XLA Modules:
  0.0 189.4 jit_solution(15630767245242950912)
XLA Ops:
  7.3 1.6 collective-permute-start.1
  8.9 1.7 collective-permute-start.3
  10.6 1.9 %collective-permute-start = (bf16[256,512]{1,0:T(8,128)(2,1)}, bf16[256,512]{1,0:T(8,128)(2,1)S(1)}, u32[]{:S(2)}, u32[]{:S(2)}) collective-permute-start(bf16[256,512]{1,0:T(8,128)(2,1)} %bitcast.45), channel_id=1, source_target_pairs={{0,4},{1,5},{2,6},{3,7},{4,8},{5,9},{6,10},{7,11},{8,12},{9,13},{1... | collective-permute-start | bytes 786440 | tf_op jit(solution)/shard_map/ppermute | solution.py:33
  12.5 2.1 %collective-permute-start.2 = (bf16[256,512]{1,0:T(8,128)(2,1)}, bf16[256,512]{1,0:T(8,128)(2,1)S(1)}, u32[]{:S(2)}, u32[]{:S(2)}) collective-permute-start(bf16[256,512]{1,0:T(8,128)(2,1)} %bitcast.46), channel_id=1, source_target_pairs={{0,12},{1,13},{2,14},{3,15},{4,0},{5,1},{6,2},{7,3},{8,4},{9,5},{1... | collective-permute-start | bytes 786440 | tf_op jit(solution)/shard_map/ppermute | solution.py:33
  14.6 2.3 %collective-permute-done.1.refs_2_ = bf16[256,512]{1,0:T(8,128)(2,1)S(1)} collective-permute-done((bf16[256,512]{1,0:T(8,128)(2,1)}, bf16[256,512]{1,0:T(8,128)(2,1)S(1)}, u32[]{:S(2)}, u32[]{:S(2)}) %collective-permute-start.1) | collective-permute-done | bytes 262176 | tf_op jit(solution)/shard_map/ppermute | solution.py:33
  17.7 3.0 %collective-permute-start.4 = (bf16[256,512]{1,0:T(8,128)(2,1)}, bf16[256,512]{1,0:T(8,128)(2,1)}, u32[]{:S(2)}, u32[]{:S(2)}) collective-permute-start(bf16[256,512]{1,0:T(8,128)(2,1)} %broadcast_select_fusion.5), channel_id=1, source_target_pairs={{1,2},{2,1},{3,0},{0,3},{5,6},{6,5},{7,4},{4,7},{9,10},{10,9},{11,... | collective-permute-start | bytes 786440 | tf_op jit(solution)/shard_map/ppermute | solution.py:46
  20.8 2.0 %collective-permute-start.5 = (bf16[256,512]{1,0:T(8,128)(2,1)S(1)}, bf16[256,512]{1,0:T(8,128)(2,1)}, u32[]{:S(2)}, u32[]{:S(2)}) collective-permute-start(bf16[256,512]{1,0:T(8,128)(2,1)S(1)} %broadcast_select_fusion.4), channel_id=1, source_target_pairs={{0,4},{4,0},{8,12},{12,8},{1,5},{5,1},{9,13},{13,9},{2,6},{6,2},{1... | collective-permute-start | bytes 786440 | tf_op jit(solution)/shard_map/ppermute | solution.py:46
  22.7 3.2 %collective-permute-start.7 = (bf16[256,512]{1,0:T(8,128)(2,1)S(1)}, bf16[256,512]{1,0:T(8,128)(2,1)S(1)}, u32[]{:S(2)}, u32[]{:S(2)}) collective-permute-start(bf16[256,512]{1,0:T(8,128)(2,1)S(1)} %collective-permute-done.2.refs_3_), channel_id=1, source_target_pairs={{0,3},{1,0},{2,1},{3,2},{4,7},{5,4},{6,5},{7,6},{8,11},{9,8},{10,9... | collective-permute-start | bytes 786440 | tf_op jit(solution)/shard_map/ppermute | solution.py:33
  26.1 4.5 %collective-permute-done.4.refs_5_ = bf16[256,512]{1,0:T(8,128)(2,1)} collective-permute-done((bf16[256,512]{1,0:T(8,128)(2,1)}, bf16[256,512]{1,0:T(8,128)(2,1)}, u32[]{:S(2)}, u32[]{:S(2)}) %collective-permute-start.4) | collective-permute-done | bytes 262176 | tf_op jit(solution)/shard_map/ppermute | solution.py:46
  30.6 2.4 %collective-permute-start.10 = (bf16[256,512]{1,0:T(8,128)(2,1)}, bf16[256,512]{1,0:T(8,128)(2,1)}, u32[]{:S(2)}, u32[]{:S(2)}) collective-permute-start(bf16[256,512]{1,0:T(8,128)(2,1)} %collective-permute-done.4.refs_5_), channel_id=1, source_target_pairs={{0,4},{1,5},{2,6},{3,7},{4,8},{5,9},{6,10},{7,11},{8,12},{9,13},{1... | collective-permute-start | bytes 786440 | tf_op jit(solution)/shard_map/ppermute | solution.py:33
  33.0 1.8 multiply_reduce_fusion
  34.8 2.6 %collective-permute-start.9 = (bf16[256,512]{1,0:T(8,128)(2,1)S(1)}, bf16[256,512]{1,0:T(8,128)(2,1)}, u32[]{:S(2)}, u32[]{:S(2)}) collective-permute-start(bf16[256,512]{1,0:T(8,128)(2,1)S(1)} %collective-permute-done.1.refs_2_), channel_id=1, source_target_pairs={{0,12},{1,13},{2,14},{3,15},{4,0},{5,1},{6,2},{7,3},{8,4},{9,5},{1... | collective-permute-start | bytes 786440 | tf_op jit(solution)/shard_map/ppermute | solution.py:33
  39.3 2.8 %collective-permute-start.13 = (bf16[256,512]{1,0:T(8,128)(2,1)}, bf16[256,512]{1,0:T(8,128)(2,1)}, u32[]{:S(2)}, u32[]{:S(2)}) collective-permute-start(bf16[256,512]{1,0:T(8,128)(2,1)} %collective-permute-done.5.refs_6_), channel_id=1, source_target_pairs={{0,3},{1,0},{2,1},{3,2},{4,7},{5,4},{6,5},{7,6},{8,11},{9,8},{10,9... | collective-permute-start | bytes 786440 | tf_op jit(solution)/shard_map/ppermute | solution.py:33
  42.8 2.7 %collective-permute-start.11 = (bf16[256,512]{1,0:T(8,128)(2,1)}, bf16[256,512]{1,0:T(8,128)(2,1)}, u32[]{:S(2)}, u32[]{:S(2)}) collective-permute-start(bf16[256,512]{1,0:T(8,128)(2,1)} %collective-permute-done.4.refs_5_), channel_id=1, source_target_pairs={{0,12},{1,13},{2,14},{3,15},{4,0},{5,1},{6,2},{7,3},{8,4},{9,5},{1... | collective-permute-start | bytes 786440 | tf_op jit(solution)/shard_map/ppermute | solution.py:33
  46.3 2.8 %collective-permute-done.13.refs_14_ = bf16[256,512]{1,0:T(8,128)(2,1)} collective-permute-done((bf16[256,512]{1,0:T(8,128)(2,1)}, bf16[256,512]{1,0:T(8,128)(2,1)}, u32[]{:S(2)}, u32[]{:S(2)}) %collective-permute-start.13) | collective-permute-done | bytes 262176 | tf_op jit(solution)/shard_map/ppermute | solution.py:33
  49.0 6.6 %collective-permute-done.11.refs_12_ = bf16[256,512]{1,0:T(8,128)(2,1)} collective-permute-done((bf16[256,512]{1,0:T(8,128)(2,1)}, bf16[256,512]{1,0:T(8,128)(2,1)}, u32[]{:S(2)}, u32[]{:S(2)}) %collective-permute-start.11) | collective-permute-done | bytes 262176 | tf_op jit(solution)/shard_map/ppermute | solution.py:33
  55.7 4.2 %collective-permute-done.14.refs_15_ = bf16[256,512]{1,0:T(8,128)(2,1)} collective-permute-done((bf16[256,512]{1,0:T(8,128)(2,1)}, bf16[256,512]{1,0:T(8,128)(2,1)}, u32[]{:S(2)}, u32[]{:S(2)}) %collective-permute-start.14) | collective-permute-done | bytes 262176 | tf_op jit(solution)/shard_map/ppermute | solution.py:33
  59.8 0.9 copy-done.7
  60.8 0.9 copy-done.10
  61.7 1.0 copy-done.13
  62.7 0.9 copy-done.15
  64.6 1.0 copy-done.21
  66.5 2.7 %projection.3.refs_0_ = bf16[128,512]{1,0:T(8,128)(2,1)S(1)} custom-call(s32[16]{0:T(128)S(1)} %stack.94.order, bf16[128,4096]{1,0:T(8,128)(2,1)S(1)} %multiply_convert_fusion.rows.q, bf16[256,512]{1,0:T(8,128)(2,1)S(1)} %bitcast.47, bf16[256,512]{1,0:T(8,128)(2,1)S(1)} %copy-done.10, bf16[256,512]{1,0:T(8,128)(2,1)S(1)} %collective-permute-done.1.refs_2_, ...), custom_call_target="tpu_custom_call" | custom-call | flops 536870912 | bytes 4194304 | tf_op jit(solution)/shard_map/projection/pallas_call | solution.py:155
  70.0 2.2 %copy-done.3 = bf16[1,4096,512]{2,1,0:T(8,128)(2,1)S(1)} copy-done((bf16[1,4096,512]{2,1,0:T(8,128)(2,1)S(1)}, bf16[1,4096,512]{2,1,0:T(8,128)(2,1)}, u32[]{:S(2)}) %copy-start.3) | copy-done | bytes 4194328
  72.1 3.1 %projection.4.refs_0_ = bf16[128,1024]{1,0:T(8,128)(2,1)} custom-call(s32[16]{0:T(128)S(1)} %stack.94.order, bf16[128,4096]{1,0:T(8,128)(2,1)S(1)} %multiply_convert_fusion.rows.q, bf16[128,512]{1,0:T(8,128)(2,1)S(1)} %projection.3.refs_0_, bf16[4096,512]{1,0:T(8,128)(2,1)S(1)} %bitcast.41), custom_call_target="tpu_custom_call" | custom-call | flops 536870912 | bytes 4194304 | tf_op jit(solution)/shard_map/projection/pallas_call | solution.py:155
  75.3 1.0 dynamic-slice_bitcast_fusion.refs_7_
  76.8 8.3 %collective-permute-done.15.refs_1_ = bf16[128,1024]{1,0:T(8,128)(2,1)} collective-permute-done((bf16[128,1024]{1,0:T(8,128)(2,1)}, bf16[128,1024]{1,0:T(8,128)(2,1)}, u32[]{:S(2)}, u32[]{:S(2)}) %collective-permute-start.15) | collective-permute-done | bytes 262176 | tf_op jit(solution)/shard_map/ppermute | solution.py:33
  85.6 3.2 %collective-permute-start.21 = (bf16[128,1024]{1,0:T(8,128)(2,1)}, bf16[128,1024]{1,0:T(8,128)(2,1)S(1)}, u32[]{:S(2)}, u32[]{:S(2)}) collective-permute-start(bf16[128,1024]{1,0:T(8,128)(2,1)} %collective-permute-done.15.refs_1_), channel_id=1, source_target_pairs={{0,3},{1,0},{2,1},{3,2},{4,7},{5,4},{6,5},{7,6},{8,11},{9,8},{10,9... | collective-permute-start | bytes 786440 | tf_op jit(solution)/shard_map/ppermute | solution.py:33
  88.7 5.3 %collective-permute-done.16.refs_2_ = bf16[128,1024]{1,0:T(8,128)(2,1)} collective-permute-done((bf16[128,1024]{1,0:T(8,128)(2,1)}, bf16[128,1024]{1,0:T(8,128)(2,1)}, u32[]{:S(2)}, u32[]{:S(2)}) %collective-permute-start.16) | collective-permute-done | bytes 262176 | tf_op jit(solution)/shard_map/ppermute | solution.py:33
  94.0 1.1 broadcast_select_fusion.1
  95.2 3.2 %collective-permute-start.18 = (bf16[128,1024]{1,0:T(8,128)(2,1)S(1)}, bf16[128,1024]{1,0:T(8,128)(2,1)S(1)}, u32[]{:S(2)}, u32[]{:S(2)}) collective-permute-start(bf16[128,1024]{1,0:T(8,128)(2,1)S(1)} %get-tuple-element.35), channel_id=1, source_target_pairs={{0,3},{1,0},{2,1},{3,2},{4,7},{5,4},{6,5},{7,6},{8,11},{9,8},{10,9... | collective-permute-start | bytes 786440 | tf_op jit(solution)/shard_map/ppermute | solution.py:33
  98.4 2.3 %collective-permute-done.20.refs_3_ = bf16[128,1024]{1,0:T(8,128)(2,1)} collective-permute-done((bf16[128,1024]{1,0:T(8,128)(2,1)}, bf16[128,1024]{1,0:T(8,128)(2,1)}, u32[]{:S(2)}, u32[]{:S(2)}) %collective-permute-start.20) | collective-permute-done | bytes 262176 | tf_op jit(solution)/shard_map/ppermute | solution.py:33
  100.9 8.1 %attention.4 = (f32[4096,128]{1,0:T(8,128)S(1)}, f32[4096,128]{1,0:T(8,128)S(1)}, f32[4096,128]{1,0:T(8,128)S(1)}) custom-call(s32[6]{0:T(128)S(1)} %stack.98.places, s32[1]{0:T(128)} %constant.168.clone.1.last, bf16[128,4096]{1,0:T(8,128)(2,1)S(1)} %multiply_convert_fusion.rows.q, s32[128,1]{1,0:T(8,128)S(1)} %copy.15.starts, ...), custom_call_target="tpu_custom_call" | custom-call | flops 1610612736 | bytes 7864320 | tf_op jit(solution)/shard_map/attention/pallas_call | solution.py:285
  109.0 1.9 %collective-permute-done.17.refs_0_ = bf16[128,1024]{1,0:T(8,128)(2,1)S(1)} collective-permute-done((bf16[128,1024]{1,0:T(8,128)(2,1)S(1)}, bf16[128,1024]{1,0:T(8,128)(2,1)S(1)}, u32[]{:S(2)}, u32[]{:S(2)}) %collective-permute-start.17) | collective-permute-done | bytes 262176 | tf_op jit(solution)/shard_map/ppermute | solution.py:33
  111.0 6.8 %attention.5 = (bf16[2,128,4096]{2,1,0:T(8,128)(2,1)}, f32[128,4096]{1,0:T(8,128)}, bf16[128,4096]{1,0:T(8,128)(2,1)S(1)}) custom-call(s32[3]{0:T(128)S(1)} %pad_add_fusion.places, s32[1]{0:T(128)} %bitcast.3.last, bf16[128,4096]{1,0:T(8,128)(2,1)S(1)} %multiply_convert_fusion.rows.q, s32[128,1]{1,0:T(8,128)S(1)} %copy.15.starts, ...), custom_call_target="tpu_custom_call" | custom-call | flops 805306368 | bytes 7077888 | tf_op jit(solution)/shard_map/attention/pallas_call | solution.py:285
  117.8 14.2 %collective-permute-done.24.rows.q = bf16[128,4096]{1,0:T(8,128)(2,1)S(1)} collective-permute-done((bf16[128,4096]{1,0:T(8,128)(2,1)S(1)}, bf16[128,4096]{1,0:T(8,128)(2,1)S(1)}, u32[]{:S(2)}, u32[]{:S(2)}) %collective-permute-start.24) | collective-permute-done | bytes 1048608 | tf_op jit(solution)/shard_map/ppermute | solution.py:348
  132.1 4.2 %projection.5.refs_0_ = bf16[128,1024]{1,0:T(8,128)(2,1)S(1)} custom-call(s32[16]{0:T(128)S(1)} %stack.94.order, bf16[128,4096]{1,0:T(8,128)(2,1)S(1)} %collective-permute-done.24.rows.q, bf16[256,512]{1,0:T(8,128)(2,1)S(1)} %bitcast.48, bf16[256,512]{1,0:T(8,128)(2,1)S(1)} %copy-done.11, bf16[256,512]{1,0:T(8,128)(2,1)S(1)} %collective-permute-done.1.refs_2_, ...), custom_call_target="tpu_custom_call" | custom-call | flops 1073741824 | bytes 8388608 | tf_op jit(solution)/shard_map/projection/pallas_call | solution.py:155
  136.4 9.9 %collective-permute-done.25.refs_1_ = bf16[128,1024]{1,0:T(8,128)(2,1)} collective-permute-done((bf16[128,1024]{1,0:T(8,128)(2,1)S(1)}, bf16[128,1024]{1,0:T(8,128)(2,1)}, u32[]{:S(2)}, u32[]{:S(2)}) %collective-permute-start.25) | collective-permute-done | bytes 262176 | tf_op jit(solution)/shard_map/ppermute | solution.py:33
  146.3 1.1 collective-permute-start.31
  147.4 2.2 %collective-permute-start.32 = (bf16[128,1024]{1,0:T(8,128)(2,1)}, bf16[128,1024]{1,0:T(8,128)(2,1)S(1)}, u32[]{:S(2)}, u32[]{:S(2)}) collective-permute-start(bf16[128,1024]{1,0:T(8,128)(2,1)} %collective-permute-done.25.refs_1_), channel_id=1, source_target_pairs={{0,3},{1,0},{2,1},{3,2},{4,7},{5,4},{6,5},{7,6},{8,11},{9,8},{10,9... | collective-permute-start | bytes 786440 | tf_op jit(solution)/shard_map/ppermute | solution.py:33
  149.6 1.4 collective-permute-start.33
  150.9 5.5 %collective-permute-done.26.refs_2_ = bf16[128,1024]{1,0:T(8,128)(2,1)S(1)} collective-permute-done((bf16[128,1024]{1,0:T(8,128)(2,1)}, bf16[128,1024]{1,0:T(8,128)(2,1)S(1)}, u32[]{:S(2)}, u32[]{:S(2)}) %collective-permute-start.26) | collective-permute-done | bytes 262176 | tf_op jit(solution)/shard_map/ppermute | solution.py:33
  156.4 1.0 broadcast_select_fusion
  158.1 1.1 collective-permute-start.27
  159.9 2.1 %collective-permute-start.28 = (bf16[128,1024]{1,0:T(8,128)(2,1)}, bf16[128,1024]{1,0:T(8,128)(2,1)}, u32[]{:S(2)}, u32[]{:S(2)}) collective-permute-start(bf16[128,1024]{1,0:T(8,128)(2,1)} %get-tuple-element.32), channel_id=1, source_target_pairs={{0,3},{1,0},{2,1},{3,2},{4,7},{5,4},{6,5},{7,6},{8,11},{9,8},{10,9... | collective-permute-start | bytes 786440 | tf_op jit(solution)/shard_map/ppermute | solution.py:33
  162.7 1.4 collective-permute-start.29
  168.1 7.8 %attention.6 = (f32[4096,128]{1,0:T(8,128)S(1)}, f32[4096,128]{1,0:T(8,128)S(1)}, f32[4096,128]{1,0:T(8,128)S(1)}) custom-call(s32[6]{0:T(128)S(1)} %stack.98.places, s32[1]{0:T(128)} %constant.168.clone.1.last, bf16[128,4096]{1,0:T(8,128)(2,1)S(1)} %collective-permute-done.24.rows.q, s32[128,1]{1,0:T(8,128)S(1)} %copy.17.starts, ...), custom_call_target="tpu_custom_call" | custom-call | flops 1610612736 | bytes 7864320 | tf_op jit(solution)/shard_map/attention/pallas_call | solution.py:285
  175.9 6.7 %attention.7 = bf16[2,128,4096]{2,1,0:T(8,128)(2,1)} custom-call(s32[3]{0:T(128)S(1)} %pad_add_fusion.places, s32[1]{0:T(128)} %constant.168.clone.1.last, bf16[128,4096]{1,0:T(8,128)(2,1)S(1)} %collective-permute-done.24.rows.q, s32[128,1]{1,0:T(8,128)S(1)} %copy.17.starts, ...), custom_call_target="tpu_custom_call", output_to_operand_aliasing={{}: (11, {})} | custom-call | flops 805306368 | bytes 7077888 | tf_op jit(solution)/shard_map/attention/pallas_call | solution.py:285
  (125 shorter events, 14.5 us)
Async XLA Ops:
  6.5 68.8 %copy-start = (bf16[2,128,4096]{2,1,0:T(8,128)(2,1)S(1)}, bf16[2,128,4096]{2,1,0:T(8,128)(2,1)}, u32[]{:S(2)}) copy-start(bf16[2,128,4096]{2,1,0:T(8,128)(2,1)} %param.8) | copy-start | bytes 6291460
  6.5 39.1 %copy-start.34 = (f32[1,4096]{1,0:T(1,128)S(1)}, f32[1,4096]{1,0:T(1,128)}, u32[]{:S(2)}) copy-start(f32[1,4096]{1,0:T(1,128)} %param.9) | copy-start | bytes 49156
  6.5 63.4 %all-gather.3.cloned.1.call-start = ((), (), s32[]{:S(2)}) async-start(), calls=%async_computation | async-start | bytes 4456448 | tf_op jit(solution)/shard_map/all_gather | solution.py:324
  7.3 9.6 %collective-permute-start.1 = (bf16[256,512]{1,0:T(8,128)(2,1)}, bf16[256,512]{1,0:T(8,128)(2,1)S(1)}, u32[]{:S(2)}, u32[]{:S(2)}) collective-permute-start(bf16[256,512]{1,0:T(8,128)(2,1)} %bitcast.43), channel_id=1, source_target_pairs={{0,1},{1,2},{2,3},{3,0},{4,5},{5,6},{6,7},{7,4},{8,9},{9,10},{10,1... | collective-permute-start | bytes 786440 | tf_op jit(solution)/shard_map/ppermute | solution.py:33
  8.9 8.0 %collective-permute-start.3 = (bf16[256,512]{1,0:T(8,128)(2,1)}, bf16[256,512]{1,0:T(8,128)(2,1)S(1)}, u32[]{:S(2)}, u32[]{:S(2)}) collective-permute-start(bf16[256,512]{1,0:T(8,128)(2,1)} %bitcast.44), channel_id=1, source_target_pairs={{0,3},{1,0},{2,1},{3,2},{4,7},{5,4},{6,5},{7,6},{8,11},{9,8},{10,9... | collective-permute-start | bytes 786440 | tf_op jit(solution)/shard_map/ppermute | solution.py:33
  10.6 10.2 %collective-permute-start = (bf16[256,512]{1,0:T(8,128)(2,1)}, bf16[256,512]{1,0:T(8,128)(2,1)S(1)}, u32[]{:S(2)}, u32[]{:S(2)}) collective-permute-start(bf16[256,512]{1,0:T(8,128)(2,1)} %bitcast.45), channel_id=1, source_target_pairs={{0,4},{1,5},{2,6},{3,7},{4,8},{5,9},{6,10},{7,11},{8,12},{9,13},{1... | collective-permute-start | bytes 786440 | tf_op jit(solution)/shard_map/ppermute | solution.py:33
  12.5 8.3 %collective-permute-start.2 = (bf16[256,512]{1,0:T(8,128)(2,1)}, bf16[256,512]{1,0:T(8,128)(2,1)S(1)}, u32[]{:S(2)}, u32[]{:S(2)}) collective-permute-start(bf16[256,512]{1,0:T(8,128)(2,1)} %bitcast.46), channel_id=1, source_target_pairs={{0,12},{1,13},{2,14},{3,15},{4,0},{5,1},{6,2},{7,3},{8,4},{9,5},{1... | collective-permute-start | bytes 786440 | tf_op jit(solution)/shard_map/ppermute | solution.py:33
  16.9 28.7 %copy-start.6 = (bf16[256,512]{1,0:T(8,128)(2,1)}, bf16[256,512]{1,0:T(8,128)(2,1)S(1)}, u32[]{:S(2)}) copy-start(bf16[256,512]{1,0:T(8,128)(2,1)S(1)} %collective-permute-done.3.refs_4_) | copy-start | bytes 786436
  17.7 12.9 %collective-permute-start.4 = (bf16[256,512]{1,0:T(8,128)(2,1)}, bf16[256,512]{1,0:T(8,128)(2,1)}, u32[]{:S(2)}, u32[]{:S(2)}) collective-permute-start(bf16[256,512]{1,0:T(8,128)(2,1)} %broadcast_select_fusion.5), channel_id=1, source_target_pairs={{1,2},{2,1},{3,0},{0,3},{5,6},{6,5},{7,4},{4,7},{9,10},{10,9},{11,... | collective-permute-start | bytes 786440 | tf_op jit(solution)/shard_map/ppermute | solution.py:46
  20.7 24.9 %copy-start.1 = (f32[1,128,4096]{2,1,0:T(8,128)S(1)}, f32[1,128,4096]{2,1,0:T(8,128)}, u32[]{:S(2)}) copy-start(f32[1,128,4096]{2,1,0:T(8,128)} %param.7) | copy-start | bytes 6291460
  20.7 24.8 %copy-start.9 = (bf16[256,512]{1,0:T(8,128)(2,1)}, bf16[256,512]{1,0:T(8,128)(2,1)S(1)}, u32[]{:S(2)}) copy-start(bf16[256,512]{1,0:T(8,128)(2,1)S(1)} %collective-permute-done.refs_1_) | copy-start | bytes 786436
  20.7 24.9 %copy-start.12 = (bf16[256,512]{1,0:T(8,128)(2,1)}, bf16[256,512]{1,0:T(8,128)(2,1)S(1)}, u32[]{:S(2)}) copy-start(bf16[256,512]{1,0:T(8,128)(2,1)S(1)} %collective-permute-done.2.refs_3_) | copy-start | bytes 786436
  20.8 14.1 %collective-permute-start.5 = (bf16[256,512]{1,0:T(8,128)(2,1)S(1)}, bf16[256,512]{1,0:T(8,128)(2,1)}, u32[]{:S(2)}, u32[]{:S(2)}) collective-permute-start(bf16[256,512]{1,0:T(8,128)(2,1)S(1)} %broadcast_select_fusion.4), channel_id=1, source_target_pairs={{0,4},{4,0},{8,12},{12,8},{1,5},{5,1},{9,13},{13,9},{2,6},{6,2},{1... | collective-permute-start | bytes 786440 | tf_op jit(solution)/shard_map/ppermute | solution.py:46
  22.7 14.7 %collective-permute-start.6 = (bf16[256,512]{1,0:T(8,128)(2,1)S(1)}, bf16[256,512]{1,0:T(8,128)(2,1)S(1)}, u32[]{:S(2)}, u32[]{:S(2)}) collective-permute-start(bf16[256,512]{1,0:T(8,128)(2,1)S(1)} %collective-permute-done.refs_1_), channel_id=1, source_target_pairs={{0,1},{1,2},{2,3},{3,0},{4,5},{5,6},{6,7},{7,4},{8,9},{9,10},{10,1... | collective-permute-start | bytes 786440 | tf_op jit(solution)/shard_map/ppermute | solution.py:33
  22.7 15.8 %collective-permute-start.7 = (bf16[256,512]{1,0:T(8,128)(2,1)S(1)}, bf16[256,512]{1,0:T(8,128)(2,1)S(1)}, u32[]{:S(2)}, u32[]{:S(2)}) collective-permute-start(bf16[256,512]{1,0:T(8,128)(2,1)S(1)} %collective-permute-done.2.refs_3_), channel_id=1, source_target_pairs={{0,3},{1,0},{2,1},{3,2},{4,7},{5,4},{6,5},{7,6},{8,11},{9,8},{10,9... | collective-permute-start | bytes 786440 | tf_op jit(solution)/shard_map/ppermute | solution.py:33
  26.0 16.2 %collective-permute-start.8 = (bf16[256,512]{1,0:T(8,128)(2,1)S(1)}, bf16[256,512]{1,0:T(8,128)(2,1)S(1)}, u32[]{:S(2)}, u32[]{:S(2)}) collective-permute-start(bf16[256,512]{1,0:T(8,128)(2,1)S(1)} %collective-permute-done.3.refs_4_), channel_id=1, source_target_pairs={{0,4},{1,5},{2,6},{3,7},{4,8},{5,9},{6,10},{7,11},{8,12},{9,13},{1... | collective-permute-start | bytes 786440 | tf_op jit(solution)/shard_map/ppermute | solution.py:33
  30.6 15.0 %collective-permute-start.10 = (bf16[256,512]{1,0:T(8,128)(2,1)}, bf16[256,512]{1,0:T(8,128)(2,1)}, u32[]{:S(2)}, u32[]{:S(2)}) collective-permute-start(bf16[256,512]{1,0:T(8,128)(2,1)} %collective-permute-done.4.refs_5_), channel_id=1, source_target_pairs={{0,4},{1,5},{2,6},{3,7},{4,8},{5,9},{6,10},{7,11},{8,12},{9,13},{1... | collective-permute-start | bytes 786440 | tf_op jit(solution)/shard_map/ppermute | solution.py:33
  34.8 11.4 %collective-permute-start.9 = (bf16[256,512]{1,0:T(8,128)(2,1)S(1)}, bf16[256,512]{1,0:T(8,128)(2,1)}, u32[]{:S(2)}, u32[]{:S(2)}) collective-permute-start(bf16[256,512]{1,0:T(8,128)(2,1)S(1)} %collective-permute-done.1.refs_2_), channel_id=1, source_target_pairs={{0,12},{1,13},{2,14},{3,15},{4,0},{5,1},{6,2},{7,3},{8,4},{9,5},{1... | collective-permute-start | bytes 786440 | tf_op jit(solution)/shard_map/ppermute | solution.py:33
  38.2 8.1 %collective-permute-start.12 = (bf16[256,512]{1,0:T(8,128)(2,1)}, bf16[256,512]{1,0:T(8,128)(2,1)}, u32[]{:S(2)}, u32[]{:S(2)}) collective-permute-start(bf16[256,512]{1,0:T(8,128)(2,1)} %collective-permute-done.5.refs_6_), channel_id=1, source_target_pairs={{0,1},{1,2},{2,3},{3,0},{4,5},{5,6},{6,7},{7,4},{8,9},{9,10},{10,1... | collective-permute-start | bytes 786440 | tf_op jit(solution)/shard_map/ppermute | solution.py:33
  39.3 9.8 %collective-permute-start.13 = (bf16[256,512]{1,0:T(8,128)(2,1)}, bf16[256,512]{1,0:T(8,128)(2,1)}, u32[]{:S(2)}, u32[]{:S(2)}) collective-permute-start(bf16[256,512]{1,0:T(8,128)(2,1)} %collective-permute-done.5.refs_6_), channel_id=1, source_target_pairs={{0,3},{1,0},{2,1},{3,2},{4,7},{5,4},{6,5},{7,6},{8,11},{9,8},{10,9... | collective-permute-start | bytes 786440 | tf_op jit(solution)/shard_map/ppermute | solution.py:33
  42.8 12.8 %collective-permute-start.11 = (bf16[256,512]{1,0:T(8,128)(2,1)}, bf16[256,512]{1,0:T(8,128)(2,1)}, u32[]{:S(2)}, u32[]{:S(2)}) collective-permute-start(bf16[256,512]{1,0:T(8,128)(2,1)} %collective-permute-done.4.refs_5_), channel_id=1, source_target_pairs={{0,12},{1,13},{2,14},{3,15},{4,0},{5,1},{6,2},{7,3},{8,4},{9,5},{1... | collective-permute-start | bytes 786440 | tf_op jit(solution)/shard_map/ppermute | solution.py:33
  45.6 14.3 %collective-permute-start.14 = (bf16[256,512]{1,0:T(8,128)(2,1)}, bf16[256,512]{1,0:T(8,128)(2,1)}, u32[]{:S(2)}, u32[]{:S(2)}) collective-permute-start(bf16[256,512]{1,0:T(8,128)(2,1)} %collective-permute-done.10.refs_11_), channel_id=1, source_target_pairs={{0,4},{1,5},{2,6},{3,7},{4,8},{5,9},{6,10},{7,11},{8,12},{9,13},{1... | collective-permute-start | bytes 786440 | tf_op jit(solution)/shard_map/ppermute | solution.py:33
  75.2 25.6 %copy-start.35 = (f32[1,4096]{1,0:T(1,128)S(1)}, f32[1,4096]{1,0:T(1,128)}, u32[]{:S(2)}) copy-start(f32[1,4096]{1,0:T(1,128)} %param.9) | copy-start | bytes 49156
  75.2 9.9 %collective-permute-start.15 = (bf16[128,1024]{1,0:T(8,128)(2,1)}, bf16[128,1024]{1,0:T(8,128)(2,1)}, u32[]{:S(2)}, u32[]{:S(2)}) collective-permute-start(bf16[128,1024]{1,0:T(8,128)(2,1)} %projection.4.refs_0_), channel_id=1, source_target_pairs={{0,4},{1,5},{2,6},{3,7},{4,8},{5,9},{6,10},{7,11},{8,12},{9,13},{1... | collective-permute-start | bytes 786440 | tf_op jit(solution)/shard_map/ppermute | solution.py:33
  85.1 8.9 %collective-permute-start.16 = (bf16[128,1024]{1,0:T(8,128)(2,1)}, bf16[128,1024]{1,0:T(8,128)(2,1)}, u32[]{:S(2)}, u32[]{:S(2)}) collective-permute-start(bf16[128,1024]{1,0:T(8,128)(2,1)} %collective-permute-done.15.refs_1_), channel_id=1, source_target_pairs={{0,4},{1,5},{2,6},{3,7},{4,8},{5,9},{6,10},{7,11},{8,12},{9,13},{1... | collective-permute-start | bytes 786440 | tf_op jit(solution)/shard_map/ppermute | solution.py:33
  85.2 15.5 %collective-permute-start.20 = (bf16[128,1024]{1,0:T(8,128)(2,1)}, bf16[128,1024]{1,0:T(8,128)(2,1)}, u32[]{:S(2)}, u32[]{:S(2)}) collective-permute-start(bf16[128,1024]{1,0:T(8,128)(2,1)} %collective-permute-done.15.refs_1_), channel_id=1, source_target_pairs={{0,1},{1,2},{2,3},{3,0},{4,5},{5,6},{6,7},{7,4},{8,9},{9,10},{10,1... | collective-permute-start | bytes 786440 | tf_op jit(solution)/shard_map/ppermute | solution.py:33
  85.6 15.2 %collective-permute-start.21 = (bf16[128,1024]{1,0:T(8,128)(2,1)}, bf16[128,1024]{1,0:T(8,128)(2,1)S(1)}, u32[]{:S(2)}, u32[]{:S(2)}) collective-permute-start(bf16[128,1024]{1,0:T(8,128)(2,1)} %collective-permute-done.15.refs_1_), channel_id=1, source_target_pairs={{0,3},{1,0},{2,1},{3,2},{4,7},{5,4},{6,5},{7,6},{8,11},{9,8},{10,9... | collective-permute-start | bytes 786440 | tf_op jit(solution)/shard_map/ppermute | solution.py:33
  88.7 12.1 %collective-permute-start.22 = (bf16[128,1024]{1,0:T(8,128)(2,1)}, bf16[128,1024]{1,0:T(8,128)(2,1)S(1)}, u32[]{:S(2)}, u32[]{:S(2)}) collective-permute-start(bf16[128,1024]{1,0:T(8,128)(2,1)} %collective-permute-done.15.refs_1_), channel_id=1, source_target_pairs={{0,2},{1,3},{2,0},{3,1},{4,6},{5,7},{6,4},{7,5},{8,10},{9,11},{10,... | collective-permute-start | bytes 786440 | tf_op jit(solution)/shard_map/ppermute | solution.py:33
  95.1 15.8 %collective-permute-start.17 = (bf16[128,1024]{1,0:T(8,128)(2,1)S(1)}, bf16[128,1024]{1,0:T(8,128)(2,1)S(1)}, u32[]{:S(2)}, u32[]{:S(2)}) collective-permute-start(bf16[128,1024]{1,0:T(8,128)(2,1)S(1)} %get-tuple-element.36), channel_id=1, source_target_pairs={{0,1},{1,2},{2,3},{3,0},{4,5},{5,6},{6,7},{7,4},{8,9},{9,10},{10,1... | collective-permute-start | bytes 786440 | tf_op jit(solution)/shard_map/ppermute | solution.py:33
  95.2 15.7 %collective-permute-start.18 = (bf16[128,1024]{1,0:T(8,128)(2,1)S(1)}, bf16[128,1024]{1,0:T(8,128)(2,1)S(1)}, u32[]{:S(2)}, u32[]{:S(2)}) collective-permute-start(bf16[128,1024]{1,0:T(8,128)(2,1)S(1)} %get-tuple-element.35), channel_id=1, source_target_pairs={{0,3},{1,0},{2,1},{3,2},{4,7},{5,4},{6,5},{7,6},{8,11},{9,8},{10,9... | collective-permute-start | bytes 786440 | tf_op jit(solution)/shard_map/ppermute | solution.py:33
  100.7 10.2 %collective-permute-start.19 = (bf16[128,1024]{1,0:T(8,128)(2,1)S(1)}, bf16[128,1024]{1,0:T(8,128)(2,1)S(1)}, u32[]{:S(2)}, u32[]{:S(2)}) collective-permute-start(bf16[128,1024]{1,0:T(8,128)(2,1)S(1)} %get-tuple-element.34), channel_id=1, source_target_pairs={{0,2},{1,3},{2,0},{3,1},{4,6},{5,7},{6,4},{7,5},{8,10},{9,11},{10,... | collective-permute-start | bytes 786440 | tf_op jit(solution)/shard_map/ppermute | solution.py:33
  100.8 8.2 %collective-permute-start.23 = (f32[1,4096]{1,0:T(1,128)S(1)}, f32[1,4096]{1,0:T(1,128)S(1)}, u32[]{:S(2)}, u32[]{:S(2)}) collective-permute-start(f32[1,4096]{1,0:T(1,128)S(1)} %copy-done.35), channel_id=1, source_target_pairs={{16,0},{32,16},{48,32},{64,48},{80,64},{96,80},{112,96},{0,112},{1... | collective-permute-start | bytes 49160 | tf_op jit(solution)/shard_map/ppermute | solution.py:327
  111.0 21.1 %copy-start.4 = (bf16[1,4096,512]{2,1,0:T(8,128)(2,1)S(1)}, bf16[1,4096,512]{2,1,0:T(8,128)(2,1)}, u32[]{:S(2)}) copy-start(bf16[1,4096,512]{2,1,0:T(8,128)(2,1)} %all-gather.3.cloned.1.call-done) | copy-start | bytes 12582916
  111.0 21.1 %copy-start.8 = (bf16[256,512]{1,0:T(8,128)(2,1)S(1)}, bf16[256,512]{1,0:T(8,128)(2,1)}, u32[]{:S(2)}) copy-start(bf16[256,512]{1,0:T(8,128)(2,1)} %copy-done.6) | copy-start | bytes 786436
  111.0 21.1 %copy-start.11 = (bf16[256,512]{1,0:T(8,128)(2,1)S(1)}, bf16[256,512]{1,0:T(8,128)(2,1)}, u32[]{:S(2)}) copy-start(bf16[256,512]{1,0:T(8,128)(2,1)} %copy-done.9) | copy-start | bytes 786436
  111.0 21.1 %copy-start.14 = (bf16[256,512]{1,0:T(8,128)(2,1)S(1)}, bf16[256,512]{1,0:T(8,128)(2,1)}, u32[]{:S(2)}) copy-start(bf16[256,512]{1,0:T(8,128)(2,1)} %copy-done.12) | copy-start | bytes 786436
  111.0 21.1 %copy-start.16 = (bf16[1,256,512]{2,1,0:T(8,128)(2,1)S(1)}, bf16[1,256,512]{2,1,0:T(8,128)(2,1)}, u32[]{:S(2)}) copy-start(bf16[1,256,512]{2,1,0:T(8,128)(2,1)} %param.10) | copy-start | bytes 786436
  111.0 21.1 %copy-start.19 = (bf16[256,512]{1,0:T(8,128)(2,1)S(1)}, bf16[256,512]{1,0:T(8,128)(2,1)}, u32[]{:S(2)}) copy-start(bf16[256,512]{1,0:T(8,128)(2,1)} %copy-done.17) | copy-start | bytes 786436
  117.8 14.2 %collective-permute-start.24 = (bf16[128,4096]{1,0:T(8,128)(2,1)S(1)}, bf16[128,4096]{1,0:T(8,128)(2,1)S(1)}, u32[]{:S(2)}, u32[]{:S(2)}) collective-permute-start(bf16[128,4096]{1,0:T(8,128)(2,1)S(1)} %get-tuple-element.19), channel_id=1, source_target_pairs={{0,16},{16,32},{32,48},{48,64},{64,80},{80,96},{96,112},{112,0},{1... | collective-permute-start | bytes 3145736 | tf_op jit(solution)/shard_map/ppermute | solution.py:348
  132.0 43.9 %collective-permute-start.30 = (f32[128,4096]{1,0:T(8,128)}, f32[128,4096]{1,0:T(8,128)}, u32[]{:S(2)}, u32[]{:S(2)}) collective-permute-start(f32[128,4096]{1,0:T(8,128)} %get-tuple-element.22), channel_id=1, source_target_pairs={{0,16},{16,32},{32,48},{48,64},{64,80},{80,96},{96,112},{112,0},{1... | collective-permute-start | bytes 6291464 | tf_op jit(solution)/shard_map/ppermute | solution.py:350
  136.4 9.9 %collective-permute-start.25 = (bf16[128,1024]{1,0:T(8,128)(2,1)S(1)}, bf16[128,1024]{1,0:T(8,128)(2,1)}, u32[]{:S(2)}, u32[]{:S(2)}) collective-permute-start(bf16[128,1024]{1,0:T(8,128)(2,1)S(1)} %projection.5.refs_0_), channel_id=1, source_target_pairs={{0,4},{1,5},{2,6},{3,7},{4,8},{5,9},{6,10},{7,11},{8,12},{9,13},{1... | collective-permute-start | bytes 786440 | tf_op jit(solution)/shard_map/ppermute | solution.py:33
  146.3 10.1 %collective-permute-start.26 = (bf16[128,1024]{1,0:T(8,128)(2,1)}, bf16[128,1024]{1,0:T(8,128)(2,1)S(1)}, u32[]{:S(2)}, u32[]{:S(2)}) collective-permute-start(bf16[128,1024]{1,0:T(8,128)(2,1)} %collective-permute-done.25.refs_1_), channel_id=1, source_target_pairs={{0,4},{1,5},{2,6},{3,7},{4,8},{5,9},{6,10},{7,11},{8,12},{9,13},{1... | collective-permute-start | bytes 786440 | tf_op jit(solution)/shard_map/ppermute | solution.py:33
  146.3 12.9 %collective-permute-start.31 = (bf16[128,1024]{1,0:T(8,128)(2,1)}, bf16[128,1024]{1,0:T(8,128)(2,1)S(1)}, u32[]{:S(2)}, u32[]{:S(2)}) collective-permute-start(bf16[128,1024]{1,0:T(8,128)(2,1)} %collective-permute-done.25.refs_1_), channel_id=1, source_target_pairs={{0,1},{1,2},{2,3},{3,0},{4,5},{5,6},{6,7},{7,4},{8,9},{9,10},{10,1... | collective-permute-start | bytes 786440 | tf_op jit(solution)/shard_map/ppermute | solution.py:33
  147.4 14.7 %collective-permute-start.32 = (bf16[128,1024]{1,0:T(8,128)(2,1)}, bf16[128,1024]{1,0:T(8,128)(2,1)S(1)}, u32[]{:S(2)}, u32[]{:S(2)}) collective-permute-start(bf16[128,1024]{1,0:T(8,128)(2,1)} %collective-permute-done.25.refs_1_), channel_id=1, source_target_pairs={{0,3},{1,0},{2,1},{3,2},{4,7},{5,4},{6,5},{7,6},{8,11},{9,8},{10,9... | collective-permute-start | bytes 786440 | tf_op jit(solution)/shard_map/ppermute | solution.py:33
  149.6 14.7 %collective-permute-start.33 = (bf16[128,1024]{1,0:T(8,128)(2,1)}, bf16[128,1024]{1,0:T(8,128)(2,1)}, u32[]{:S(2)}, u32[]{:S(2)}) collective-permute-start(bf16[128,1024]{1,0:T(8,128)(2,1)} %collective-permute-done.25.refs_1_), channel_id=1, source_target_pairs={{0,2},{1,3},{2,0},{3,1},{4,6},{5,7},{6,4},{7,5},{8,10},{9,11},{10,... | collective-permute-start | bytes 786440 | tf_op jit(solution)/shard_map/ppermute | solution.py:33
  158.1 17.8 %collective-permute-start.27 = (bf16[128,1024]{1,0:T(8,128)(2,1)}, bf16[128,1024]{1,0:T(8,128)(2,1)S(1)}, u32[]{:S(2)}, u32[]{:S(2)}) collective-permute-start(bf16[128,1024]{1,0:T(8,128)(2,1)} %get-tuple-element.33), channel_id=1, source_target_pairs={{0,1},{1,2},{2,3},{3,0},{4,5},{5,6},{6,7},{7,4},{8,9},{9,10},{10,1... | collective-permute-start | bytes 786440 | tf_op jit(solution)/shard_map/ppermute | solution.py:33
  159.9 16.0 %collective-permute-start.28 = (bf16[128,1024]{1,0:T(8,128)(2,1)}, bf16[128,1024]{1,0:T(8,128)(2,1)}, u32[]{:S(2)}, u32[]{:S(2)}) collective-permute-start(bf16[128,1024]{1,0:T(8,128)(2,1)} %get-tuple-element.32), channel_id=1, source_target_pairs={{0,3},{1,0},{2,1},{3,2},{4,7},{5,4},{6,5},{7,6},{8,11},{9,8},{10,9... | collective-permute-start | bytes 786440 | tf_op jit(solution)/shard_map/ppermute | solution.py:33
  162.7 13.2 %collective-permute-start.29 = (bf16[128,1024]{1,0:T(8,128)(2,1)}, bf16[128,1024]{1,0:T(8,128)(2,1)}, u32[]{:S(2)}, u32[]{:S(2)}) collective-permute-start(bf16[128,1024]{1,0:T(8,128)(2,1)} %get-tuple-element.31), channel_id=1, source_target_pairs={{0,2},{1,3},{2,0},{3,1},{4,6},{5,7},{6,4},{7,5},{8,10},{9,11},{10,... | collective-permute-start | bytes 786440 | tf_op jit(solution)/shard_map/ppermute | solution.py:33
  (25 other events, 99.6 us)
Sparse Core Ops, SparseCore 0:
  9.5 60.4 all-gather.2

commit v4 on v3

--- a/solution.py
+++ b/solution.py
@@ -18,6 +18,10 @@
 MASK_FLOOR = -1e30
 SIDE = 4
 VMEM = 28 << 20
+WHOLE = 56 << 20
+DOCUMENTS = 8
+PLACES = 9
+INFO = PLACES + W * (1 + DOCUMENTS) + 1
 TOGETHER = 4
 DEPTH = 256
 SCALE = HEAD_SIZE ** (-0.5)
@@ -33,24 +37,10 @@
     return lax.ppermute(block, "ctx", pairs)
 
 
-def swapped(block, first, along_z=False):
-    pairs = []
-    for other in range(SIDE):
-        for at in (first, first + 2):
-            a, b = at % SIDE, (at + 1) % SIDE
-            if along_z:
-                a, b = a * SIDE + other, b * SIDE + other
-            else:
-                a, b = other * SIDE + a, other * SIDE + b
-            pairs += [(a, b), (b, a)]
-    return lax.ppermute(block, "ctx", pairs)
-
-
 def tree_gather(own, z, y):
     zp, yp, zm, ym = moved(own, 1, 0), moved(own, 0, 1), moved(own, -1, 0), moved(own, 0, -1)
     got = {(0, 0): own, (1, 0): zp, (0, 1): yp, (3, 0): zm, (0, 3): ym}
-    got[0, 2] = swapped(jnp.where(y % 2 == 1, yp, ym), 1)
-    got[2, 0] = swapped(jnp.where(z % 2 == 1, zm, zp), 0, True)
+    got[0, 2], got[2, 0] = moved(own, 0, 2), moved(own, 2, 0)
     got[1, 1] = moved(zp, 0, 1)
     got[3, 3] = moved(zm, 0, -1)
     got[1, 3] = moved(ym, 1, 0)
@@ -138,7 +128,7 @@
         by_head(out, total.astype(out.dtype), 1, True)
 
 
-def projection(rows, order, key_blocks=(), keys=None, values=None):
+def projection(rows, order, key_blocks=(), keys=None, values=None, vmem=VMEM):
     tokens, width = rows.shape
     n_keys = len(key_blocks)
     in_vmem, in_hbm = pl.BlockSpec(memory_space=pltpu.VMEM), pl.BlockSpec(memory_space=pl.ANY)
@@ -158,7 +148,7 @@
         out_specs=in_vmem,
         out_shape=jax.ShapeDtypeStruct((tokens, columns), jnp.bfloat16),
         scratch_shapes=[*scratch, pltpu.SemaphoreType.DMA((n_copies,))],
-        compiler_params=pltpu.CompilerParams(vmem_limit_bytes=VMEM),
+        compiler_params=pltpu.CompilerParams(vmem_limit_bytes=vmem),
         cost_estimate=pl.CostEstimate(
             flops=2 * tokens * width * KV_WIDTH * len(scratch),
             transcendentals=0,
@@ -168,7 +158,7 @@
     )(*operands)
 
 
-def attention_body(n_blocks, stage, places, last, q, starts, *refs):
+def attention_body(n_blocks, stage, tick, info, q, *refs):
     blocks, refs = refs[:n_blocks], refs[n_blocks:]
     if stage == "first":
         out_mix, out_sum, out_high = refs
@@ -180,10 +170,14 @@
     tokens = q.shape[0]
     column = lax.broadcasted_iota(jnp.int32, (tokens, tokens), 1)
     row = lax.broadcasted_iota(jnp.int32, (tokens, tokens), 0)
-    low = jnp.broadcast_to(starts[...], (tokens, tokens))
+    ends = PLACES + tick * (1 + DOCUMENTS)
+    low = jnp.full((tokens, tokens), info[ends], jnp.int32)
+    for j in range(1, 1 + DOCUMENTS):
+        low = jnp.where(row >= info[ends + j], info[ends + j], low)
     bias = []
     for b in range(n_blocks):
-        allowed = column - places[b] * tokens >= low
+        place = info[b if stage == "first" else PLACES - n_blocks + b]
+        allowed = column - place * tokens >= low
         if stage == "first" and b == 0:
             allowed = allowed & (column <= row)
         bias.append(jnp.where(allowed, 0.0, MASK_FLOOR))
@@ -226,7 +220,7 @@
             new = x[:, where] + out[j * tokens : (j + 1) * tokens]
             produced[0, :, where] = new.astype(jnp.bfloat16)
             if stage != "last":
-                new = jnp.where(last[0] == 1, first[:, where].astype(jnp.float32), new)
+                new = jnp.where(info[INFO - 1] == 1, first[:, where].astype(jnp.float32), new)
                 stream[:, where] = new
                 at = pl.multiple_of(g * GROUP_WIDTH, GROUP_WIDTH) + (h + j) * HEAD_SIZE
                 rows[:, pl.ds(at, HEAD_SIZE)] = new
@@ -246,36 +240,34 @@
             normed[:, at] = (rows[:, at] * factor * gain[:, at]).astype(jnp.bfloat16)
 
 
-def attention(blocks, places, q, starts, part=None, x=None, onward=None, produced=None):
+def attention(blocks, info, tick, q, part=None, x=None, onward=None, produced=None):
     tokens, width = q.shape
     n_blocks = len(blocks)
     span = n_blocks * tokens
     stage = "first" if part is None else "last" if onward is None else "onward"
-    flag = jnp.zeros((1,), jnp.int32) if onward is None else onward[0]
     whole = lambda g, *_: (0, 0)
     by_group = pl.BlockSpec((tokens, GROUP_WIDTH), lambda g, *_: (0, g))
     by_rows = pl.BlockSpec((HEAD_GROUPS * tokens, HEAD_SIZE), lambda g, *_: (g, 0))
-    in_specs = [by_group, pl.BlockSpec((tokens, 1), whole)]
+    in_specs = [by_group]
     in_specs += [pl.BlockSpec((tokens, 2 * HEAD_SIZE), lambda g, *_: (0, g))] * n_blocks
-    operands = [q, starts, *blocks]
+    operands = [q, *blocks]
     scratch = []
     aliases = {}
     if stage == "first":
         out_specs = [by_rows] * 3
         out_shape = [jax.ShapeDtypeStruct((QUERY_HEADS * tokens, HEAD_SIZE), jnp.float32)] * 3
     else:
-        tick = 0 if stage == "onward" else W - 1
         in_specs += [by_group] + [by_rows] * 3
         operands += [x, *part]
         out_specs = [pl.BlockSpec((1, tokens, GROUP_WIDTH), lambda g, *_: (tick, 0, g))]
         out_shape = [jax.ShapeDtypeStruct((W, tokens, width), jnp.bfloat16)]
     if stage == "last":
-        aliases = {2 + len(operands): 0}
+        aliases = {1 + len(operands): 0}
         in_specs += [pl.BlockSpec(memory_space=pl.ANY)]
         operands += [produced]
     if stage == "onward":
         in_specs += [by_group, pl.BlockSpec((1, width), whole)]
-        operands += [onward[1], onward[2]]
+        operands += [*onward]
         out_specs += [by_group, pl.BlockSpec((tokens, width), whole)]
         out_shape += [
             jax.ShapeDtypeStruct((tokens, width), jnp.float32),
@@ -283,9 +275,9 @@
         ]
         scratch += [pltpu.VMEM((tokens, width), jnp.float32)]
     return pl.pallas_call(
-        functools.partial(attention_body, n_blocks, stage),
+        functools.partial(attention_body, n_blocks, stage, tick),
         grid_spec=pltpu.PrefetchScalarGridSpec(
-            num_scalar_prefetch=2,
+            num_scalar_prefetch=1,
             grid=(KEY_VALUE_HEADS,),
             in_specs=in_specs,
             out_specs=out_specs,
@@ -300,14 +292,13 @@
             bytes_accessed=tokens * width * 12 + span * 2 * KV_WIDTH * 2,
         ),
         name="attention",
-    )(places, flag, *operands)
-
-
-def document_starts(lengths, positions):
+    )(info, *operands)
+
+
+def document_bounds(lengths, own_first):
     count = lengths.shape[0]
-    upto = jnp.arange(count)[:, None] >= jnp.arange(count)[None, :]
-    ends = jnp.sum(jnp.where(upto, lengths[None, :], 0), axis=1)
-    return jnp.max(jnp.where(positions[:, None] >= ends[None, :], ends[None, :], 0), axis=1, keepdims=True)
+    upto = jnp.arange(count + 1)[:, None] > jnp.arange(count)[None, :]
+    return jnp.sum(jnp.where(upto, lengths[None, :], 0), axis=1) - own_first
 
 
 def shards(carried, arrivals, gains, key_rows, value_rows, lengths, permutation):
@@ -327,31 +318,29 @@
     next_gain = lax.ppermute(gain, "section", back)
     chosen = permutation[0]
     first = lax.dynamic_index_in_dim(arrivals, chosen, 0, keepdims=False)
-    positions = context * tokens + jnp.arange(tokens, dtype=jnp.int32)
     sequences = [phase, jnp.where(phase == 0, phases + chosen, phase - 1)]
-    starts = [
-        document_starts(lax.dynamic_index_in_dim(lengths, s, 0, keepdims=False), positions) - context * tokens
+    bounds = [
+        document_bounds(lax.dynamic_index_in_dim(lengths, s, 0, keepdims=False), context * tokens)
         for s in sequences
     ]
     is_last = (phase == phases - 1).astype(jnp.int32).reshape(1)
+    info = jnp.concatenate([window_places(y), *bounds, is_last])
 
     mean = jnp.mean(stream * stream, axis=-1, keepdims=True)
     normed = (stream * lax.rsqrt(mean + EPSILON) * gain).astype(jnp.bfloat16)
-    places = window_places(y)
     keys = projection(normed, order, key_blocks)
-    own = projection(normed, order, (), keys, value_weights)
+    keys, info, first = lax.optimization_barrier((keys, info, first))
+    own = projection(normed, order, (), keys, value_weights, WHOLE)
     early, late = window_blocks(own, y)
-    part = attention(early, places[: len(early)], normed, starts[0])
-    produced, stream, normed = attention(
-        late, places[len(early) :], normed, starts[0], part, stream, (is_last, first, next_gain)
-    )
+    part = attention(early, info, 0, normed)
+    produced, stream, normed = attention(late, info, 0, normed, part, stream, (first, next_gain))
     normed = lax.ppermute(normed, "section", onward)
     normed, stream = lax.optimization_barrier((normed, stream))
     stream = lax.ppermute(stream, "section", onward)
     own = projection(normed, order, key_blocks, None, value_weights)
     early, late = window_blocks(own, y)
-    part = attention(early, places[: len(early)], normed, starts[1])
-    (produced,) = attention(late, places[len(early) :], normed, starts[1], part, stream, None, produced)
+    part = attention(early, info, 1, normed)
+    (produced,) = attention(late, info, 1, normed, part, stream, None, produced)
     return produced[:, None]
 
 

time: 192 us -> 188 us (0.979)
  waiting for transfers between devices: 69.2 us -> 86.4 us
  local copies, waits for them, and re-layouts: 18.7 us -> 7.01 us
  starting transfers between devices: 42.6 us -> 36.6 us
  other arithmetic: 5.33 us -> 3.36 us
    ppermute x29 -> x31, waiting for transfers between devices: 49.1 us -> 65.7 us  [moved(): return lax.ppermute(block, 'ctx', pairs)]
    unnamed x76 -> x50, local copies, waits for them, and re-layouts: 17 us -> 5.51 us
    all_gather x1, waiting for transfers between devices: 0.73 us -> 5.86 us  [shards(): value_weights = lax.all_gather(value_rows[0], 'ctx', axis=0, tiled=True)]
    ppermute x2 -> x0, starting transfers between devices: 4.97 us -> none  [swapped(): return lax.ppermute(block, 'ctx', pairs)]
    ppermute x2 -> x0, waiting for transfers between devices: 4.46 us -> none  [swapped(): return lax.ppermute(block, 'ctx', pairs)]
    pallas_call x4, Pallas kernels: 29.4 us -> 26.7 us  [attention(): pl.pallas_call(functools.partial(attention_body, n_blocks, stage, tick),...]
    pallas_call x3, Pallas kernels: 10 us -> 12.1 us  [projection(): pl.pallas_call(functools.partial(projection_body, n_keys, keys is not Non...]
    ppermute x29 -> x31, starting transfers between devices: 37.7 us -> 36.5 us  [moved(): return lax.ppermute(block, 'ctx', pairs)]
  transfers between devices with their start and end apart: 35 -> 35, of which waited for: 14 -> 22; matrix products, arithmetic and copies ran while one was open for 4% -> 3% of each run, Pallas kernels for 12% -> 12%
where the time goes in v4:
time: 188 us; the launch traced here: 186 us
  waiting for transfers between devices  86.4 us (46%)
  Pallas kernels  38.8 us (21%)
  starting transfers between devices  36.6 us (19%)
  between operations  14 us (7%)
  local copies, waits for them, and re-layouts  7.01 us (4%)
  other arithmetic  3.36 us (2%)
    ppermute x31, waiting for transfers between devices, moved(): return lax.ppermute(block, 'ctx', pairs)  65.7 us
    ppermute x31, starting transfers between devices, moved(): return lax.ppermute(block, 'ctx', pairs)  36.5 us
    pallas_call x4, Pallas kernels, attention(): pl.pallas_call(functools.partial(attention_body, n_blocks, stage, tick),...  26.7 us
    ppermute x1, waiting for transfers between devices, shards(): normed = lax.ppermute(normed, 'section', onward)  14.2 us
    pallas_call x3, Pallas kernels, projection(): pl.pallas_call(functools.partial(projection_body, n_keys, keys is not Non...  12.1 us
    all_gather x1, waiting for transfers between devices, shards(): value_weights = lax.all_gather(value_rows[0], 'ctx', axis=0, tiled=True)  5.86 us
    unnamed x50, local copies, waits for them, and re-layouts  5.51 us
  transfers between devices with their start and end apart: 35, of which 22 were waited for; matrix products, arithmetic and copies ran while one was open for 3% of the time, Pallas kernels for 12%

profile of v4, /device:TPU:2, one launch (start us, length us, event | category | flops | bytes accessed | tf_op | source)
XLA Modules:
  0.0 186.1 jit_solution(18309202059536350158)
XLA Ops:
  7.3 4.0 %collective-permute-start.5 = (bf16[256,512]{1,0:T(8,128)(2,1)}, bf16[256,512]{1,0:T(8,128)(2,1)}, u32[]{:S(2)}, u32[]{:S(2)}) collective-permute-start(bf16[256,512]{1,0:T(8,128)(2,1)} %bitcast.39), channel_id=1, source_target_pairs={{0,8},{1,9},{2,10},{3,11},{4,12},{5,13},{6,14},{7,15},{8,0},{9,1},... | collective-permute-start | bytes 786440 | tf_op jit(solution)/shard_map/ppermute | solution.py:37
  11.2 3.2 %collective-permute-start.4 = (bf16[256,512]{1,0:T(8,128)(2,1)}, bf16[256,512]{1,0:T(8,128)(2,1)}, u32[]{:S(2)}, u32[]{:S(2)}) collective-permute-start(bf16[256,512]{1,0:T(8,128)(2,1)} %bitcast.40), channel_id=1, source_target_pairs={{0,2},{1,3},{2,0},{3,1},{4,6},{5,7},{6,4},{7,5},{8,10},{9,11},{10,... | collective-permute-start | bytes 786440 | tf_op jit(solution)/shard_map/ppermute | solution.py:37
  14.4 1.1 collective-permute-start.3
  16.2 1.0 collective-permute-start.1
  17.2 1.8 multiply_reduce_fusion
  20.0 1.4 collective-permute-start
  21.4 0.9 collective-permute-done.4.refs_5_
  22.3 3.1 %collective-permute-start.13 = (bf16[256,512]{1,0:T(8,128)(2,1)}, bf16[256,512]{1,0:T(8,128)(2,1)}, u32[]{:S(2)}, u32[]{:S(2)}) collective-permute-start(bf16[256,512]{1,0:T(8,128)(2,1)} %collective-permute-done.5.refs_6_), channel_id=1, source_target_pairs={{0,3},{1,0},{2,1},{3,2},{4,7},{5,4},{6,5},{7,6},{8,11},{9,8},{10,9... | collective-permute-start | bytes 786440 | tf_op jit(solution)/shard_map/ppermute | solution.py:37
  25.3 4.8 %collective-permute-done.3.refs_4_ = bf16[256,512]{1,0:T(8,128)(2,1)} collective-permute-done((bf16[256,512]{1,0:T(8,128)(2,1)}, bf16[256,512]{1,0:T(8,128)(2,1)}, u32[]{:S(2)}, u32[]{:S(2)}) %collective-permute-start.3) | collective-permute-done | bytes 262176 | tf_op jit(solution)/shard_map/ppermute | solution.py:37
  30.3 1.9 %collective-permute-start.10 = (bf16[256,512]{1,0:T(8,128)(2,1)}, bf16[256,512]{1,0:T(8,128)(2,1)}, u32[]{:S(2)}, u32[]{:S(2)}) collective-permute-start(bf16[256,512]{1,0:T(8,128)(2,1)} %collective-permute-done.4.refs_5_), channel_id=1, source_target_pairs={{0,4},{1,5},{2,6},{3,7},{4,8},{5,9},{6,10},{7,11},{8,12},{9,13},{1... | collective-permute-start | bytes 786440 | tf_op jit(solution)/shard_map/ppermute | solution.py:37
  32.6 1.2 collective-permute-start.8
  33.8 2.8 %collective-permute-done.13.refs_14_ = bf16[256,512]{1,0:T(8,128)(2,1)} collective-permute-done((bf16[256,512]{1,0:T(8,128)(2,1)}, bf16[256,512]{1,0:T(8,128)(2,1)}, u32[]{:S(2)}, u32[]{:S(2)}) %collective-permute-start.13) | collective-permute-done | bytes 262176 | tf_op jit(solution)/shard_map/ppermute | solution.py:37
  36.6 2.6 %collective-permute-start.7 = (bf16[256,512]{1,0:T(8,128)(2,1)}, bf16[256,512]{1,0:T(8,128)(2,1)S(1)}, u32[]{:S(2)}, u32[]{:S(2)}) collective-permute-start(bf16[256,512]{1,0:T(8,128)(2,1)} %collective-permute-done.2.refs_3_), channel_id=1, source_target_pairs={{0,3},{1,0},{2,1},{3,2},{4,7},{5,4},{6,5},{7,6},{8,11},{9,8},{10,9... | collective-permute-start | bytes 786440 | tf_op jit(solution)/shard_map/ppermute | solution.py:37
  40.1 1.2 collective-permute-done.10.refs_11_
  42.0 1.1 dynamic-slice_bitcast_fusion.refs_7_
  43.1 3.7 %collective-permute-done.8.refs_9_ = bf16[256,512]{1,0:T(8,128)(2,1)S(1)} collective-permute-done((bf16[256,512]{1,0:T(8,128)(2,1)}, bf16[256,512]{1,0:T(8,128)(2,1)S(1)}, u32[]{:S(2)}, u32[]{:S(2)}) %collective-permute-start.8) | collective-permute-done | bytes 262176 | tf_op jit(solution)/shard_map/ppermute | solution.py:37
  46.8 2.1 %collective-permute-done.9.refs_10_ = bf16[256,512]{1,0:T(8,128)(2,1)S(1)} collective-permute-done((bf16[256,512]{1,0:T(8,128)(2,1)}, bf16[256,512]{1,0:T(8,128)(2,1)S(1)}, u32[]{:S(2)}, u32[]{:S(2)}) %collective-permute-start.9) | collective-permute-done | bytes 262176 | tf_op jit(solution)/shard_map/ppermute | solution.py:37
  48.9 2.3 %collective-permute-done.6.refs_7_ = bf16[256,512]{1,0:T(8,128)(2,1)S(1)} collective-permute-done((bf16[256,512]{1,0:T(8,128)(2,1)}, bf16[256,512]{1,0:T(8,128)(2,1)S(1)}, u32[]{:S(2)}, u32[]{:S(2)}) %collective-permute-start.6) | collective-permute-done | bytes 262176 | tf_op jit(solution)/shard_map/ppermute | solution.py:37
  51.2 4.5 %collective-permute-done.14.refs_15_ = bf16[256,512]{1,0:T(8,128)(2,1)S(1)} collective-permute-done((bf16[256,512]{1,0:T(8,128)(2,1)}, bf16[256,512]{1,0:T(8,128)(2,1)S(1)}, u32[]{:S(2)}, u32[]{:S(2)}) %collective-permute-start.14) | collective-permute-done | bytes 262176 | tf_op jit(solution)/shard_map/ppermute | solution.py:37
  55.8 3.0 %projection.3.refs_0_ = bf16[128,512]{1,0:T(8,128)(2,1)S(1)} custom-call(s32[16]{0:T(128)S(1)} %stack.85.order, bf16[128,4096]{1,0:T(8,128)(2,1)S(1)} %multiply_convert_fusion.rows.q, bf16[256,512]{1,0:T(8,128)(2,1)S(1)} %bitcast.45, bf16[256,512]{1,0:T(8,128)(2,1)} %collective-permute-done.refs_1_, bf16[256,512]{1,0:T(8,128)(2,1)} %collective-permute-done.1.refs_2_, ...), custom_call_target="tpu_custom_call" | custom-call | flops 536870912 | bytes 4194304 | tf_op jit(solution)/shard_map/projection/pallas_call | solution.py:145
  63.0 5.9 %all-gather.3.cloned.1.call-done = bf16[1,4096,512]{2,1,0:T(8,128)(2,1)} async-done(((bf16[1,256,512]{2,1,0:T(8,128)(2,1)}), bf16[1,4096,512]{2,1,0:T(8,128)(2,1)}) %all-gather.3.cloned.1.call-update) | async-done | bytes 4194320 | tf_op jit(solution)/shard_map/all_gather | solution.py:315
  68.9 4.5 %projection.4.refs_0_ = bf16[128,1024]{1,0:T(8,128)(2,1)} custom-call(s32[16]{0:T(128)} %copy-done.20, bf16[128,4096]{1,0:T(8,128)(2,1)} %copy-done.4, bf16[128,512]{1,0:T(8,128)(2,1)} %copy-done.19, bf16[4096,512]{1,0:T(8,128)(2,1)} %bitcast.37), custom_call_target="tpu_custom_call" | custom-call | flops 536870912 | bytes 4194304 | tf_op jit(solution)/shard_map/projection/pallas_call | solution.py:145
  73.8 9.5 %collective-permute-done.15.refs_1_ = bf16[128,1024]{1,0:T(8,128)(2,1)} collective-permute-done((bf16[128,1024]{1,0:T(8,128)(2,1)}, bf16[128,1024]{1,0:T(8,128)(2,1)}, u32[]{:S(2)}, u32[]{:S(2)}) %collective-permute-start.15) | collective-permute-done | bytes 262176 | tf_op jit(solution)/shard_map/ppermute | solution.py:37
  83.3 2.4 %collective-permute-start.22 = (bf16[128,1024]{1,0:T(8,128)(2,1)}, bf16[128,1024]{1,0:T(8,128)(2,1)}, u32[]{:S(2)}, u32[]{:S(2)}) collective-permute-start(bf16[128,1024]{1,0:T(8,128)(2,1)} %collective-permute-done.15.refs_1_), channel_id=1, source_target_pairs={{0,2},{1,3},{2,0},{3,1},{4,6},{5,7},{6,4},{7,5},{8,10},{9,11},{10,... | collective-permute-start | bytes 786440 | tf_op jit(solution)/shard_map/ppermute | solution.py:37
  86.4 1.3 collective-permute-start.20
  87.7 4.5 %collective-permute-done.16.refs_2_ = bf16[128,1024]{1,0:T(8,128)(2,1)} collective-permute-done((bf16[128,1024]{1,0:T(8,128)(2,1)}, bf16[128,1024]{1,0:T(8,128)(2,1)}, u32[]{:S(2)}, u32[]{:S(2)}) %collective-permute-start.16) | collective-permute-done | bytes 262176 | tf_op jit(solution)/shard_map/ppermute | solution.py:37
  92.2 1.1 broadcast_select_fusion.1
  93.3 2.5 %collective-permute-start.19 = (bf16[128,1024]{1,0:T(8,128)(2,1)S(1)}, bf16[128,1024]{1,0:T(8,128)(2,1)S(1)}, u32[]{:S(2)}, u32[]{:S(2)}) collective-permute-start(bf16[128,1024]{1,0:T(8,128)(2,1)S(1)} %get-tuple-element.38), channel_id=1, source_target_pairs={{0,2},{1,3},{2,0},{3,1},{4,6},{5,7},{6,4},{7,5},{8,10},{9,11},{10,... | collective-permute-start | bytes 786440 | tf_op jit(solution)/shard_map/ppermute | solution.py:37
  96.5 1.3 collective-permute-start.17
  97.8 1.2 collective-permute-done.21.refs_4_
  98.9 3.8 %collective-permute-done.20.refs_3_ = bf16[128,1024]{1,0:T(8,128)(2,1)S(1)} collective-permute-done((bf16[128,1024]{1,0:T(8,128)(2,1)}, bf16[128,1024]{1,0:T(8,128)(2,1)S(1)}, u32[]{:S(2)}, u32[]{:S(2)}) %collective-permute-start.20) | collective-permute-done | bytes 262176 | tf_op jit(solution)/shard_map/ppermute | solution.py:37
  102.7 0.9 copy-done.18
  103.7 7.7 %attention.4 = (f32[4096,128]{1,0:T(8,128)S(1)}, f32[4096,128]{1,0:T(8,128)S(1)}, f32[4096,128]{1,0:T(8,128)S(1)}) custom-call(s32[28]{0:T(128)S(1)} %concatenate.3.info, bf16[128,4096]{1,0:T(8,128)(2,1)S(1)} %copy-done.5, bf16[128,1024]{1,0:T(8,128)(2,1)S(1)} %copy-done.18, bf16[128,1024]{1,0:T(8,128)(2,1)} %collective-permute-done.15.refs_1_, ...), custom_call_target="tpu_custom_call" | custom-call | flops 1610612736 | bytes 7864320 | tf_op jit(solution)/shard_map/attention/pallas_call | solution.py:277
  111.5 6.5 %attention.5 = (bf16[2,128,4096]{2,1,0:T(8,128)(2,1)}, f32[128,4096]{1,0:T(8,128)S(1)}, bf16[128,4096]{1,0:T(8,128)(2,1)S(1)}) custom-call(s32[28]{0:T(128)S(1)} %concatenate.3.info, bf16[128,4096]{1,0:T(8,128)(2,1)S(1)} %copy-done.5, bf16[128,1024]{1,0:T(8,128)(2,1)S(1)} %collective-permute-done.17.refs_0_, ...), custom_call_target="tpu_custom_call" | custom-call | flops 805306368 | bytes 7077888 | tf_op jit(solution)/shard_map/attention/pallas_call | solution.py:277
  118.1 14.2 %collective-permute-done.24.rows.q = bf16[128,4096]{1,0:T(8,128)(2,1)S(1)} collective-permute-done((bf16[128,4096]{1,0:T(8,128)(2,1)S(1)}, bf16[128,4096]{1,0:T(8,128)(2,1)S(1)}, u32[]{:S(2)}, u32[]{:S(2)}) %collective-permute-start.24) | collective-permute-done | bytes 1048608 | tf_op jit(solution)/shard_map/ppermute | solution.py:337
  132.4 4.5 %projection.5.refs_0_ = bf16[128,1024]{1,0:T(8,128)(2,1)S(1)} custom-call(s32[16]{0:T(128)S(1)} %copy-done.21, bf16[128,4096]{1,0:T(8,128)(2,1)S(1)} %collective-permute-done.24.rows.q, bf16[256,512]{1,0:T(8,128)(2,1)S(1)} %bitcast.46, bf16[256,512]{1,0:T(8,128)(2,1)} %collective-permute-done.refs_1_, bf16[256,512]{1,0:T(8,128)(2,1)} %collective-permute-done.1.refs_2_, ...), custom_call_target="tpu_custom_call" | custom-call | flops 1073741824 | bytes 8388608 | tf_op jit(solution)/shard_map/projection/pallas_call | solution.py:145
  137.0 9.5 %collective-permute-done.25.refs_1_ = bf16[128,1024]{1,0:T(8,128)(2,1)S(1)} collective-permute-done((bf16[128,1024]{1,0:T(8,128)(2,1)S(1)}, bf16[128,1024]{1,0:T(8,128)(2,1)S(1)}, u32[]{:S(2)}, u32[]{:S(2)}) %collective-permute-start.25) | collective-permute-done | bytes 262176 | tf_op jit(solution)/shard_map/ppermute | solution.py:37
  146.9 1.3 collective-permute-start.32
  148.2 0.7 collective-permute-start.31
  148.9 7.7 %collective-permute-done.26.refs_2_ = bf16[128,1024]{1,0:T(8,128)(2,1)S(1)} collective-permute-done((bf16[128,1024]{1,0:T(8,128)(2,1)S(1)}, bf16[128,1024]{1,0:T(8,128)(2,1)S(1)}, u32[]{:S(2)}, u32[]{:S(2)}) %collective-permute-start.26) | collective-permute-done | bytes 262176 | tf_op jit(solution)/shard_map/ppermute | solution.py:37
  157.2 1.0 collective-permute-start.28
  158.2 1.6 collective-permute-done.32.refs_4_
  159.8 1.9 %collective-permute-start.27 = (bf16[128,1024]{1,0:T(8,128)(2,1)S(1)}, bf16[128,1024]{1,0:T(8,128)(2,1)S(1)}, u32[]{:S(2)}, u32[]{:S(2)}) collective-permute-start(bf16[128,1024]{1,0:T(8,128)(2,1)S(1)} %get-tuple-element.37), channel_id=1, source_target_pairs={{0,1},{1,2},{2,3},{3,0},{4,5},{5,6},{6,7},{7,4},{8,9},{9,10},{10,1... | collective-permute-start | bytes 786440 | tf_op jit(solution)/shard_map/ppermute | solution.py:37
  161.7 1.0 collective-permute-done.31.refs_3_
  162.7 7.0 %attention.6 = (f32[4096,128]{1,0:T(8,128)S(1)}, f32[4096,128]{1,0:T(8,128)S(1)}, f32[4096,128]{1,0:T(8,128)S(1)}) custom-call(s32[28]{0:T(128)S(1)} %concatenate.3.info, bf16[128,4096]{1,0:T(8,128)(2,1)S(1)} %collective-permute-done.24.rows.q, bf16[128,1024]{1,0:T(8,128)(2,1)S(1)} %projection.5.refs_0_, ...), custom_call_target="tpu_custom_call" | custom-call | flops 1610612736 | bytes 7864320 | tf_op jit(solution)/shard_map/attention/pallas_call | solution.py:277
  169.7 0.9 collective-permute-done.28.refs_1_
  170.7 3.1 %collective-permute-done.27.refs_0_ = bf16[128,1024]{1,0:T(8,128)(2,1)S(1)} collective-permute-done((bf16[128,1024]{1,0:T(8,128)(2,1)S(1)}, bf16[128,1024]{1,0:T(8,128)(2,1)S(1)}, u32[]{:S(2)}, u32[]{:S(2)}) %collective-permute-start.27) | collective-permute-done | bytes 262176 | tf_op jit(solution)/shard_map/ppermute | solution.py:37
  173.8 5.5 %attention.7 = bf16[2,128,4096]{2,1,0:T(8,128)(2,1)} custom-call(s32[28]{0:T(128)S(1)} %concatenate.3.info, bf16[128,4096]{1,0:T(8,128)(2,1)S(1)} %collective-permute-done.24.rows.q, bf16[128,1024]{1,0:T(8,128)(2,1)S(1)} %collective-permute-done.27.refs_0_, bf16[128,1024]{1,0:T(8,128)(2,1)S(1)} %collective-permute-done.28.refs_1_, ...), custom_call_target="tpu_custom_call", output_to_operand_aliasing={{}: (9, {})} | custom-call | flops 805306368 | bytes 7077888 | tf_op jit(solution)/shard_map/attention/pallas_call | solution.py:277
  (92 shorter events, 11.4 us)
Async XLA Ops:
  6.5 35.4 %copy-start = (bf16[2,128,4096]{2,1,0:T(8,128)(2,1)S(1)}, bf16[2,128,4096]{2,1,0:T(8,128)(2,1)}, u32[]{:S(2)}) copy-start(bf16[2,128,4096]{2,1,0:T(8,128)(2,1)} %param.8) | copy-start | bytes 6291460
  6.5 62.3 %all-gather.3.cloned.1.call-start = ((), (), s32[]{:S(2)}) async-start(), calls=%async_computation | async-start | bytes 4456448 | tf_op jit(solution)/shard_map/all_gather | solution.py:315
  7.3 12.7 %collective-permute-start.5 = (bf16[256,512]{1,0:T(8,128)(2,1)}, bf16[256,512]{1,0:T(8,128)(2,1)}, u32[]{:S(2)}, u32[]{:S(2)}) collective-permute-start(bf16[256,512]{1,0:T(8,128)(2,1)} %bitcast.39), channel_id=1, source_target_pairs={{0,8},{1,9},{2,10},{3,11},{4,12},{5,13},{6,14},{7,15},{8,0},{9,1},... | collective-permute-start | bytes 786440 | tf_op jit(solution)/shard_map/ppermute | solution.py:37
  11.2 11.1 %collective-permute-start.4 = (bf16[256,512]{1,0:T(8,128)(2,1)}, bf16[256,512]{1,0:T(8,128)(2,1)}, u32[]{:S(2)}, u32[]{:S(2)}) collective-permute-start(bf16[256,512]{1,0:T(8,128)(2,1)} %bitcast.40), channel_id=1, source_target_pairs={{0,2},{1,3},{2,0},{3,1},{4,6},{5,7},{6,4},{7,5},{8,10},{9,11},{10,... | collective-permute-start | bytes 786440 | tf_op jit(solution)/shard_map/ppermute | solution.py:37
  14.4 15.7 %collective-permute-start.3 = (bf16[256,512]{1,0:T(8,128)(2,1)}, bf16[256,512]{1,0:T(8,128)(2,1)}, u32[]{:S(2)}, u32[]{:S(2)}) collective-permute-start(bf16[256,512]{1,0:T(8,128)(2,1)} %bitcast.41), channel_id=1, source_target_pairs={{0,3},{1,0},{2,1},{3,2},{4,7},{5,4},{6,5},{7,6},{8,11},{9,8},{10,9... | collective-permute-start | bytes 786440 | tf_op jit(solution)/shard_map/ppermute | solution.py:37
  15.5 14.7 %collective-permute-start.2 = (bf16[256,512]{1,0:T(8,128)(2,1)}, bf16[256,512]{1,0:T(8,128)(2,1)}, u32[]{:S(2)}, u32[]{:S(2)}) collective-permute-start(bf16[256,512]{1,0:T(8,128)(2,1)} %bitcast.42), channel_id=1, source_target_pairs={{0,12},{1,13},{2,14},{3,15},{4,0},{5,1},{6,2},{7,3},{8,4},{9,5},{1... | collective-permute-start | bytes 786440 | tf_op jit(solution)/shard_map/ppermute | solution.py:37
  16.2 14.1 %collective-permute-start.1 = (bf16[256,512]{1,0:T(8,128)(2,1)}, bf16[256,512]{1,0:T(8,128)(2,1)}, u32[]{:S(2)}, u32[]{:S(2)}) collective-permute-start(bf16[256,512]{1,0:T(8,128)(2,1)} %bitcast.43), channel_id=1, source_target_pairs={{0,1},{1,2},{2,3},{3,0},{4,5},{5,6},{6,7},{7,4},{8,9},{9,10},{10,1... | collective-permute-start | bytes 786440 | tf_op jit(solution)/shard_map/ppermute | solution.py:37
  19.3 39.5 %copy-start.4 = (bf16[128,4096]{1,0:T(8,128)(2,1)}, bf16[128,4096]{1,0:T(8,128)(2,1)S(1)}, u32[]{:S(2)}) copy-start(bf16[128,4096]{1,0:T(8,128)(2,1)S(1)} %multiply_convert_fusion.rows.q) | copy-start | bytes 3145732
  20.0 12.5 %collective-permute-start = (bf16[256,512]{1,0:T(8,128)(2,1)S(1)}, bf16[256,512]{1,0:T(8,128)(2,1)}, u32[]{:S(2)}, u32[]{:S(2)}) collective-permute-start(bf16[256,512]{1,0:T(8,128)(2,1)S(1)} %bitcast.44), channel_id=1, source_target_pairs={{0,4},{1,5},{2,6},{3,7},{4,8},{5,9},{6,10},{7,11},{8,12},{9,13},{1... | collective-permute-start | bytes 786440 | tf_op jit(solution)/shard_map/ppermute | solution.py:37
  22.3 14.4 %collective-permute-start.13 = (bf16[256,512]{1,0:T(8,128)(2,1)}, bf16[256,512]{1,0:T(8,128)(2,1)}, u32[]{:S(2)}, u32[]{:S(2)}) collective-permute-start(bf16[256,512]{1,0:T(8,128)(2,1)} %collective-permute-done.5.refs_6_), channel_id=1, source_target_pairs={{0,3},{1,0},{2,1},{3,2},{4,7},{5,4},{6,5},{7,6},{8,11},{9,8},{10,9... | collective-permute-start | bytes 786440 | tf_op jit(solution)/shard_map/ppermute | solution.py:37
  30.2 9.3 %collective-permute-start.12 = (bf16[256,512]{1,0:T(8,128)(2,1)}, bf16[256,512]{1,0:T(8,128)(2,1)}, u32[]{:S(2)}, u32[]{:S(2)}) collective-permute-start(bf16[256,512]{1,0:T(8,128)(2,1)} %collective-permute-done.5.refs_6_), channel_id=1, source_target_pairs={{0,1},{1,2},{2,3},{3,0},{4,5},{5,6},{6,7},{7,4},{8,9},{9,10},{10,1... | collective-permute-start | bytes 786440 | tf_op jit(solution)/shard_map/ppermute | solution.py:37
  30.2 9.8 %collective-permute-start.11 = (bf16[256,512]{1,0:T(8,128)(2,1)}, bf16[256,512]{1,0:T(8,128)(2,1)}, u32[]{:S(2)}, u32[]{:S(2)}) collective-permute-start(bf16[256,512]{1,0:T(8,128)(2,1)} %collective-permute-done.4.refs_5_), channel_id=1, source_target_pairs={{0,12},{1,13},{2,14},{3,15},{4,0},{5,1},{6,2},{7,3},{8,4},{9,5},{1... | collective-permute-start | bytes 786440 | tf_op jit(solution)/shard_map/ppermute | solution.py:37
  30.3 11.0 %collective-permute-start.10 = (bf16[256,512]{1,0:T(8,128)(2,1)}, bf16[256,512]{1,0:T(8,128)(2,1)}, u32[]{:S(2)}, u32[]{:S(2)}) collective-permute-start(bf16[256,512]{1,0:T(8,128)(2,1)} %collective-permute-done.4.refs_5_), channel_id=1, source_target_pairs={{0,4},{1,5},{2,6},{3,7},{4,8},{5,9},{6,10},{7,11},{8,12},{9,13},{1... | collective-permute-start | bytes 786440 | tf_op jit(solution)/shard_map/ppermute | solution.py:37
  32.5 26.3 %copy-start.20 = (s32[16]{0:T(128)}, s32[16]{0:T(128)S(1)}, u32[]{:S(2)}) copy-start(s32[16]{0:T(128)S(1)} %stack.85.order) | copy-start | bytes 196
  32.6 14.2 %collective-permute-start.8 = (bf16[256,512]{1,0:T(8,128)(2,1)}, bf16[256,512]{1,0:T(8,128)(2,1)S(1)}, u32[]{:S(2)}, u32[]{:S(2)}) collective-permute-start(bf16[256,512]{1,0:T(8,128)(2,1)} %collective-permute-done.3.refs_4_), channel_id=1, source_target_pairs={{0,4},{1,5},{2,6},{3,7},{4,8},{5,9},{6,10},{7,11},{8,12},{9,13},{1... | collective-permute-start | bytes 786440 | tf_op jit(solution)/shard_map/ppermute | solution.py:37
  36.6 10.1 %collective-permute-start.7 = (bf16[256,512]{1,0:T(8,128)(2,1)}, bf16[256,512]{1,0:T(8,128)(2,1)S(1)}, u32[]{:S(2)}, u32[]{:S(2)}) collective-permute-start(bf16[256,512]{1,0:T(8,128)(2,1)} %collective-permute-done.2.refs_3_), channel_id=1, source_target_pairs={{0,3},{1,0},{2,1},{3,2},{4,7},{5,4},{6,5},{7,6},{8,11},{9,8},{10,9... | collective-permute-start | bytes 786440 | tf_op jit(solution)/shard_map/ppermute | solution.py:37
  39.5 9.4 %collective-permute-start.9 = (bf16[256,512]{1,0:T(8,128)(2,1)}, bf16[256,512]{1,0:T(8,128)(2,1)S(1)}, u32[]{:S(2)}, u32[]{:S(2)}) collective-permute-start(bf16[256,512]{1,0:T(8,128)(2,1)} %collective-permute-done.1.refs_2_), channel_id=1, source_target_pairs={{0,12},{1,13},{2,14},{3,15},{4,0},{5,1},{6,2},{7,3},{8,4},{9,5},{1... | collective-permute-start | bytes 786440 | tf_op jit(solution)/shard_map/ppermute | solution.py:37
  40.0 11.2 %collective-permute-start.6 = (bf16[256,512]{1,0:T(8,128)(2,1)}, bf16[256,512]{1,0:T(8,128)(2,1)S(1)}, u32[]{:S(2)}, u32[]{:S(2)}) collective-permute-start(bf16[256,512]{1,0:T(8,128)(2,1)} %collective-permute-done.refs_1_), channel_id=1, source_target_pairs={{0,1},{1,2},{2,3},{3,0},{4,5},{5,6},{6,7},{7,4},{8,9},{9,10},{10,1... | collective-permute-start | bytes 786440 | tf_op jit(solution)/shard_map/ppermute | solution.py:37
  41.3 14.5 %collective-permute-start.14 = (bf16[256,512]{1,0:T(8,128)(2,1)}, bf16[256,512]{1,0:T(8,128)(2,1)S(1)}, u32[]{:S(2)}, u32[]{:S(2)}) collective-permute-start(bf16[256,512]{1,0:T(8,128)(2,1)} %collective-permute-done.10.refs_11_), channel_id=1, source_target_pairs={{0,4},{1,5},{2,6},{3,7},{4,8},{5,9},{6,10},{7,11},{8,12},{9,13},{1... | collective-permute-start | bytes 786440 | tf_op jit(solution)/shard_map/ppermute | solution.py:37
  68.9 33.8 %copy-start.5 = (bf16[128,4096]{1,0:T(8,128)(2,1)S(1)}, bf16[128,4096]{1,0:T(8,128)(2,1)}, u32[]{:S(2)}) copy-start(bf16[128,4096]{1,0:T(8,128)(2,1)} %copy-done.4) | copy-start | bytes 3145732
  73.4 9.9 %collective-permute-start.15 = (bf16[128,1024]{1,0:T(8,128)(2,1)}, bf16[128,1024]{1,0:T(8,128)(2,1)}, u32[]{:S(2)}, u32[]{:S(2)}) collective-permute-start(bf16[128,1024]{1,0:T(8,128)(2,1)} %projection.4.refs_0_), channel_id=1, source_target_pairs={{0,4},{1,5},{2,6},{3,7},{4,8},{5,9},{6,10},{7,11},{8,12},{9,13},{1... | collective-permute-start | bytes 786440 | tf_op jit(solution)/shard_map/ppermute | solution.py:37
  83.3 8.9 %collective-permute-start.16 = (bf16[128,1024]{1,0:T(8,128)(2,1)}, bf16[128,1024]{1,0:T(8,128)(2,1)}, u32[]{:S(2)}, u32[]{:S(2)}) collective-permute-start(bf16[128,1024]{1,0:T(8,128)(2,1)} %collective-permute-done.15.refs_1_), channel_id=1, source_target_pairs={{0,4},{1,5},{2,6},{3,7},{4,8},{5,9},{6,10},{7,11},{8,12},{9,13},{1... | collective-permute-start | bytes 786440 | tf_op jit(solution)/shard_map/ppermute | solution.py:37
  83.3 13.2 %collective-permute-start.22 = (bf16[128,1024]{1,0:T(8,128)(2,1)}, bf16[128,1024]{1,0:T(8,128)(2,1)}, u32[]{:S(2)}, u32[]{:S(2)}) collective-permute-start(bf16[128,1024]{1,0:T(8,128)(2,1)} %collective-permute-done.15.refs_1_), channel_id=1, source_target_pairs={{0,2},{1,3},{2,0},{3,1},{4,6},{5,7},{6,4},{7,5},{8,10},{9,11},{10,... | collective-permute-start | bytes 786440 | tf_op jit(solution)/shard_map/ppermute | solution.py:37
  85.7 13.3 %collective-permute-start.21 = (bf16[128,1024]{1,0:T(8,128)(2,1)}, bf16[128,1024]{1,0:T(8,128)(2,1)S(1)}, u32[]{:S(2)}, u32[]{:S(2)}) collective-permute-start(bf16[128,1024]{1,0:T(8,128)(2,1)} %collective-permute-done.15.refs_1_), channel_id=1, source_target_pairs={{0,3},{1,0},{2,1},{3,2},{4,7},{5,4},{6,5},{7,6},{8,11},{9,8},{10,9... | collective-permute-start | bytes 786440 | tf_op jit(solution)/shard_map/ppermute | solution.py:37
  86.4 16.3 %collective-permute-start.20 = (bf16[128,1024]{1,0:T(8,128)(2,1)}, bf16[128,1024]{1,0:T(8,128)(2,1)S(1)}, u32[]{:S(2)}, u32[]{:S(2)}) collective-permute-start(bf16[128,1024]{1,0:T(8,128)(2,1)} %collective-permute-done.15.refs_1_), channel_id=1, source_target_pairs={{0,1},{1,2},{2,3},{3,0},{4,5},{5,6},{6,7},{7,4},{8,9},{9,10},{10,1... | collective-permute-start | bytes 786440 | tf_op jit(solution)/shard_map/ppermute | solution.py:37
  93.3 18.1 %collective-permute-start.19 = (bf16[128,1024]{1,0:T(8,128)(2,1)S(1)}, bf16[128,1024]{1,0:T(8,128)(2,1)S(1)}, u32[]{:S(2)}, u32[]{:S(2)}) collective-permute-start(bf16[128,1024]{1,0:T(8,128)(2,1)S(1)} %get-tuple-element.38), channel_id=1, source_target_pairs={{0,2},{1,3},{2,0},{3,1},{4,6},{5,7},{6,4},{7,5},{8,10},{9,11},{10,... | collective-permute-start | bytes 786440 | tf_op jit(solution)/shard_map/ppermute | solution.py:37
  95.7 15.7 %collective-permute-start.18 = (bf16[128,1024]{1,0:T(8,128)(2,1)S(1)}, bf16[128,1024]{1,0:T(8,128)(2,1)S(1)}, u32[]{:S(2)}, u32[]{:S(2)}) collective-permute-start(bf16[128,1024]{1,0:T(8,128)(2,1)S(1)} %get-tuple-element.39), channel_id=1, source_target_pairs={{0,3},{1,0},{2,1},{3,2},{4,7},{5,4},{6,5},{7,6},{8,11},{9,8},{10,9... | collective-permute-start | bytes 786440 | tf_op jit(solution)/shard_map/ppermute | solution.py:37
  96.5 15.0 %copy-start.2 = (f32[1,128,4096]{2,1,0:T(8,128)S(1)}, f32[1,128,4096]{2,1,0:T(8,128)}, u32[]{:S(2)}) copy-start(f32[1,128,4096]{2,1,0:T(8,128)} %param.7) | copy-start | bytes 6291460
  96.5 15.0 %copy-start.6 = (bf16[128,4096]{1,0:T(8,128)(2,1)S(1)}, bf16[128,4096]{1,0:T(8,128)(2,1)}, u32[]{:S(2)}) copy-start(bf16[128,4096]{1,0:T(8,128)(2,1)} %dynamic-slice_bitcast_fusion.refs_7_) | copy-start | bytes 3145732
  96.5 14.9 %collective-permute-start.17 = (bf16[128,1024]{1,0:T(8,128)(2,1)S(1)}, bf16[128,1024]{1,0:T(8,128)(2,1)S(1)}, u32[]{:S(2)}, u32[]{:S(2)}) collective-permute-start(bf16[128,1024]{1,0:T(8,128)(2,1)S(1)} %get-tuple-element.40), channel_id=1, source_target_pairs={{0,1},{1,2},{2,3},{3,0},{4,5},{5,6},{6,7},{7,4},{8,9},{9,10},{10,1... | collective-permute-start | bytes 786440 | tf_op jit(solution)/shard_map/ppermute | solution.py:37
  98.9 12.5 %collective-permute-start.23 = (f32[1,4096]{1,0:T(1,128)S(1)}, f32[1,4096]{1,0:T(1,128)S(1)}, u32[]{:S(2)}, u32[]{:S(2)}) collective-permute-start(f32[1,4096]{1,0:T(1,128)S(1)} %copy-done.22), channel_id=1, source_target_pairs={{16,0},{32,16},{48,32},{64,48},{80,64},{96,80},{112,96},{0,112},{1... | collective-permute-start | bytes 49160 | tf_op jit(solution)/shard_map/ppermute | solution.py:318
  111.5 20.8 %copy-start.3 = (bf16[1,4096,512]{2,1,0:T(8,128)(2,1)S(1)}, bf16[1,4096,512]{2,1,0:T(8,128)(2,1)}, u32[]{:S(2)}) copy-start(bf16[1,4096,512]{2,1,0:T(8,128)(2,1)} %all-gather.3.cloned.1.call-done) | copy-start | bytes 12582916
  111.5 20.8 %copy-start.9 = (bf16[256,512]{1,0:T(8,128)(2,1)S(1)}, bf16[256,512]{1,0:T(8,128)(2,1)}, u32[]{:S(2)}) copy-start(bf16[256,512]{1,0:T(8,128)(2,1)} %copy-done.8) | copy-start | bytes 786436
  111.5 20.8 %copy-start.11 = (bf16[256,512]{1,0:T(8,128)(2,1)S(1)}, bf16[256,512]{1,0:T(8,128)(2,1)}, u32[]{:S(2)}) copy-start(bf16[256,512]{1,0:T(8,128)(2,1)} %copy-done.10) | copy-start | bytes 786436
  111.5 20.8 %copy-start.13 = (bf16[256,512]{1,0:T(8,128)(2,1)S(1)}, bf16[256,512]{1,0:T(8,128)(2,1)}, u32[]{:S(2)}) copy-start(bf16[256,512]{1,0:T(8,128)(2,1)} %copy-done.12) | copy-start | bytes 786436
  111.5 20.8 %copy-start.15 = (bf16[256,512]{1,0:T(8,128)(2,1)S(1)}, bf16[256,512]{1,0:T(8,128)(2,1)}, u32[]{:S(2)}) copy-start(bf16[256,512]{1,0:T(8,128)(2,1)} %copy-done.14) | copy-start | bytes 786436
  111.5 20.8 %copy-start.17 = (bf16[256,512]{1,0:T(8,128)(2,1)S(1)}, bf16[256,512]{1,0:T(8,128)(2,1)}, u32[]{:S(2)}) copy-start(bf16[256,512]{1,0:T(8,128)(2,1)} %copy-done.16) | copy-start | bytes 786436
  111.5 20.8 %copy-start.21 = (s32[16]{0:T(128)S(1)}, s32[16]{0:T(128)}, u32[]{:S(2)}) copy-start(s32[16]{0:T(128)} %copy-done.20) | copy-start | bytes 196
  118.1 14.2 %collective-permute-start.24 = (bf16[128,4096]{1,0:T(8,128)(2,1)S(1)}, bf16[128,4096]{1,0:T(8,128)(2,1)S(1)}, u32[]{:S(2)}, u32[]{:S(2)}) collective-permute-start(bf16[128,4096]{1,0:T(8,128)(2,1)S(1)} %get-tuple-element.25), channel_id=1, source_target_pairs={{0,16},{16,32},{32,48},{48,64},{64,80},{80,96},{96,112},{112,0},{1... | collective-permute-start | bytes 3145736 | tf_op jit(solution)/shard_map/ppermute | solution.py:337
  132.3 41.5 %collective-permute-start.30 = (f32[128,4096]{1,0:T(8,128)S(1)}, f32[128,4096]{1,0:T(8,128)S(1)}, u32[]{:S(2)}, u32[]{:S(2)}) collective-permute-start(f32[128,4096]{1,0:T(8,128)S(1)} %get-tuple-element.28), channel_id=1, source_target_pairs={{0,16},{16,32},{32,48},{48,64},{64,80},{80,96},{96,112},{112,0},{1... | collective-permute-start | bytes 6291464 | tf_op jit(solution)/shard_map/ppermute | solution.py:339
  136.9 9.6 %collective-permute-start.25 = (bf16[128,1024]{1,0:T(8,128)(2,1)S(1)}, bf16[128,1024]{1,0:T(8,128)(2,1)S(1)}, u32[]{:S(2)}, u32[]{:S(2)}) collective-permute-start(bf16[128,1024]{1,0:T(8,128)(2,1)S(1)} %projection.5.refs_0_), channel_id=1, source_target_pairs={{0,4},{1,5},{2,6},{3,7},{4,8},{5,9},{6,10},{7,11},{8,12},{9,13},{1... | collective-permute-start | bytes 786440 | tf_op jit(solution)/shard_map/ppermute | solution.py:37
  146.5 10.1 %collective-permute-start.26 = (bf16[128,1024]{1,0:T(8,128)(2,1)S(1)}, bf16[128,1024]{1,0:T(8,128)(2,1)S(1)}, u32[]{:S(2)}, u32[]{:S(2)}) collective-permute-start(bf16[128,1024]{1,0:T(8,128)(2,1)S(1)} %collective-permute-done.25.refs_1_), channel_id=1, source_target_pairs={{0,4},{1,5},{2,6},{3,7},{4,8},{5,9},{6,10},{7,11},{8,12},{9,13},{1... | collective-permute-start | bytes 786440 | tf_op jit(solution)/shard_map/ppermute | solution.py:37
  146.5 10.7 %collective-permute-start.33 = (bf16[128,1024]{1,0:T(8,128)(2,1)S(1)}, bf16[128,1024]{1,0:T(8,128)(2,1)S(1)}, u32[]{:S(2)}, u32[]{:S(2)}) collective-permute-start(bf16[128,1024]{1,0:T(8,128)(2,1)S(1)} %collective-permute-done.25.refs_1_), channel_id=1, source_target_pairs={{0,2},{1,3},{2,0},{3,1},{4,6},{5,7},{6,4},{7,5},{8,10},{9,11},{10,... | collective-permute-start | bytes 786440 | tf_op jit(solution)/shard_map/ppermute | solution.py:37
  146.9 12.9 %collective-permute-start.32 = (bf16[128,1024]{1,0:T(8,128)(2,1)S(1)}, bf16[128,1024]{1,0:T(8,128)(2,1)S(1)}, u32[]{:S(2)}, u32[]{:S(2)}) collective-permute-start(bf16[128,1024]{1,0:T(8,128)(2,1)S(1)} %collective-permute-done.25.refs_1_), channel_id=1, source_target_pairs={{0,3},{1,0},{2,1},{3,2},{4,7},{5,4},{6,5},{7,6},{8,11},{9,8},{10,9... | collective-permute-start | bytes 786440 | tf_op jit(solution)/shard_map/ppermute | solution.py:37
  148.2 14.5 %collective-permute-start.31 = (bf16[128,1024]{1,0:T(8,128)(2,1)S(1)}, bf16[128,1024]{1,0:T(8,128)(2,1)S(1)}, u32[]{:S(2)}, u32[]{:S(2)}) collective-permute-start(bf16[128,1024]{1,0:T(8,128)(2,1)S(1)} %collective-permute-done.25.refs_1_), channel_id=1, source_target_pairs={{0,1},{1,2},{2,3},{3,0},{4,5},{5,6},{6,7},{7,4},{8,9},{9,10},{10,1... | collective-permute-start | bytes 786440 | tf_op jit(solution)/shard_map/ppermute | solution.py:37
  156.7 13.0 %collective-permute-start.29 = (bf16[128,1024]{1,0:T(8,128)(2,1)S(1)}, bf16[128,1024]{1,0:T(8,128)(2,1)S(1)}, u32[]{:S(2)}, u32[]{:S(2)}) collective-permute-start(bf16[128,1024]{1,0:T(8,128)(2,1)S(1)} %get-tuple-element.35), channel_id=1, source_target_pairs={{0,2},{1,3},{2,0},{3,1},{4,6},{5,7},{6,4},{7,5},{8,10},{9,11},{10,... | collective-permute-start | bytes 786440 | tf_op jit(solution)/shard_map/ppermute | solution.py:37
  157.2 13.5 %collective-permute-start.28 = (bf16[128,1024]{1,0:T(8,128)(2,1)S(1)}, bf16[128,1024]{1,0:T(8,128)(2,1)S(1)}, u32[]{:S(2)}, u32[]{:S(2)}) collective-permute-start(bf16[128,1024]{1,0:T(8,128)(2,1)S(1)} %get-tuple-element.36), channel_id=1, source_target_pairs={{0,3},{1,0},{2,1},{3,2},{4,7},{5,4},{6,5},{7,6},{8,11},{9,8},{10,9... | collective-permute-start | bytes 786440 | tf_op jit(solution)/shard_map/ppermute | solution.py:37
  159.8 14.0 %collective-permute-start.27 = (bf16[128,1024]{1,0:T(8,128)(2,1)S(1)}, bf16[128,1024]{1,0:T(8,128)(2,1)S(1)}, u32[]{:S(2)}, u32[]{:S(2)}) collective-permute-start(bf16[128,1024]{1,0:T(8,128)(2,1)S(1)} %get-tuple-element.37), channel_id=1, source_target_pairs={{0,1},{1,2},{2,3},{3,0},{4,5},{5,6},{6,7},{7,4},{8,9},{9,10},{10,1... | collective-permute-start | bytes 786440 | tf_op jit(solution)/shard_map/ppermute | solution.py:37
  (12 other events, 31.8 us)
Sparse Core Ops, SparseCore 0:
  9.5 59.3 all-gather.2

commit v5 on v4

--- a/solution.py
+++ b/solution.py
@@ -165,7 +165,7 @@
     elif stage == "last":
         x, mix, sums, highs, _, produced = refs
     else:
-        x, mix, sums, highs, first, gain, produced, stream, normed, rows = refs
+        x, mix, sums, highs, first, gain, produced, stream, normed, rows, squares = refs
     g = pl.program_id(0)
     tokens = q.shape[0]
     column = lax.broadcasted_iota(jnp.int32, (tokens, tokens), 1)
@@ -186,6 +186,7 @@
     k = jnp.concatenate([block[:, :HEAD_SIZE] for block in blocks], axis=0)
     v = jnp.concatenate([block[:, HEAD_SIZE:] for block in blocks], axis=0)
     v = jnp.concatenate([v, jnp.ones_like(v)], axis=1)
+    squared = None
     for h in range(0, HEAD_GROUPS, TOGETHER):
         qs = [q[:, (h + j) * HEAD_SIZE : (h + j + 1) * HEAD_SIZE] for j in range(TOGETHER)]
         s = lax.dot_general(
@@ -224,16 +225,14 @@
                 stream[:, where] = new
                 at = pl.multiple_of(g * GROUP_WIDTH, GROUP_WIDTH) + (h + j) * HEAD_SIZE
                 rows[:, pl.ds(at, HEAD_SIZE)] = new
+                squared = new * new if squared is None else squared + new * new
     if stage != "onward":
         return
+    squares[...] = jnp.where(g == 0, squared, squares[...] + squared)
 
     @pl.when(g == KEY_VALUE_HEADS - 1)
     def _():
-        total = jnp.zeros((tokens, 128), jnp.float32)
-        for c in range(0, rows.shape[1], 128):
-            piece = rows[:, c : c + 128]
-            total = total + piece * piece
-        mean = jnp.sum(total, axis=1, keepdims=True) * (1.0 / rows.shape[1])
+        mean = jnp.sum(squares[...], axis=1, keepdims=True) * (1.0 / rows.shape[1])
         factor = lax.rsqrt(mean + EPSILON)
         for c in range(0, rows.shape[1], 128):
             at = slice(c, c + 128)
@@ -273,7 +272,7 @@
             jax.ShapeDtypeStruct((tokens, width), jnp.float32),
             jax.ShapeDtypeStruct((tokens, width), jnp.bfloat16),
         ]
-        scratch += [pltpu.VMEM((tokens, width), jnp.float32)]
+        scratch += [pltpu.VMEM((tokens, width), jnp.float32), pltpu.VMEM((tokens, HEAD_SIZE), jnp.float32)]
     return pl.pallas_call(
         functools.partial(attention_body, n_blocks, stage, tick),
         grid_spec=pltpu.PrefetchScalarGridSpec(

time: 188 us -> 188 us (level)
  no operation moved by 1% of the time
where the time goes in v5:
time: 188 us; the launch traced here: 186 us
  waiting for transfers between devices  86.4 us (46%)
  Pallas kernels  38.9 us (21%)
  starting transfers between devices  36.6 us (19%)
  between operations  14 us (7%)
  local copies, waits for them, and re-layouts  7.01 us (4%)
  other arithmetic  3.36 us (2%)
    ppermute x31, waiting for transfers between devices, moved(): return lax.ppermute(block, 'ctx', pairs)  65.6 us
    ppermute x31, starting transfers between devices, moved(): return lax.ppermute(block, 'ctx', pairs)  36.6 us
    pallas_call x4, Pallas kernels, attention(): pl.pallas_call(functools.partial(attention_body, n_blocks, stage, tick),...  26.9 us
    ppermute x1, waiting for transfers between devices, shards(): normed = lax.ppermute(normed, 'section', onward)  14.2 us
    pallas_call x3, Pallas kernels, projection(): pl.pallas_call(functools.partial(projection_body, n_keys, keys is not Non...  12.1 us
    all_gather x1, waiting for transfers between devices, shards(): value_weights = lax.all_gather(value_rows[0], 'ctx', axis=0, tiled=True)  5.86 us
    unnamed x50, local copies, waits for them, and re-layouts  5.51 us
  transfers between devices with their start and end apart: 35, of which 22 were waited for; matrix products, arithmetic and copies ran while one was open for 3% of the time, Pallas kernels for 12%

profile of v5, /device:TPU:2, one launch (start us, length us, event | category | flops | bytes accessed | tf_op | source)
XLA Modules:
  0.0 186.3 jit_solution(6807626892606494378)
XLA Ops:
  7.3 4.0 %collective-permute-start.5 = (bf16[256,512]{1,0:T(8,128)(2,1)}, bf16[256,512]{1,0:T(8,128)(2,1)}, u32[]{:S(2)}, u32[]{:S(2)}) collective-permute-start(bf16[256,512]{1,0:T(8,128)(2,1)} %bitcast.39), channel_id=1, source_target_pairs={{0,8},{1,9},{2,10},{3,11},{4,12},{5,13},{6,14},{7,15},{8,0},{9,1},... | collective-permute-start | bytes 786440 | tf_op jit(solution)/shard_map/ppermute | solution.py:37
  11.2 3.2 %collective-permute-start.4 = (bf16[256,512]{1,0:T(8,128)(2,1)}, bf16[256,512]{1,0:T(8,128)(2,1)}, u32[]{:S(2)}, u32[]{:S(2)}) collective-permute-start(bf16[256,512]{1,0:T(8,128)(2,1)} %bitcast.40), channel_id=1, source_target_pairs={{0,2},{1,3},{2,0},{3,1},{4,6},{5,7},{6,4},{7,5},{8,10},{9,11},{10,... | collective-permute-start | bytes 786440 | tf_op jit(solution)/shard_map/ppermute | solution.py:37
  14.4 1.1 collective-permute-start.3
  16.2 1.0 collective-permute-start.1
  17.2 1.8 multiply_reduce_fusion
  20.0 1.4 collective-permute-start
  21.4 0.9 collective-permute-done.4.refs_5_
  22.3 3.1 %collective-permute-start.13 = (bf16[256,512]{1,0:T(8,128)(2,1)}, bf16[256,512]{1,0:T(8,128)(2,1)}, u32[]{:S(2)}, u32[]{:S(2)}) collective-permute-start(bf16[256,512]{1,0:T(8,128)(2,1)} %collective-permute-done.5.refs_6_), channel_id=1, source_target_pairs={{0,3},{1,0},{2,1},{3,2},{4,7},{5,4},{6,5},{7,6},{8,11},{9,8},{10,9... | collective-permute-start | bytes 786440 | tf_op jit(solution)/shard_map/ppermute | solution.py:37
  25.3 4.8 %collective-permute-done.3.refs_4_ = bf16[256,512]{1,0:T(8,128)(2,1)} collective-permute-done((bf16[256,512]{1,0:T(8,128)(2,1)}, bf16[256,512]{1,0:T(8,128)(2,1)}, u32[]{:S(2)}, u32[]{:S(2)}) %collective-permute-start.3) | collective-permute-done | bytes 262176 | tf_op jit(solution)/shard_map/ppermute | solution.py:37
  30.3 1.9 %collective-permute-start.10 = (bf16[256,512]{1,0:T(8,128)(2,1)}, bf16[256,512]{1,0:T(8,128)(2,1)}, u32[]{:S(2)}, u32[]{:S(2)}) collective-permute-start(bf16[256,512]{1,0:T(8,128)(2,1)} %collective-permute-done.4.refs_5_), channel_id=1, source_target_pairs={{0,4},{1,5},{2,6},{3,7},{4,8},{5,9},{6,10},{7,11},{8,12},{9,13},{1... | collective-permute-start | bytes 786440 | tf_op jit(solution)/shard_map/ppermute | solution.py:37
  32.6 1.2 collective-permute-start.8
  33.8 2.8 %collective-permute-done.13.refs_14_ = bf16[256,512]{1,0:T(8,128)(2,1)} collective-permute-done((bf16[256,512]{1,0:T(8,128)(2,1)}, bf16[256,512]{1,0:T(8,128)(2,1)}, u32[]{:S(2)}, u32[]{:S(2)}) %collective-permute-start.13) | collective-permute-done | bytes 262176 | tf_op jit(solution)/shard_map/ppermute | solution.py:37
  36.6 2.6 %collective-permute-start.7 = (bf16[256,512]{1,0:T(8,128)(2,1)}, bf16[256,512]{1,0:T(8,128)(2,1)S(1)}, u32[]{:S(2)}, u32[]{:S(2)}) collective-permute-start(bf16[256,512]{1,0:T(8,128)(2,1)} %collective-permute-done.2.refs_3_), channel_id=1, source_target_pairs={{0,3},{1,0},{2,1},{3,2},{4,7},{5,4},{6,5},{7,6},{8,11},{9,8},{10,9... | collective-permute-start | bytes 786440 | tf_op jit(solution)/shard_map/ppermute | solution.py:37
  40.1 1.2 collective-permute-done.10.refs_11_
  42.0 1.1 dynamic-slice_bitcast_fusion.refs_7_
  43.1 3.7 %collective-permute-done.8.refs_9_ = bf16[256,512]{1,0:T(8,128)(2,1)S(1)} collective-permute-done((bf16[256,512]{1,0:T(8,128)(2,1)}, bf16[256,512]{1,0:T(8,128)(2,1)S(1)}, u32[]{:S(2)}, u32[]{:S(2)}) %collective-permute-start.8) | collective-permute-done | bytes 262176 | tf_op jit(solution)/shard_map/ppermute | solution.py:37
  46.8 2.1 %collective-permute-done.9.refs_10_ = bf16[256,512]{1,0:T(8,128)(2,1)S(1)} collective-permute-done((bf16[256,512]{1,0:T(8,128)(2,1)}, bf16[256,512]{1,0:T(8,128)(2,1)S(1)}, u32[]{:S(2)}, u32[]{:S(2)}) %collective-permute-start.9) | collective-permute-done | bytes 262176 | tf_op jit(solution)/shard_map/ppermute | solution.py:37
  48.9 2.3 %collective-permute-done.6.refs_7_ = bf16[256,512]{1,0:T(8,128)(2,1)S(1)} collective-permute-done((bf16[256,512]{1,0:T(8,128)(2,1)}, bf16[256,512]{1,0:T(8,128)(2,1)S(1)}, u32[]{:S(2)}, u32[]{:S(2)}) %collective-permute-start.6) | collective-permute-done | bytes 262176 | tf_op jit(solution)/shard_map/ppermute | solution.py:37
  51.2 4.5 %collective-permute-done.14.refs_15_ = bf16[256,512]{1,0:T(8,128)(2,1)S(1)} collective-permute-done((bf16[256,512]{1,0:T(8,128)(2,1)}, bf16[256,512]{1,0:T(8,128)(2,1)S(1)}, u32[]{:S(2)}, u32[]{:S(2)}) %collective-permute-start.14) | collective-permute-done | bytes 262176 | tf_op jit(solution)/shard_map/ppermute | solution.py:37
  55.8 3.0 %projection.3.refs_0_ = bf16[128,512]{1,0:T(8,128)(2,1)S(1)} custom-call(s32[16]{0:T(128)S(1)} %stack.85.order, bf16[128,4096]{1,0:T(8,128)(2,1)S(1)} %multiply_convert_fusion.rows.q, bf16[256,512]{1,0:T(8,128)(2,1)S(1)} %bitcast.45, bf16[256,512]{1,0:T(8,128)(2,1)} %collective-permute-done.refs_1_, bf16[256,512]{1,0:T(8,128)(2,1)} %collective-permute-done.1.refs_2_, ...), custom_call_target="tpu_custom_call" | custom-call | flops 536870912 | bytes 4194304 | tf_op jit(solution)/shard_map/projection/pallas_call | solution.py:145
  63.0 5.9 %all-gather.3.cloned.1.call-done = bf16[1,4096,512]{2,1,0:T(8,128)(2,1)} async-done(((bf16[1,256,512]{2,1,0:T(8,128)(2,1)}), bf16[1,4096,512]{2,1,0:T(8,128)(2,1)}) %all-gather.3.cloned.1.call-update) | async-done | bytes 4194320 | tf_op jit(solution)/shard_map/all_gather | solution.py:314
  68.9 4.5 %projection.4.refs_0_ = bf16[128,1024]{1,0:T(8,128)(2,1)} custom-call(s32[16]{0:T(128)} %copy-done.20, bf16[128,4096]{1,0:T(8,128)(2,1)} %copy-done.4, bf16[128,512]{1,0:T(8,128)(2,1)} %copy-done.19, bf16[4096,512]{1,0:T(8,128)(2,1)} %bitcast.37), custom_call_target="tpu_custom_call" | custom-call | flops 536870912 | bytes 4194304 | tf_op jit(solution)/shard_map/projection/pallas_call | solution.py:145
  73.8 9.5 %collective-permute-done.15.refs_1_ = bf16[128,1024]{1,0:T(8,128)(2,1)} collective-permute-done((bf16[128,1024]{1,0:T(8,128)(2,1)}, bf16[128,1024]{1,0:T(8,128)(2,1)}, u32[]{:S(2)}, u32[]{:S(2)}) %collective-permute-start.15) | collective-permute-done | bytes 262176 | tf_op jit(solution)/shard_map/ppermute | solution.py:37
  83.3 2.4 %collective-permute-start.22 = (bf16[128,1024]{1,0:T(8,128)(2,1)}, bf16[128,1024]{1,0:T(8,128)(2,1)}, u32[]{:S(2)}, u32[]{:S(2)}) collective-permute-start(bf16[128,1024]{1,0:T(8,128)(2,1)} %collective-permute-done.15.refs_1_), channel_id=1, source_target_pairs={{0,2},{1,3},{2,0},{3,1},{4,6},{5,7},{6,4},{7,5},{8,10},{9,11},{10,... | collective-permute-start | bytes 786440 | tf_op jit(solution)/shard_map/ppermute | solution.py:37
  86.4 1.3 collective-permute-start.20
  87.7 4.5 %collective-permute-done.16.refs_2_ = bf16[128,1024]{1,0:T(8,128)(2,1)} collective-permute-done((bf16[128,1024]{1,0:T(8,128)(2,1)}, bf16[128,1024]{1,0:T(8,128)(2,1)}, u32[]{:S(2)}, u32[]{:S(2)}) %collective-permute-start.16) | collective-permute-done | bytes 262176 | tf_op jit(solution)/shard_map/ppermute | solution.py:37
  92.2 1.1 broadcast_select_fusion.1
  93.3 2.5 %collective-permute-start.19 = (bf16[128,1024]{1,0:T(8,128)(2,1)S(1)}, bf16[128,1024]{1,0:T(8,128)(2,1)S(1)}, u32[]{:S(2)}, u32[]{:S(2)}) collective-permute-start(bf16[128,1024]{1,0:T(8,128)(2,1)S(1)} %get-tuple-element.38), channel_id=1, source_target_pairs={{0,2},{1,3},{2,0},{3,1},{4,6},{5,7},{6,4},{7,5},{8,10},{9,11},{10,... | collective-permute-start | bytes 786440 | tf_op jit(solution)/shard_map/ppermute | solution.py:37
  96.5 1.3 collective-permute-start.17
  97.8 1.2 collective-permute-done.21.refs_4_
  98.9 3.8 %collective-permute-done.20.refs_3_ = bf16[128,1024]{1,0:T(8,128)(2,1)S(1)} collective-permute-done((bf16[128,1024]{1,0:T(8,128)(2,1)}, bf16[128,1024]{1,0:T(8,128)(2,1)S(1)}, u32[]{:S(2)}, u32[]{:S(2)}) %collective-permute-start.20) | collective-permute-done | bytes 262176 | tf_op jit(solution)/shard_map/ppermute | solution.py:37
  102.7 0.9 copy-done.18
  103.7 7.7 %attention.4 = (f32[4096,128]{1,0:T(8,128)S(1)}, f32[4096,128]{1,0:T(8,128)S(1)}, f32[4096,128]{1,0:T(8,128)S(1)}) custom-call(s32[28]{0:T(128)S(1)} %concatenate.3.info, bf16[128,4096]{1,0:T(8,128)(2,1)S(1)} %copy-done.5, bf16[128,1024]{1,0:T(8,128)(2,1)S(1)} %copy-done.18, bf16[128,1024]{1,0:T(8,128)(2,1)} %collective-permute-done.15.refs_1_, ...), custom_call_target="tpu_custom_call" | custom-call | flops 1610612736 | bytes 7864320 | tf_op jit(solution)/shard_map/attention/pallas_call | solution.py:276
  111.5 6.7 %attention.5 = (bf16[2,128,4096]{2,1,0:T(8,128)(2,1)}, f32[128,4096]{1,0:T(8,128)S(1)}, bf16[128,4096]{1,0:T(8,128)(2,1)S(1)}) custom-call(s32[28]{0:T(128)S(1)} %concatenate.3.info, bf16[128,4096]{1,0:T(8,128)(2,1)S(1)} %copy-done.5, bf16[128,1024]{1,0:T(8,128)(2,1)S(1)} %collective-permute-done.17.refs_0_, ...), custom_call_target="tpu_custom_call" | custom-call | flops 805306368 | bytes 7077888 | tf_op jit(solution)/shard_map/attention/pallas_call | solution.py:276
  118.2 14.2 %collective-permute-done.24.rows.q = bf16[128,4096]{1,0:T(8,128)(2,1)S(1)} collective-permute-done((bf16[128,4096]{1,0:T(8,128)(2,1)S(1)}, bf16[128,4096]{1,0:T(8,128)(2,1)S(1)}, u32[]{:S(2)}, u32[]{:S(2)}) %collective-permute-start.24) | collective-permute-done | bytes 1048608 | tf_op jit(solution)/shard_map/ppermute | solution.py:336
  132.5 4.5 %projection.5.refs_0_ = bf16[128,1024]{1,0:T(8,128)(2,1)S(1)} custom-call(s32[16]{0:T(128)S(1)} %copy-done.21, bf16[128,4096]{1,0:T(8,128)(2,1)S(1)} %collective-permute-done.24.rows.q, bf16[256,512]{1,0:T(8,128)(2,1)S(1)} %bitcast.46, bf16[256,512]{1,0:T(8,128)(2,1)} %collective-permute-done.refs_1_, bf16[256,512]{1,0:T(8,128)(2,1)} %collective-permute-done.1.refs_2_, ...), custom_call_target="tpu_custom_call" | custom-call | flops 1073741824 | bytes 8388608 | tf_op jit(solution)/shard_map/projection/pallas_call | solution.py:145
  137.1 9.5 %collective-permute-done.25.refs_1_ = bf16[128,1024]{1,0:T(8,128)(2,1)S(1)} collective-permute-done((bf16[128,1024]{1,0:T(8,128)(2,1)S(1)}, bf16[128,1024]{1,0:T(8,128)(2,1)S(1)}, u32[]{:S(2)}, u32[]{:S(2)}) %collective-permute-start.25) | collective-permute-done | bytes 262176 | tf_op jit(solution)/shard_map/ppermute | solution.py:37
  147.1 1.3 collective-permute-start.32
  148.3 0.8 collective-permute-start.31
  149.1 7.6 %collective-permute-done.26.refs_2_ = bf16[128,1024]{1,0:T(8,128)(2,1)S(1)} collective-permute-done((bf16[128,1024]{1,0:T(8,128)(2,1)S(1)}, bf16[128,1024]{1,0:T(8,128)(2,1)S(1)}, u32[]{:S(2)}, u32[]{:S(2)}) %collective-permute-start.26) | collective-permute-done | bytes 262176 | tf_op jit(solution)/shard_map/ppermute | solution.py:37
  157.3 1.0 collective-permute-start.28
  158.3 1.6 collective-permute-done.32.refs_4_
  160.0 1.9 %collective-permute-start.27 = (bf16[128,1024]{1,0:T(8,128)(2,1)S(1)}, bf16[128,1024]{1,0:T(8,128)(2,1)S(1)}, u32[]{:S(2)}, u32[]{:S(2)}) collective-permute-start(bf16[128,1024]{1,0:T(8,128)(2,1)S(1)} %get-tuple-element.37), channel_id=1, source_target_pairs={{0,1},{1,2},{2,3},{3,0},{4,5},{5,6},{6,7},{7,4},{8,9},{9,10},{10,1... | collective-permute-start | bytes 786440 | tf_op jit(solution)/shard_map/ppermute | solution.py:37
  161.9 1.0 collective-permute-done.31.refs_3_
  162.9 7.0 %attention.6 = (f32[4096,128]{1,0:T(8,128)S(1)}, f32[4096,128]{1,0:T(8,128)S(1)}, f32[4096,128]{1,0:T(8,128)S(1)}) custom-call(s32[28]{0:T(128)S(1)} %concatenate.3.info, bf16[128,4096]{1,0:T(8,128)(2,1)S(1)} %collective-permute-done.24.rows.q, bf16[128,1024]{1,0:T(8,128)(2,1)S(1)} %projection.5.refs_0_, ...), custom_call_target="tpu_custom_call" | custom-call | flops 1610612736 | bytes 7864320 | tf_op jit(solution)/shard_map/attention/pallas_call | solution.py:276
  169.9 0.9 collective-permute-done.28.refs_1_
  170.8 3.1 %collective-permute-done.27.refs_0_ = bf16[128,1024]{1,0:T(8,128)(2,1)S(1)} collective-permute-done((bf16[128,1024]{1,0:T(8,128)(2,1)S(1)}, bf16[128,1024]{1,0:T(8,128)(2,1)S(1)}, u32[]{:S(2)}, u32[]{:S(2)}) %collective-permute-start.27) | collective-permute-done | bytes 262176 | tf_op jit(solution)/shard_map/ppermute | solution.py:37
  173.9 5.5 %attention.7 = bf16[2,128,4096]{2,1,0:T(8,128)(2,1)} custom-call(s32[28]{0:T(128)S(1)} %concatenate.3.info, bf16[128,4096]{1,0:T(8,128)(2,1)S(1)} %collective-permute-done.24.rows.q, bf16[128,1024]{1,0:T(8,128)(2,1)S(1)} %collective-permute-done.27.refs_0_, bf16[128,1024]{1,0:T(8,128)(2,1)S(1)} %collective-permute-done.28.refs_1_, ...), custom_call_target="tpu_custom_call", output_to_operand_aliasing={{}: (9, {})} | custom-call | flops 805306368 | bytes 7077888 | tf_op jit(solution)/shard_map/attention/pallas_call | solution.py:276
  (92 shorter events, 11.4 us)
Async XLA Ops:
  6.5 35.4 %copy-start = (bf16[2,128,4096]{2,1,0:T(8,128)(2,1)S(1)}, bf16[2,128,4096]{2,1,0:T(8,128)(2,1)}, u32[]{:S(2)}) copy-start(bf16[2,128,4096]{2,1,0:T(8,128)(2,1)} %param.8) | copy-start | bytes 6291460
  6.5 62.3 %all-gather.3.cloned.1.call-start = ((), (), s32[]{:S(2)}) async-start(), calls=%async_computation | async-start | bytes 4456448 | tf_op jit(solution)/shard_map/all_gather | solution.py:314
  7.3 12.7 %collective-permute-start.5 = (bf16[256,512]{1,0:T(8,128)(2,1)}, bf16[256,512]{1,0:T(8,128)(2,1)}, u32[]{:S(2)}, u32[]{:S(2)}) collective-permute-start(bf16[256,512]{1,0:T(8,128)(2,1)} %bitcast.39), channel_id=1, source_target_pairs={{0,8},{1,9},{2,10},{3,11},{4,12},{5,13},{6,14},{7,15},{8,0},{9,1},... | collective-permute-start | bytes 786440 | tf_op jit(solution)/shard_map/ppermute | solution.py:37
  11.2 11.1 %collective-permute-start.4 = (bf16[256,512]{1,0:T(8,128)(2,1)}, bf16[256,512]{1,0:T(8,128)(2,1)}, u32[]{:S(2)}, u32[]{:S(2)}) collective-permute-start(bf16[256,512]{1,0:T(8,128)(2,1)} %bitcast.40), channel_id=1, source_target_pairs={{0,2},{1,3},{2,0},{3,1},{4,6},{5,7},{6,4},{7,5},{8,10},{9,11},{10,... | collective-permute-start | bytes 786440 | tf_op jit(solution)/shard_map/ppermute | solution.py:37
  14.4 15.7 %collective-permute-start.3 = (bf16[256,512]{1,0:T(8,128)(2,1)}, bf16[256,512]{1,0:T(8,128)(2,1)}, u32[]{:S(2)}, u32[]{:S(2)}) collective-permute-start(bf16[256,512]{1,0:T(8,128)(2,1)} %bitcast.41), channel_id=1, source_target_pairs={{0,3},{1,0},{2,1},{3,2},{4,7},{5,4},{6,5},{7,6},{8,11},{9,8},{10,9... | collective-permute-start | bytes 786440 | tf_op jit(solution)/shard_map/ppermute | solution.py:37
  15.5 14.7 %collective-permute-start.2 = (bf16[256,512]{1,0:T(8,128)(2,1)}, bf16[256,512]{1,0:T(8,128)(2,1)}, u32[]{:S(2)}, u32[]{:S(2)}) collective-permute-start(bf16[256,512]{1,0:T(8,128)(2,1)} %bitcast.42), channel_id=1, source_target_pairs={{0,12},{1,13},{2,14},{3,15},{4,0},{5,1},{6,2},{7,3},{8,4},{9,5},{1... | collective-permute-start | bytes 786440 | tf_op jit(solution)/shard_map/ppermute | solution.py:37
  16.2 14.1 %collective-permute-start.1 = (bf16[256,512]{1,0:T(8,128)(2,1)}, bf16[256,512]{1,0:T(8,128)(2,1)}, u32[]{:S(2)}, u32[]{:S(2)}) collective-permute-start(bf16[256,512]{1,0:T(8,128)(2,1)} %bitcast.43), channel_id=1, source_target_pairs={{0,1},{1,2},{2,3},{3,0},{4,5},{5,6},{6,7},{7,4},{8,9},{9,10},{10,1... | collective-permute-start | bytes 786440 | tf_op jit(solution)/shard_map/ppermute | solution.py:37
  19.3 39.5 %copy-start.4 = (bf16[128,4096]{1,0:T(8,128)(2,1)}, bf16[128,4096]{1,0:T(8,128)(2,1)S(1)}, u32[]{:S(2)}) copy-start(bf16[128,4096]{1,0:T(8,128)(2,1)S(1)} %multiply_convert_fusion.rows.q) | copy-start | bytes 3145732
  20.0 12.5 %collective-permute-start = (bf16[256,512]{1,0:T(8,128)(2,1)S(1)}, bf16[256,512]{1,0:T(8,128)(2,1)}, u32[]{:S(2)}, u32[]{:S(2)}) collective-permute-start(bf16[256,512]{1,0:T(8,128)(2,1)S(1)} %bitcast.44), channel_id=1, source_target_pairs={{0,4},{1,5},{2,6},{3,7},{4,8},{5,9},{6,10},{7,11},{8,12},{9,13},{1... | collective-permute-start | bytes 786440 | tf_op jit(solution)/shard_map/ppermute | solution.py:37
  22.3 14.4 %collective-permute-start.13 = (bf16[256,512]{1,0:T(8,128)(2,1)}, bf16[256,512]{1,0:T(8,128)(2,1)}, u32[]{:S(2)}, u32[]{:S(2)}) collective-permute-start(bf16[256,512]{1,0:T(8,128)(2,1)} %collective-permute-done.5.refs_6_), channel_id=1, source_target_pairs={{0,3},{1,0},{2,1},{3,2},{4,7},{5,4},{6,5},{7,6},{8,11},{9,8},{10,9... | collective-permute-start | bytes 786440 | tf_op jit(solution)/shard_map/ppermute | solution.py:37
  30.2 9.3 %collective-permute-start.12 = (bf16[256,512]{1,0:T(8,128)(2,1)}, bf16[256,512]{1,0:T(8,128)(2,1)}, u32[]{:S(2)}, u32[]{:S(2)}) collective-permute-start(bf16[256,512]{1,0:T(8,128)(2,1)} %collective-permute-done.5.refs_6_), channel_id=1, source_target_pairs={{0,1},{1,2},{2,3},{3,0},{4,5},{5,6},{6,7},{7,4},{8,9},{9,10},{10,1... | collective-permute-start | bytes 786440 | tf_op jit(solution)/shard_map/ppermute | solution.py:37
  30.2 9.8 %collective-permute-start.11 = (bf16[256,512]{1,0:T(8,128)(2,1)}, bf16[256,512]{1,0:T(8,128)(2,1)}, u32[]{:S(2)}, u32[]{:S(2)}) collective-permute-start(bf16[256,512]{1,0:T(8,128)(2,1)} %collective-permute-done.4.refs_5_), channel_id=1, source_target_pairs={{0,12},{1,13},{2,14},{3,15},{4,0},{5,1},{6,2},{7,3},{8,4},{9,5},{1... | collective-permute-start | bytes 786440 | tf_op jit(solution)/shard_map/ppermute | solution.py:37
  30.3 11.0 %collective-permute-start.10 = (bf16[256,512]{1,0:T(8,128)(2,1)}, bf16[256,512]{1,0:T(8,128)(2,1)}, u32[]{:S(2)}, u32[]{:S(2)}) collective-permute-start(bf16[256,512]{1,0:T(8,128)(2,1)} %collective-permute-done.4.refs_5_), channel_id=1, source_target_pairs={{0,4},{1,5},{2,6},{3,7},{4,8},{5,9},{6,10},{7,11},{8,12},{9,13},{1... | collective-permute-start | bytes 786440 | tf_op jit(solution)/shard_map/ppermute | solution.py:37
  32.5 26.3 %copy-start.20 = (s32[16]{0:T(128)}, s32[16]{0:T(128)S(1)}, u32[]{:S(2)}) copy-start(s32[16]{0:T(128)S(1)} %stack.85.order) | copy-start | bytes 196
  32.6 14.2 %collective-permute-start.8 = (bf16[256,512]{1,0:T(8,128)(2,1)}, bf16[256,512]{1,0:T(8,128)(2,1)S(1)}, u32[]{:S(2)}, u32[]{:S(2)}) collective-permute-start(bf16[256,512]{1,0:T(8,128)(2,1)} %collective-permute-done.3.refs_4_), channel_id=1, source_target_pairs={{0,4},{1,5},{2,6},{3,7},{4,8},{5,9},{6,10},{7,11},{8,12},{9,13},{1... | collective-permute-start | bytes 786440 | tf_op jit(solution)/shard_map/ppermute | solution.py:37
  36.6 10.1 %collective-permute-start.7 = (bf16[256,512]{1,0:T(8,128)(2,1)}, bf16[256,512]{1,0:T(8,128)(2,1)S(1)}, u32[]{:S(2)}, u32[]{:S(2)}) collective-permute-start(bf16[256,512]{1,0:T(8,128)(2,1)} %collective-permute-done.2.refs_3_), channel_id=1, source_target_pairs={{0,3},{1,0},{2,1},{3,2},{4,7},{5,4},{6,5},{7,6},{8,11},{9,8},{10,9... | collective-permute-start | bytes 786440 | tf_op jit(solution)/shard_map/ppermute | solution.py:37
  39.5 9.4 %collective-permute-start.9 = (bf16[256,512]{1,0:T(8,128)(2,1)}, bf16[256,512]{1,0:T(8,128)(2,1)S(1)}, u32[]{:S(2)}, u32[]{:S(2)}) collective-permute-start(bf16[256,512]{1,0:T(8,128)(2,1)} %collective-permute-done.1.refs_2_), channel_id=1, source_target_pairs={{0,12},{1,13},{2,14},{3,15},{4,0},{5,1},{6,2},{7,3},{8,4},{9,5},{1... | collective-permute-start | bytes 786440 | tf_op jit(solution)/shard_map/ppermute | solution.py:37
  40.0 11.2 %collective-permute-start.6 = (bf16[256,512]{1,0:T(8,128)(2,1)}, bf16[256,512]{1,0:T(8,128)(2,1)S(1)}, u32[]{:S(2)}, u32[]{:S(2)}) collective-permute-start(bf16[256,512]{1,0:T(8,128)(2,1)} %collective-permute-done.refs_1_), channel_id=1, source_target_pairs={{0,1},{1,2},{2,3},{3,0},{4,5},{5,6},{6,7},{7,4},{8,9},{9,10},{10,1... | collective-permute-start | bytes 786440 | tf_op jit(solution)/shard_map/ppermute | solution.py:37
  41.3 14.5 %collective-permute-start.14 = (bf16[256,512]{1,0:T(8,128)(2,1)}, bf16[256,512]{1,0:T(8,128)(2,1)S(1)}, u32[]{:S(2)}, u32[]{:S(2)}) collective-permute-start(bf16[256,512]{1,0:T(8,128)(2,1)} %collective-permute-done.10.refs_11_), channel_id=1, source_target_pairs={{0,4},{1,5},{2,6},{3,7},{4,8},{5,9},{6,10},{7,11},{8,12},{9,13},{1... | collective-permute-start | bytes 786440 | tf_op jit(solution)/shard_map/ppermute | solution.py:37
  68.9 33.8 %copy-start.5 = (bf16[128,4096]{1,0:T(8,128)(2,1)S(1)}, bf16[128,4096]{1,0:T(8,128)(2,1)}, u32[]{:S(2)}) copy-start(bf16[128,4096]{1,0:T(8,128)(2,1)} %copy-done.4) | copy-start | bytes 3145732
  73.4 9.9 %collective-permute-start.15 = (bf16[128,1024]{1,0:T(8,128)(2,1)}, bf16[128,1024]{1,0:T(8,128)(2,1)}, u32[]{:S(2)}, u32[]{:S(2)}) collective-permute-start(bf16[128,1024]{1,0:T(8,128)(2,1)} %projection.4.refs_0_), channel_id=1, source_target_pairs={{0,4},{1,5},{2,6},{3,7},{4,8},{5,9},{6,10},{7,11},{8,12},{9,13},{1... | collective-permute-start | bytes 786440 | tf_op jit(solution)/shard_map/ppermute | solution.py:37
  83.3 8.9 %collective-permute-start.16 = (bf16[128,1024]{1,0:T(8,128)(2,1)}, bf16[128,1024]{1,0:T(8,128)(2,1)}, u32[]{:S(2)}, u32[]{:S(2)}) collective-permute-start(bf16[128,1024]{1,0:T(8,128)(2,1)} %collective-permute-done.15.refs_1_), channel_id=1, source_target_pairs={{0,4},{1,5},{2,6},{3,7},{4,8},{5,9},{6,10},{7,11},{8,12},{9,13},{1... | collective-permute-start | bytes 786440 | tf_op jit(solution)/shard_map/ppermute | solution.py:37
  83.3 13.2 %collective-permute-start.22 = (bf16[128,1024]{1,0:T(8,128)(2,1)}, bf16[128,1024]{1,0:T(8,128)(2,1)}, u32[]{:S(2)}, u32[]{:S(2)}) collective-permute-start(bf16[128,1024]{1,0:T(8,128)(2,1)} %collective-permute-done.15.refs_1_), channel_id=1, source_target_pairs={{0,2},{1,3},{2,0},{3,1},{4,6},{5,7},{6,4},{7,5},{8,10},{9,11},{10,... | collective-permute-start | bytes 786440 | tf_op jit(solution)/shard_map/ppermute | solution.py:37
  85.7 13.3 %collective-permute-start.21 = (bf16[128,1024]{1,0:T(8,128)(2,1)}, bf16[128,1024]{1,0:T(8,128)(2,1)S(1)}, u32[]{:S(2)}, u32[]{:S(2)}) collective-permute-start(bf16[128,1024]{1,0:T(8,128)(2,1)} %collective-permute-done.15.refs_1_), channel_id=1, source_target_pairs={{0,3},{1,0},{2,1},{3,2},{4,7},{5,4},{6,5},{7,6},{8,11},{9,8},{10,9... | collective-permute-start | bytes 786440 | tf_op jit(solution)/shard_map/ppermute | solution.py:37
  86.4 16.3 %collective-permute-start.20 = (bf16[128,1024]{1,0:T(8,128)(2,1)}, bf16[128,1024]{1,0:T(8,128)(2,1)S(1)}, u32[]{:S(2)}, u32[]{:S(2)}) collective-permute-start(bf16[128,1024]{1,0:T(8,128)(2,1)} %collective-permute-done.15.refs_1_), channel_id=1, source_target_pairs={{0,1},{1,2},{2,3},{3,0},{4,5},{5,6},{6,7},{7,4},{8,9},{9,10},{10,1... | collective-permute-start | bytes 786440 | tf_op jit(solution)/shard_map/ppermute | solution.py:37
  93.3 18.1 %collective-permute-start.19 = (bf16[128,1024]{1,0:T(8,128)(2,1)S(1)}, bf16[128,1024]{1,0:T(8,128)(2,1)S(1)}, u32[]{:S(2)}, u32[]{:S(2)}) collective-permute-start(bf16[128,1024]{1,0:T(8,128)(2,1)S(1)} %get-tuple-element.38), channel_id=1, source_target_pairs={{0,2},{1,3},{2,0},{3,1},{4,6},{5,7},{6,4},{7,5},{8,10},{9,11},{10,... | collective-permute-start | bytes 786440 | tf_op jit(solution)/shard_map/ppermute | solution.py:37
  95.7 15.7 %collective-permute-start.18 = (bf16[128,1024]{1,0:T(8,128)(2,1)S(1)}, bf16[128,1024]{1,0:T(8,128)(2,1)S(1)}, u32[]{:S(2)}, u32[]{:S(2)}) collective-permute-start(bf16[128,1024]{1,0:T(8,128)(2,1)S(1)} %get-tuple-element.39), channel_id=1, source_target_pairs={{0,3},{1,0},{2,1},{3,2},{4,7},{5,4},{6,5},{7,6},{8,11},{9,8},{10,9... | collective-permute-start | bytes 786440 | tf_op jit(solution)/shard_map/ppermute | solution.py:37
  96.5 15.0 %copy-start.2 = (f32[1,128,4096]{2,1,0:T(8,128)S(1)}, f32[1,128,4096]{2,1,0:T(8,128)}, u32[]{:S(2)}) copy-start(f32[1,128,4096]{2,1,0:T(8,128)} %param.7) | copy-start | bytes 6291460
  96.5 15.0 %copy-start.6 = (bf16[128,4096]{1,0:T(8,128)(2,1)S(1)}, bf16[128,4096]{1,0:T(8,128)(2,1)}, u32[]{:S(2)}) copy-start(bf16[128,4096]{1,0:T(8,128)(2,1)} %dynamic-slice_bitcast_fusion.refs_7_) | copy-start | bytes 3145732
  96.5 14.9 %collective-permute-start.17 = (bf16[128,1024]{1,0:T(8,128)(2,1)S(1)}, bf16[128,1024]{1,0:T(8,128)(2,1)S(1)}, u32[]{:S(2)}, u32[]{:S(2)}) collective-permute-start(bf16[128,1024]{1,0:T(8,128)(2,1)S(1)} %get-tuple-element.40), channel_id=1, source_target_pairs={{0,1},{1,2},{2,3},{3,0},{4,5},{5,6},{6,7},{7,4},{8,9},{9,10},{10,1... | collective-permute-start | bytes 786440 | tf_op jit(solution)/shard_map/ppermute | solution.py:37
  98.9 12.5 %collective-permute-start.23 = (f32[1,4096]{1,0:T(1,128)S(1)}, f32[1,4096]{1,0:T(1,128)S(1)}, u32[]{:S(2)}, u32[]{:S(2)}) collective-permute-start(f32[1,4096]{1,0:T(1,128)S(1)} %copy-done.22), channel_id=1, source_target_pairs={{16,0},{32,16},{48,32},{64,48},{80,64},{96,80},{112,96},{0,112},{1... | collective-permute-start | bytes 49160 | tf_op jit(solution)/shard_map/ppermute | solution.py:317
  111.5 21.0 %copy-start.3 = (bf16[1,4096,512]{2,1,0:T(8,128)(2,1)S(1)}, bf16[1,4096,512]{2,1,0:T(8,128)(2,1)}, u32[]{:S(2)}) copy-start(bf16[1,4096,512]{2,1,0:T(8,128)(2,1)} %all-gather.3.cloned.1.call-done) | copy-start | bytes 12582916
  111.5 21.0 %copy-start.9 = (bf16[256,512]{1,0:T(8,128)(2,1)S(1)}, bf16[256,512]{1,0:T(8,128)(2,1)}, u32[]{:S(2)}) copy-start(bf16[256,512]{1,0:T(8,128)(2,1)} %copy-done.8) | copy-start | bytes 786436
  111.5 21.0 %copy-start.11 = (bf16[256,512]{1,0:T(8,128)(2,1)S(1)}, bf16[256,512]{1,0:T(8,128)(2,1)}, u32[]{:S(2)}) copy-start(bf16[256,512]{1,0:T(8,128)(2,1)} %copy-done.10) | copy-start | bytes 786436
  111.5 21.0 %copy-start.13 = (bf16[256,512]{1,0:T(8,128)(2,1)S(1)}, bf16[256,512]{1,0:T(8,128)(2,1)}, u32[]{:S(2)}) copy-start(bf16[256,512]{1,0:T(8,128)(2,1)} %copy-done.12) | copy-start | bytes 786436
  111.5 21.0 %copy-start.15 = (bf16[256,512]{1,0:T(8,128)(2,1)S(1)}, bf16[256,512]{1,0:T(8,128)(2,1)}, u32[]{:S(2)}) copy-start(bf16[256,512]{1,0:T(8,128)(2,1)} %copy-done.14) | copy-start | bytes 786436
  111.5 21.0 %copy-start.17 = (bf16[256,512]{1,0:T(8,128)(2,1)S(1)}, bf16[256,512]{1,0:T(8,128)(2,1)}, u32[]{:S(2)}) copy-start(bf16[256,512]{1,0:T(8,128)(2,1)} %copy-done.16) | copy-start | bytes 786436
  111.5 21.0 %copy-start.21 = (s32[16]{0:T(128)S(1)}, s32[16]{0:T(128)}, u32[]{:S(2)}) copy-start(s32[16]{0:T(128)} %copy-done.20) | copy-start | bytes 196
  118.2 14.2 %collective-permute-start.24 = (bf16[128,4096]{1,0:T(8,128)(2,1)S(1)}, bf16[128,4096]{1,0:T(8,128)(2,1)S(1)}, u32[]{:S(2)}, u32[]{:S(2)}) collective-permute-start(bf16[128,4096]{1,0:T(8,128)(2,1)S(1)} %get-tuple-element.25), channel_id=1, source_target_pairs={{0,16},{16,32},{32,48},{48,64},{64,80},{80,96},{96,112},{112,0},{1... | collective-permute-start | bytes 3145736 | tf_op jit(solution)/shard_map/ppermute | solution.py:336
  132.4 41.5 %collective-permute-start.30 = (f32[128,4096]{1,0:T(8,128)S(1)}, f32[128,4096]{1,0:T(8,128)S(1)}, u32[]{:S(2)}, u32[]{:S(2)}) collective-permute-start(f32[128,4096]{1,0:T(8,128)S(1)} %get-tuple-element.28), channel_id=1, source_target_pairs={{0,16},{16,32},{32,48},{48,64},{64,80},{80,96},{96,112},{112,0},{1... | collective-permute-start | bytes 6291464 | tf_op jit(solution)/shard_map/ppermute | solution.py:338
  137.0 9.6 %collective-permute-start.25 = (bf16[128,1024]{1,0:T(8,128)(2,1)S(1)}, bf16[128,1024]{1,0:T(8,128)(2,1)S(1)}, u32[]{:S(2)}, u32[]{:S(2)}) collective-permute-start(bf16[128,1024]{1,0:T(8,128)(2,1)S(1)} %projection.5.refs_0_), channel_id=1, source_target_pairs={{0,4},{1,5},{2,6},{3,7},{4,8},{5,9},{6,10},{7,11},{8,12},{9,13},{1... | collective-permute-start | bytes 786440 | tf_op jit(solution)/shard_map/ppermute | solution.py:37
  146.6 10.1 %collective-permute-start.26 = (bf16[128,1024]{1,0:T(8,128)(2,1)S(1)}, bf16[128,1024]{1,0:T(8,128)(2,1)S(1)}, u32[]{:S(2)}, u32[]{:S(2)}) collective-permute-start(bf16[128,1024]{1,0:T(8,128)(2,1)S(1)} %collective-permute-done.25.refs_1_), channel_id=1, source_target_pairs={{0,4},{1,5},{2,6},{3,7},{4,8},{5,9},{6,10},{7,11},{8,12},{9,13},{1... | collective-permute-start | bytes 786440 | tf_op jit(solution)/shard_map/ppermute | solution.py:37
  146.6 10.7 %collective-permute-start.33 = (bf16[128,1024]{1,0:T(8,128)(2,1)S(1)}, bf16[128,1024]{1,0:T(8,128)(2,1)S(1)}, u32[]{:S(2)}, u32[]{:S(2)}) collective-permute-start(bf16[128,1024]{1,0:T(8,128)(2,1)S(1)} %collective-permute-done.25.refs_1_), channel_id=1, source_target_pairs={{0,2},{1,3},{2,0},{3,1},{4,6},{5,7},{6,4},{7,5},{8,10},{9,11},{10,... | collective-permute-start | bytes 786440 | tf_op jit(solution)/shard_map/ppermute | solution.py:37
  147.1 12.9 %collective-permute-start.32 = (bf16[128,1024]{1,0:T(8,128)(2,1)S(1)}, bf16[128,1024]{1,0:T(8,128)(2,1)S(1)}, u32[]{:S(2)}, u32[]{:S(2)}) collective-permute-start(bf16[128,1024]{1,0:T(8,128)(2,1)S(1)} %collective-permute-done.25.refs_1_), channel_id=1, source_target_pairs={{0,3},{1,0},{2,1},{3,2},{4,7},{5,4},{6,5},{7,6},{8,11},{9,8},{10,9... | collective-permute-start | bytes 786440 | tf_op jit(solution)/shard_map/ppermute | solution.py:37
  148.3 14.5 %collective-permute-start.31 = (bf16[128,1024]{1,0:T(8,128)(2,1)S(1)}, bf16[128,1024]{1,0:T(8,128)(2,1)S(1)}, u32[]{:S(2)}, u32[]{:S(2)}) collective-permute-start(bf16[128,1024]{1,0:T(8,128)(2,1)S(1)} %collective-permute-done.25.refs_1_), channel_id=1, source_target_pairs={{0,1},{1,2},{2,3},{3,0},{4,5},{5,6},{6,7},{7,4},{8,9},{9,10},{10,1... | collective-permute-start | bytes 786440 | tf_op jit(solution)/shard_map/ppermute | solution.py:37
  156.8 13.0 %collective-permute-start.29 = (bf16[128,1024]{1,0:T(8,128)(2,1)S(1)}, bf16[128,1024]{1,0:T(8,128)(2,1)S(1)}, u32[]{:S(2)}, u32[]{:S(2)}) collective-permute-start(bf16[128,1024]{1,0:T(8,128)(2,1)S(1)} %get-tuple-element.35), channel_id=1, source_target_pairs={{0,2},{1,3},{2,0},{3,1},{4,6},{5,7},{6,4},{7,5},{8,10},{9,11},{10,... | collective-permute-start | bytes 786440 | tf_op jit(solution)/shard_map/ppermute | solution.py:37
  157.3 13.5 %collective-permute-start.28 = (bf16[128,1024]{1,0:T(8,128)(2,1)S(1)}, bf16[128,1024]{1,0:T(8,128)(2,1)S(1)}, u32[]{:S(2)}, u32[]{:S(2)}) collective-permute-start(bf16[128,1024]{1,0:T(8,128)(2,1)S(1)} %get-tuple-element.36), channel_id=1, source_target_pairs={{0,3},{1,0},{2,1},{3,2},{4,7},{5,4},{6,5},{7,6},{8,11},{9,8},{10,9... | collective-permute-start | bytes 786440 | tf_op jit(solution)/shard_map/ppermute | solution.py:37
  160.0 14.0 %collective-permute-start.27 = (bf16[128,1024]{1,0:T(8,128)(2,1)S(1)}, bf16[128,1024]{1,0:T(8,128)(2,1)S(1)}, u32[]{:S(2)}, u32[]{:S(2)}) collective-permute-start(bf16[128,1024]{1,0:T(8,128)(2,1)S(1)} %get-tuple-element.37), channel_id=1, source_target_pairs={{0,1},{1,2},{2,3},{3,0},{4,5},{5,6},{6,7},{7,4},{8,9},{9,10},{10,1... | collective-permute-start | bytes 786440 | tf_op jit(solution)/shard_map/ppermute | solution.py:37
  (12 other events, 31.8 us)
Sparse Core Ops, SparseCore 0:
  9.5 59.3 all-gather.2

commit v6 on v5

--- a/solution.py
+++ b/solution.py
@@ -23,6 +23,7 @@
 PLACES = 9
 INFO = PLACES + W * (1 + DOCUMENTS) + 1
 TOGETHER = 4
+FIRST_TOGETHER = 2
 DEPTH = 256
 SCALE = HEAD_SIZE ** (-0.5)
 LOG2E = 1.4426950408889634
@@ -166,6 +167,7 @@
         x, mix, sums, highs, _, produced = refs
     else:
         x, mix, sums, highs, first, gain, produced, stream, normed, rows, squares = refs
+    together = FIRST_TOGETHER if stage == "first" else TOGETHER
     g = pl.program_id(0)
     tokens = q.shape[0]
     column = lax.broadcasted_iota(jnp.int32, (tokens, tokens), 1)
@@ -182,13 +184,13 @@
             allowed = allowed & (column <= row)
         bias.append(jnp.where(allowed, 0.0, MASK_FLOOR))
     bias = jnp.concatenate(bias, axis=1)
-    bias = jnp.concatenate([bias] * TOGETHER, axis=0)
+    bias = jnp.concatenate([bias] * together, axis=0)
     k = jnp.concatenate([block[:, :HEAD_SIZE] for block in blocks], axis=0)
     v = jnp.concatenate([block[:, HEAD_SIZE:] for block in blocks], axis=0)
     v = jnp.concatenate([v, jnp.ones_like(v)], axis=1)
     squared = None
-    for h in range(0, HEAD_GROUPS, TOGETHER):
-        qs = [q[:, (h + j) * HEAD_SIZE : (h + j + 1) * HEAD_SIZE] for j in range(TOGETHER)]
+    for h in range(0, HEAD_GROUPS, together):
+        qs = [q[:, (h + j) * HEAD_SIZE : (h + j + 1) * HEAD_SIZE] for j in range(together)]
         s = lax.dot_general(
             jnp.concatenate(qs, axis=0),
             k,
@@ -196,7 +198,7 @@
             preferred_element_type=jnp.float32,
         )
         s = s + bias
-        here = slice(h * tokens, (h + TOGETHER) * tokens)
+        here = slice(h * tokens, (h + together) * tokens)
         high = jnp.max(s, axis=1, keepdims=True)
         high = jnp.broadcast_to(high, (high.shape[0], HEAD_SIZE))
         if stage != "first":
@@ -216,7 +218,7 @@
             continue
         kept = jnp.exp2((before - high) * (SCALE * LOG2E))
         out = (mixed + mix[here] * kept) / (total + sums[here] * kept)
-        for j in range(TOGETHER):
+        for j in range(together):
             where = slice((h + j) * HEAD_SIZE, (h + j + 1) * HEAD_SIZE)
             new = x[:, where] + out[j * tokens : (j + 1) * tokens]
             produced[0, :, where] = new.astype(jnp.bfloat16)

time: 188 us -> 188 us (level)
  transfers between devices with their start and end apart: 35 -> 35, of which waited for: 22 -> 21; matrix products, arithmetic and copies ran while one was open for 3% -> 3% of each run, Pallas kernels for 12% -> 11%
where the time goes in v6:
time: 188 us; the launch traced here: 186 us
  waiting for transfers between devices  85.6 us (46%)
  starting transfers between devices  37.9 us (20%)
  Pallas kernels  37.9 us (20%)
  between operations  14 us (7%)
  local copies, waits for them, and re-layouts  7.01 us (4%)
  other arithmetic  3.36 us (2%)
    ppermute x31, waiting for transfers between devices, moved(): return lax.ppermute(block, 'ctx', pairs)  64.8 us
    ppermute x31, starting transfers between devices, moved(): return lax.ppermute(block, 'ctx', pairs)  37.9 us
    pallas_call x4, Pallas kernels, attention(): pl.pallas_call(functools.partial(attention_body, n_blocks, stage, tick),...  25.8 us
    ppermute x1, waiting for transfers between devices, shards(): normed = lax.ppermute(normed, 'section', onward)  14.2 us
    pallas_call x3, Pallas kernels, projection(): pl.pallas_call(functools.partial(projection_body, n_keys, keys is not Non...  12 us
    all_gather x1, waiting for transfers between devices, shards(): value_weights = lax.all_gather(value_rows[0], 'ctx', axis=0, tiled=True)  5.86 us
    unnamed x50, local copies, waits for them, and re-layouts  5.51 us
  transfers between devices with their start and end apart: 35, of which 21 were waited for; matrix products, arithmetic and copies ran while one was open for 3% of the time, Pallas kernels for 11%

profile of v6, /device:TPU:2, one launch (start us, length us, event | category | flops | bytes accessed | tf_op | source)
XLA Modules:
  0.0 185.7 jit_solution(1581501583369983649)
XLA Ops:
  7.3 4.0 %collective-permute-start.5 = (bf16[256,512]{1,0:T(8,128)(2,1)}, bf16[256,512]{1,0:T(8,128)(2,1)}, u32[]{:S(2)}, u32[]{:S(2)}) collective-permute-start(bf16[256,512]{1,0:T(8,128)(2,1)} %bitcast.39), channel_id=1, source_target_pairs={{0,8},{1,9},{2,10},{3,11},{4,12},{5,13},{6,14},{7,15},{8,0},{9,1},... | collective-permute-start | bytes 786440 | tf_op jit(solution)/shard_map/ppermute | solution.py:38
  11.2 3.2 %collective-permute-start.4 = (bf16[256,512]{1,0:T(8,128)(2,1)}, bf16[256,512]{1,0:T(8,128)(2,1)}, u32[]{:S(2)}, u32[]{:S(2)}) collective-permute-start(bf16[256,512]{1,0:T(8,128)(2,1)} %bitcast.40), channel_id=1, source_target_pairs={{0,2},{1,3},{2,0},{3,1},{4,6},{5,7},{6,4},{7,5},{8,10},{9,11},{10,... | collective-permute-start | bytes 786440 | tf_op jit(solution)/shard_map/ppermute | solution.py:38
  14.4 1.1 collective-permute-start.3
  16.2 1.0 collective-permute-start.1
  17.2 1.8 multiply_reduce_fusion
  20.0 1.4 collective-permute-start
  21.4 0.9 collective-permute-done.4.refs_5_
  22.3 3.1 %collective-permute-start.13 = (bf16[256,512]{1,0:T(8,128)(2,1)}, bf16[256,512]{1,0:T(8,128)(2,1)}, u32[]{:S(2)}, u32[]{:S(2)}) collective-permute-start(bf16[256,512]{1,0:T(8,128)(2,1)} %collective-permute-done.5.refs_6_), channel_id=1, source_target_pairs={{0,3},{1,0},{2,1},{3,2},{4,7},{5,4},{6,5},{7,6},{8,11},{9,8},{10,9... | collective-permute-start | bytes 786440 | tf_op jit(solution)/shard_map/ppermute | solution.py:38
  25.3 4.8 %collective-permute-done.3.refs_4_ = bf16[256,512]{1,0:T(8,128)(2,1)} collective-permute-done((bf16[256,512]{1,0:T(8,128)(2,1)}, bf16[256,512]{1,0:T(8,128)(2,1)}, u32[]{:S(2)}, u32[]{:S(2)}) %collective-permute-start.3) | collective-permute-done | bytes 262176 | tf_op jit(solution)/shard_map/ppermute | solution.py:38
  30.3 1.9 %collective-permute-start.10 = (bf16[256,512]{1,0:T(8,128)(2,1)}, bf16[256,512]{1,0:T(8,128)(2,1)}, u32[]{:S(2)}, u32[]{:S(2)}) collective-permute-start(bf16[256,512]{1,0:T(8,128)(2,1)} %collective-permute-done.4.refs_5_), channel_id=1, source_target_pairs={{0,4},{1,5},{2,6},{3,7},{4,8},{5,9},{6,10},{7,11},{8,12},{9,13},{1... | collective-permute-start | bytes 786440 | tf_op jit(solution)/shard_map/ppermute | solution.py:38
  32.6 1.2 collective-permute-start.8
  33.8 2.8 %collective-permute-done.13.refs_14_ = bf16[256,512]{1,0:T(8,128)(2,1)} collective-permute-done((bf16[256,512]{1,0:T(8,128)(2,1)}, bf16[256,512]{1,0:T(8,128)(2,1)}, u32[]{:S(2)}, u32[]{:S(2)}) %collective-permute-start.13) | collective-permute-done | bytes 262176 | tf_op jit(solution)/shard_map/ppermute | solution.py:38
  36.6 2.6 %collective-permute-start.7 = (bf16[256,512]{1,0:T(8,128)(2,1)}, bf16[256,512]{1,0:T(8,128)(2,1)S(1)}, u32[]{:S(2)}, u32[]{:S(2)}) collective-permute-start(bf16[256,512]{1,0:T(8,128)(2,1)} %collective-permute-done.2.refs_3_), channel_id=1, source_target_pairs={{0,3},{1,0},{2,1},{3,2},{4,7},{5,4},{6,5},{7,6},{8,11},{9,8},{10,9... | collective-permute-start | bytes 786440 | tf_op jit(solution)/shard_map/ppermute | solution.py:38
  40.1 1.2 collective-permute-done.10.refs_11_
  42.0 1.1 dynamic-slice_bitcast_fusion.refs_7_
  43.1 3.7 %collective-permute-done.8.refs_9_ = bf16[256,512]{1,0:T(8,128)(2,1)S(1)} collective-permute-done((bf16[256,512]{1,0:T(8,128)(2,1)}, bf16[256,512]{1,0:T(8,128)(2,1)S(1)}, u32[]{:S(2)}, u32[]{:S(2)}) %collective-permute-start.8) | collective-permute-done | bytes 262176 | tf_op jit(solution)/shard_map/ppermute | solution.py:38
  46.8 2.1 %collective-permute-done.9.refs_10_ = bf16[256,512]{1,0:T(8,128)(2,1)S(1)} collective-permute-done((bf16[256,512]{1,0:T(8,128)(2,1)}, bf16[256,512]{1,0:T(8,128)(2,1)S(1)}, u32[]{:S(2)}, u32[]{:S(2)}) %collective-permute-start.9) | collective-permute-done | bytes 262176 | tf_op jit(solution)/shard_map/ppermute | solution.py:38
  48.9 2.3 %collective-permute-done.6.refs_7_ = bf16[256,512]{1,0:T(8,128)(2,1)S(1)} collective-permute-done((bf16[256,512]{1,0:T(8,128)(2,1)}, bf16[256,512]{1,0:T(8,128)(2,1)S(1)}, u32[]{:S(2)}, u32[]{:S(2)}) %collective-permute-start.6) | collective-permute-done | bytes 262176 | tf_op jit(solution)/shard_map/ppermute | solution.py:38
  51.2 4.5 %collective-permute-done.14.refs_15_ = bf16[256,512]{1,0:T(8,128)(2,1)S(1)} collective-permute-done((bf16[256,512]{1,0:T(8,128)(2,1)}, bf16[256,512]{1,0:T(8,128)(2,1)S(1)}, u32[]{:S(2)}, u32[]{:S(2)}) %collective-permute-start.14) | collective-permute-done | bytes 262176 | tf_op jit(solution)/shard_map/ppermute | solution.py:38
  55.8 3.0 %projection.3.refs_0_ = bf16[128,512]{1,0:T(8,128)(2,1)S(1)} custom-call(s32[16]{0:T(128)S(1)} %stack.85.order, bf16[128,4096]{1,0:T(8,128)(2,1)S(1)} %multiply_convert_fusion.rows.q, bf16[256,512]{1,0:T(8,128)(2,1)S(1)} %bitcast.45, bf16[256,512]{1,0:T(8,128)(2,1)} %collective-permute-done.refs_1_, bf16[256,512]{1,0:T(8,128)(2,1)} %collective-permute-done.1.refs_2_, ...), custom_call_target="tpu_custom_call" | custom-call | flops 536870912 | bytes 4194304 | tf_op jit(solution)/shard_map/projection/pallas_call | solution.py:146
  63.0 5.9 %all-gather.3.cloned.1.call-done = bf16[1,4096,512]{2,1,0:T(8,128)(2,1)} async-done(((bf16[1,256,512]{2,1,0:T(8,128)(2,1)}), bf16[1,4096,512]{2,1,0:T(8,128)(2,1)}) %all-gather.3.cloned.1.call-update) | async-done | bytes 4194320 | tf_op jit(solution)/shard_map/all_gather | solution.py:316
  68.9 4.5 %projection.4.refs_0_ = bf16[128,1024]{1,0:T(8,128)(2,1)} custom-call(s32[16]{0:T(128)} %copy-done.20, bf16[128,4096]{1,0:T(8,128)(2,1)} %copy-done.4, bf16[128,512]{1,0:T(8,128)(2,1)} %copy-done.19, bf16[4096,512]{1,0:T(8,128)(2,1)} %bitcast.37), custom_call_target="tpu_custom_call" | custom-call | flops 536870912 | bytes 4194304 | tf_op jit(solution)/shard_map/projection/pallas_call | solution.py:146
  73.8 9.5 %collective-permute-done.15.refs_1_ = bf16[128,1024]{1,0:T(8,128)(2,1)} collective-permute-done((bf16[128,1024]{1,0:T(8,128)(2,1)}, bf16[128,1024]{1,0:T(8,128)(2,1)}, u32[]{:S(2)}, u32[]{:S(2)}) %collective-permute-start.15) | collective-permute-done | bytes 262176 | tf_op jit(solution)/shard_map/ppermute | solution.py:38
  83.3 2.4 %collective-permute-start.22 = (bf16[128,1024]{1,0:T(8,128)(2,1)}, bf16[128,1024]{1,0:T(8,128)(2,1)}, u32[]{:S(2)}, u32[]{:S(2)}) collective-permute-start(bf16[128,1024]{1,0:T(8,128)(2,1)} %collective-permute-done.15.refs_1_), channel_id=1, source_target_pairs={{0,2},{1,3},{2,0},{3,1},{4,6},{5,7},{6,4},{7,5},{8,10},{9,11},{10,... | collective-permute-start | bytes 786440 | tf_op jit(solution)/shard_map/ppermute | solution.py:38
  86.4 1.3 collective-permute-start.20
  87.7 4.5 %collective-permute-done.16.refs_2_ = bf16[128,1024]{1,0:T(8,128)(2,1)} collective-permute-done((bf16[128,1024]{1,0:T(8,128)(2,1)}, bf16[128,1024]{1,0:T(8,128)(2,1)}, u32[]{:S(2)}, u32[]{:S(2)}) %collective-permute-start.16) | collective-permute-done | bytes 262176 | tf_op jit(solution)/shard_map/ppermute | solution.py:38
  92.2 1.1 broadcast_select_fusion.1
  93.3 2.5 %collective-permute-start.19 = (bf16[128,1024]{1,0:T(8,128)(2,1)S(1)}, bf16[128,1024]{1,0:T(8,128)(2,1)S(1)}, u32[]{:S(2)}, u32[]{:S(2)}) collective-permute-start(bf16[128,1024]{1,0:T(8,128)(2,1)S(1)} %get-tuple-element.38), channel_id=1, source_target_pairs={{0,2},{1,3},{2,0},{3,1},{4,6},{5,7},{6,4},{7,5},{8,10},{9,11},{10,... | collective-permute-start | bytes 786440 | tf_op jit(solution)/shard_map/ppermute | solution.py:38
  96.5 1.3 collective-permute-start.17
  97.8 1.2 collective-permute-done.21.refs_4_
  98.9 3.8 %collective-permute-done.20.refs_3_ = bf16[128,1024]{1,0:T(8,128)(2,1)S(1)} collective-permute-done((bf16[128,1024]{1,0:T(8,128)(2,1)}, bf16[128,1024]{1,0:T(8,128)(2,1)S(1)}, u32[]{:S(2)}, u32[]{:S(2)}) %collective-permute-start.20) | collective-permute-done | bytes 262176 | tf_op jit(solution)/shard_map/ppermute | solution.py:38
  102.7 0.9 copy-done.18
  103.7 7.2 %attention.4 = (f32[4096,128]{1,0:T(8,128)S(1)}, f32[4096,128]{1,0:T(8,128)S(1)}, f32[4096,128]{1,0:T(8,128)S(1)}) custom-call(s32[28]{0:T(128)S(1)} %concatenate.3.info, bf16[128,4096]{1,0:T(8,128)(2,1)S(1)} %copy-done.5, bf16[128,1024]{1,0:T(8,128)(2,1)S(1)} %copy-done.18, bf16[128,1024]{1,0:T(8,128)(2,1)} %collective-permute-done.15.refs_1_, ...), custom_call_target="tpu_custom_call" | custom-call | flops 1610612736 | bytes 7864320 | tf_op jit(solution)/shard_map/attention/pallas_call | solution.py:278
  111.0 6.7 %attention.5 = (bf16[2,128,4096]{2,1,0:T(8,128)(2,1)}, f32[128,4096]{1,0:T(8,128)S(1)}, bf16[128,4096]{1,0:T(8,128)(2,1)S(1)}) custom-call(s32[28]{0:T(128)S(1)} %concatenate.3.info, bf16[128,4096]{1,0:T(8,128)(2,1)S(1)} %copy-done.5, bf16[128,1024]{1,0:T(8,128)(2,1)S(1)} %collective-permute-done.17.refs_0_, ...), custom_call_target="tpu_custom_call" | custom-call | flops 805306368 | bytes 7077888 | tf_op jit(solution)/shard_map/attention/pallas_call | solution.py:278
  117.7 14.2 %collective-permute-done.24.rows.q = bf16[128,4096]{1,0:T(8,128)(2,1)S(1)} collective-permute-done((bf16[128,4096]{1,0:T(8,128)(2,1)S(1)}, bf16[128,4096]{1,0:T(8,128)(2,1)S(1)}, u32[]{:S(2)}, u32[]{:S(2)}) %collective-permute-start.24) | collective-permute-done | bytes 1048608 | tf_op jit(solution)/shard_map/ppermute | solution.py:338
  132.0 4.5 %projection.5.refs_0_ = bf16[128,1024]{1,0:T(8,128)(2,1)S(1)} custom-call(s32[16]{0:T(128)S(1)} %copy-done.21, bf16[128,4096]{1,0:T(8,128)(2,1)S(1)} %collective-permute-done.24.rows.q, bf16[256,512]{1,0:T(8,128)(2,1)S(1)} %bitcast.46, bf16[256,512]{1,0:T(8,128)(2,1)} %collective-permute-done.refs_1_, bf16[256,512]{1,0:T(8,128)(2,1)} %collective-permute-done.1.refs_2_, ...), custom_call_target="tpu_custom_call" | custom-call | flops 1073741824 | bytes 8388608 | tf_op jit(solution)/shard_map/projection/pallas_call | solution.py:146
  136.6 9.5 %collective-permute-done.25.refs_1_ = bf16[128,1024]{1,0:T(8,128)(2,1)S(1)} collective-permute-done((bf16[128,1024]{1,0:T(8,128)(2,1)S(1)}, bf16[128,1024]{1,0:T(8,128)(2,1)S(1)}, u32[]{:S(2)}, u32[]{:S(2)}) %collective-permute-start.25) | collective-permute-done | bytes 262176 | tf_op jit(solution)/shard_map/ppermute | solution.py:38
  146.1 1.0 collective-permute-start.33
  147.1 1.3 collective-permute-start.32
  149.1 7.1 %collective-permute-done.26.refs_2_ = bf16[128,1024]{1,0:T(8,128)(2,1)S(1)} collective-permute-done((bf16[128,1024]{1,0:T(8,128)(2,1)S(1)}, bf16[128,1024]{1,0:T(8,128)(2,1)S(1)}, u32[]{:S(2)}, u32[]{:S(2)}) %collective-permute-start.26) | collective-permute-done | bytes 262176 | tf_op jit(solution)/shard_map/ppermute | solution.py:38
  156.3 0.8 collective-permute-start.29
  157.1 1.3 collective-permute-start.28
  158.3 1.6 collective-permute-done.32.refs_4_
  160.0 1.9 %collective-permute-start.27 = (bf16[128,1024]{1,0:T(8,128)(2,1)S(1)}, bf16[128,1024]{1,0:T(8,128)(2,1)S(1)}, u32[]{:S(2)}, u32[]{:S(2)}) collective-permute-start(bf16[128,1024]{1,0:T(8,128)(2,1)S(1)} %get-tuple-element.37), channel_id=1, source_target_pairs={{0,1},{1,2},{2,3},{3,0},{4,5},{5,6},{6,7},{7,4},{8,9},{9,10},{10,1... | collective-permute-start | bytes 786440 | tf_op jit(solution)/shard_map/ppermute | solution.py:38
  162.3 6.5 %attention.6 = (f32[4096,128]{1,0:T(8,128)S(1)}, f32[4096,128]{1,0:T(8,128)S(1)}, f32[4096,128]{1,0:T(8,128)S(1)}) custom-call(s32[28]{0:T(128)S(1)} %concatenate.3.info, bf16[128,4096]{1,0:T(8,128)(2,1)S(1)} %collective-permute-done.24.rows.q, bf16[128,1024]{1,0:T(8,128)(2,1)S(1)} %projection.5.refs_0_, ...), custom_call_target="tpu_custom_call" | custom-call | flops 1610612736 | bytes 7864320 | tf_op jit(solution)/shard_map/attention/pallas_call | solution.py:278
  168.8 2.0 %collective-permute-done.28.refs_1_ = bf16[128,1024]{1,0:T(8,128)(2,1)S(1)} collective-permute-done((bf16[128,1024]{1,0:T(8,128)(2,1)S(1)}, bf16[128,1024]{1,0:T(8,128)(2,1)S(1)}, u32[]{:S(2)}, u32[]{:S(2)}) %collective-permute-start.28) | collective-permute-done | bytes 262176 | tf_op jit(solution)/shard_map/ppermute | solution.py:38
  170.8 2.6 %collective-permute-done.27.refs_0_ = bf16[128,1024]{1,0:T(8,128)(2,1)S(1)} collective-permute-done((bf16[128,1024]{1,0:T(8,128)(2,1)S(1)}, bf16[128,1024]{1,0:T(8,128)(2,1)S(1)}, u32[]{:S(2)}, u32[]{:S(2)}) %collective-permute-start.27) | collective-permute-done | bytes 262176 | tf_op jit(solution)/shard_map/ppermute | solution.py:38
  173.4 5.5 %attention.7 = bf16[2,128,4096]{2,1,0:T(8,128)(2,1)} custom-call(s32[28]{0:T(128)S(1)} %concatenate.3.info, bf16[128,4096]{1,0:T(8,128)(2,1)S(1)} %collective-permute-done.24.rows.q, bf16[128,1024]{1,0:T(8,128)(2,1)S(1)} %collective-permute-done.27.refs_0_, bf16[128,1024]{1,0:T(8,128)(2,1)S(1)} %collective-permute-done.28.refs_1_, ...), custom_call_target="tpu_custom_call", output_to_operand_aliasing={{}: (9, {})} | custom-call | flops 805306368 | bytes 7077888 | tf_op jit(solution)/shard_map/attention/pallas_call | solution.py:278
  (92 shorter events, 11.6 us)
Async XLA Ops:
  6.5 35.4 %copy-start = (bf16[2,128,4096]{2,1,0:T(8,128)(2,1)S(1)}, bf16[2,128,4096]{2,1,0:T(8,128)(2,1)}, u32[]{:S(2)}) copy-start(bf16[2,128,4096]{2,1,0:T(8,128)(2,1)} %param.8) | copy-start | bytes 6291460
  6.5 62.3 %all-gather.3.cloned.1.call-start = ((), (), s32[]{:S(2)}) async-start(), calls=%async_computation | async-start | bytes 4456448 | tf_op jit(solution)/shard_map/all_gather | solution.py:316
  7.3 12.7 %collective-permute-start.5 = (bf16[256,512]{1,0:T(8,128)(2,1)}, bf16[256,512]{1,0:T(8,128)(2,1)}, u32[]{:S(2)}, u32[]{:S(2)}) collective-permute-start(bf16[256,512]{1,0:T(8,128)(2,1)} %bitcast.39), channel_id=1, source_target_pairs={{0,8},{1,9},{2,10},{3,11},{4,12},{5,13},{6,14},{7,15},{8,0},{9,1},... | collective-permute-start | bytes 786440 | tf_op jit(solution)/shard_map/ppermute | solution.py:38
  11.2 11.1 %collective-permute-start.4 = (bf16[256,512]{1,0:T(8,128)(2,1)}, bf16[256,512]{1,0:T(8,128)(2,1)}, u32[]{:S(2)}, u32[]{:S(2)}) collective-permute-start(bf16[256,512]{1,0:T(8,128)(2,1)} %bitcast.40), channel_id=1, source_target_pairs={{0,2},{1,3},{2,0},{3,1},{4,6},{5,7},{6,4},{7,5},{8,10},{9,11},{10,... | collective-permute-start | bytes 786440 | tf_op jit(solution)/shard_map/ppermute | solution.py:38
  14.4 15.7 %collective-permute-start.3 = (bf16[256,512]{1,0:T(8,128)(2,1)}, bf16[256,512]{1,0:T(8,128)(2,1)}, u32[]{:S(2)}, u32[]{:S(2)}) collective-permute-start(bf16[256,512]{1,0:T(8,128)(2,1)} %bitcast.41), channel_id=1, source_target_pairs={{0,3},{1,0},{2,1},{3,2},{4,7},{5,4},{6,5},{7,6},{8,11},{9,8},{10,9... | collective-permute-start | bytes 786440 | tf_op jit(solution)/shard_map/ppermute | solution.py:38
  15.5 14.7 %collective-permute-start.2 = (bf16[256,512]{1,0:T(8,128)(2,1)}, bf16[256,512]{1,0:T(8,128)(2,1)}, u32[]{:S(2)}, u32[]{:S(2)}) collective-permute-start(bf16[256,512]{1,0:T(8,128)(2,1)} %bitcast.42), channel_id=1, source_target_pairs={{0,12},{1,13},{2,14},{3,15},{4,0},{5,1},{6,2},{7,3},{8,4},{9,5},{1... | collective-permute-start | bytes 786440 | tf_op jit(solution)/shard_map/ppermute | solution.py:38
  16.2 14.1 %collective-permute-start.1 = (bf16[256,512]{1,0:T(8,128)(2,1)}, bf16[256,512]{1,0:T(8,128)(2,1)}, u32[]{:S(2)}, u32[]{:S(2)}) collective-permute-start(bf16[256,512]{1,0:T(8,128)(2,1)} %bitcast.43), channel_id=1, source_target_pairs={{0,1},{1,2},{2,3},{3,0},{4,5},{5,6},{6,7},{7,4},{8,9},{9,10},{10,1... | collective-permute-start | bytes 786440 | tf_op jit(solution)/shard_map/ppermute | solution.py:38
  19.3 39.5 %copy-start.4 = (bf16[128,4096]{1,0:T(8,128)(2,1)}, bf16[128,4096]{1,0:T(8,128)(2,1)S(1)}, u32[]{:S(2)}) copy-start(bf16[128,4096]{1,0:T(8,128)(2,1)S(1)} %multiply_convert_fusion.rows.q) | copy-start | bytes 3145732
  20.0 12.5 %collective-permute-start = (bf16[256,512]{1,0:T(8,128)(2,1)S(1)}, bf16[256,512]{1,0:T(8,128)(2,1)}, u32[]{:S(2)}, u32[]{:S(2)}) collective-permute-start(bf16[256,512]{1,0:T(8,128)(2,1)S(1)} %bitcast.44), channel_id=1, source_target_pairs={{0,4},{1,5},{2,6},{3,7},{4,8},{5,9},{6,10},{7,11},{8,12},{9,13},{1... | collective-permute-start | bytes 786440 | tf_op jit(solution)/shard_map/ppermute | solution.py:38
  22.3 14.4 %collective-permute-start.13 = (bf16[256,512]{1,0:T(8,128)(2,1)}, bf16[256,512]{1,0:T(8,128)(2,1)}, u32[]{:S(2)}, u32[]{:S(2)}) collective-permute-start(bf16[256,512]{1,0:T(8,128)(2,1)} %collective-permute-done.5.refs_6_), channel_id=1, source_target_pairs={{0,3},{1,0},{2,1},{3,2},{4,7},{5,4},{6,5},{7,6},{8,11},{9,8},{10,9... | collective-permute-start | bytes 786440 | tf_op jit(solution)/shard_map/ppermute | solution.py:38
  30.2 9.3 %collective-permute-start.12 = (bf16[256,512]{1,0:T(8,128)(2,1)}, bf16[256,512]{1,0:T(8,128)(2,1)}, u32[]{:S(2)}, u32[]{:S(2)}) collective-permute-start(bf16[256,512]{1,0:T(8,128)(2,1)} %collective-permute-done.5.refs_6_), channel_id=1, source_target_pairs={{0,1},{1,2},{2,3},{3,0},{4,5},{5,6},{6,7},{7,4},{8,9},{9,10},{10,1... | collective-permute-start | bytes 786440 | tf_op jit(solution)/shard_map/ppermute | solution.py:38
  30.2 9.8 %collective-permute-start.11 = (bf16[256,512]{1,0:T(8,128)(2,1)}, bf16[256,512]{1,0:T(8,128)(2,1)}, u32[]{:S(2)}, u32[]{:S(2)}) collective-permute-start(bf16[256,512]{1,0:T(8,128)(2,1)} %collective-permute-done.4.refs_5_), channel_id=1, source_target_pairs={{0,12},{1,13},{2,14},{3,15},{4,0},{5,1},{6,2},{7,3},{8,4},{9,5},{1... | collective-permute-start | bytes 786440 | tf_op jit(solution)/shard_map/ppermute | solution.py:38
  30.3 11.0 %collective-permute-start.10 = (bf16[256,512]{1,0:T(8,128)(2,1)}, bf16[256,512]{1,0:T(8,128)(2,1)}, u32[]{:S(2)}, u32[]{:S(2)}) collective-permute-start(bf16[256,512]{1,0:T(8,128)(2,1)} %collective-permute-done.4.refs_5_), channel_id=1, source_target_pairs={{0,4},{1,5},{2,6},{3,7},{4,8},{5,9},{6,10},{7,11},{8,12},{9,13},{1... | collective-permute-start | bytes 786440 | tf_op jit(solution)/shard_map/ppermute | solution.py:38
  32.5 26.3 %copy-start.20 = (s32[16]{0:T(128)}, s32[16]{0:T(128)S(1)}, u32[]{:S(2)}) copy-start(s32[16]{0:T(128)S(1)} %stack.85.order) | copy-start | bytes 196
  32.6 14.2 %collective-permute-start.8 = (bf16[256,512]{1,0:T(8,128)(2,1)}, bf16[256,512]{1,0:T(8,128)(2,1)S(1)}, u32[]{:S(2)}, u32[]{:S(2)}) collective-permute-start(bf16[256,512]{1,0:T(8,128)(2,1)} %collective-permute-done.3.refs_4_), channel_id=1, source_target_pairs={{0,4},{1,5},{2,6},{3,7},{4,8},{5,9},{6,10},{7,11},{8,12},{9,13},{1... | collective-permute-start | bytes 786440 | tf_op jit(solution)/shard_map/ppermute | solution.py:38
  36.6 10.1 %collective-permute-start.7 = (bf16[256,512]{1,0:T(8,128)(2,1)}, bf16[256,512]{1,0:T(8,128)(2,1)S(1)}, u32[]{:S(2)}, u32[]{:S(2)}) collective-permute-start(bf16[256,512]{1,0:T(8,128)(2,1)} %collective-permute-done.2.refs_3_), channel_id=1, source_target_pairs={{0,3},{1,0},{2,1},{3,2},{4,7},{5,4},{6,5},{7,6},{8,11},{9,8},{10,9... | collective-permute-start | bytes 786440 | tf_op jit(solution)/shard_map/ppermute | solution.py:38
  39.5 9.4 %collective-permute-start.9 = (bf16[256,512]{1,0:T(8,128)(2,1)}, bf16[256,512]{1,0:T(8,128)(2,1)S(1)}, u32[]{:S(2)}, u32[]{:S(2)}) collective-permute-start(bf16[256,512]{1,0:T(8,128)(2,1)} %collective-permute-done.1.refs_2_), channel_id=1, source_target_pairs={{0,12},{1,13},{2,14},{3,15},{4,0},{5,1},{6,2},{7,3},{8,4},{9,5},{1... | collective-permute-start | bytes 786440 | tf_op jit(solution)/shard_map/ppermute | solution.py:38
  40.0 11.2 %collective-permute-start.6 = (bf16[256,512]{1,0:T(8,128)(2,1)}, bf16[256,512]{1,0:T(8,128)(2,1)S(1)}, u32[]{:S(2)}, u32[]{:S(2)}) collective-permute-start(bf16[256,512]{1,0:T(8,128)(2,1)} %collective-permute-done.refs_1_), channel_id=1, source_target_pairs={{0,1},{1,2},{2,3},{3,0},{4,5},{5,6},{6,7},{7,4},{8,9},{9,10},{10,1... | collective-permute-start | bytes 786440 | tf_op jit(solution)/shard_map/ppermute | solution.py:38
  41.3 14.5 %collective-permute-start.14 = (bf16[256,512]{1,0:T(8,128)(2,1)}, bf16[256,512]{1,0:T(8,128)(2,1)S(1)}, u32[]{:S(2)}, u32[]{:S(2)}) collective-permute-start(bf16[256,512]{1,0:T(8,128)(2,1)} %collective-permute-done.10.refs_11_), channel_id=1, source_target_pairs={{0,4},{1,5},{2,6},{3,7},{4,8},{5,9},{6,10},{7,11},{8,12},{9,13},{1... | collective-permute-start | bytes 786440 | tf_op jit(solution)/shard_map/ppermute | solution.py:38
  68.9 33.8 %copy-start.5 = (bf16[128,4096]{1,0:T(8,128)(2,1)S(1)}, bf16[128,4096]{1,0:T(8,128)(2,1)}, u32[]{:S(2)}) copy-start(bf16[128,4096]{1,0:T(8,128)(2,1)} %copy-done.4) | copy-start | bytes 3145732
  73.4 9.9 %collective-permute-start.15 = (bf16[128,1024]{1,0:T(8,128)(2,1)}, bf16[128,1024]{1,0:T(8,128)(2,1)}, u32[]{:S(2)}, u32[]{:S(2)}) collective-permute-start(bf16[128,1024]{1,0:T(8,128)(2,1)} %projection.4.refs_0_), channel_id=1, source_target_pairs={{0,4},{1,5},{2,6},{3,7},{4,8},{5,9},{6,10},{7,11},{8,12},{9,13},{1... | collective-permute-start | bytes 786440 | tf_op jit(solution)/shard_map/ppermute | solution.py:38
  83.3 8.9 %collective-permute-start.16 = (bf16[128,1024]{1,0:T(8,128)(2,1)}, bf16[128,1024]{1,0:T(8,128)(2,1)}, u32[]{:S(2)}, u32[]{:S(2)}) collective-permute-start(bf16[128,1024]{1,0:T(8,128)(2,1)} %collective-permute-done.15.refs_1_), channel_id=1, source_target_pairs={{0,4},{1,5},{2,6},{3,7},{4,8},{5,9},{6,10},{7,11},{8,12},{9,13},{1... | collective-permute-start | bytes 786440 | tf_op jit(solution)/shard_map/ppermute | solution.py:38
  83.3 13.2 %collective-permute-start.22 = (bf16[128,1024]{1,0:T(8,128)(2,1)}, bf16[128,1024]{1,0:T(8,128)(2,1)}, u32[]{:S(2)}, u32[]{:S(2)}) collective-permute-start(bf16[128,1024]{1,0:T(8,128)(2,1)} %collective-permute-done.15.refs_1_), channel_id=1, source_target_pairs={{0,2},{1,3},{2,0},{3,1},{4,6},{5,7},{6,4},{7,5},{8,10},{9,11},{10,... | collective-permute-start | bytes 786440 | tf_op jit(solution)/shard_map/ppermute | solution.py:38
  85.7 13.3 %collective-permute-start.21 = (bf16[128,1024]{1,0:T(8,128)(2,1)}, bf16[128,1024]{1,0:T(8,128)(2,1)S(1)}, u32[]{:S(2)}, u32[]{:S(2)}) collective-permute-start(bf16[128,1024]{1,0:T(8,128)(2,1)} %collective-permute-done.15.refs_1_), channel_id=1, source_target_pairs={{0,3},{1,0},{2,1},{3,2},{4,7},{5,4},{6,5},{7,6},{8,11},{9,8},{10,9... | collective-permute-start | bytes 786440 | tf_op jit(solution)/shard_map/ppermute | solution.py:38
  86.4 16.3 %collective-permute-start.20 = (bf16[128,1024]{1,0:T(8,128)(2,1)}, bf16[128,1024]{1,0:T(8,128)(2,1)S(1)}, u32[]{:S(2)}, u32[]{:S(2)}) collective-permute-start(bf16[128,1024]{1,0:T(8,128)(2,1)} %collective-permute-done.15.refs_1_), channel_id=1, source_target_pairs={{0,1},{1,2},{2,3},{3,0},{4,5},{5,6},{6,7},{7,4},{8,9},{9,10},{10,1... | collective-permute-start | bytes 786440 | tf_op jit(solution)/shard_map/ppermute | solution.py:38
  93.3 17.6 %collective-permute-start.19 = (bf16[128,1024]{1,0:T(8,128)(2,1)S(1)}, bf16[128,1024]{1,0:T(8,128)(2,1)S(1)}, u32[]{:S(2)}, u32[]{:S(2)}) collective-permute-start(bf16[128,1024]{1,0:T(8,128)(2,1)S(1)} %get-tuple-element.38), channel_id=1, source_target_pairs={{0,2},{1,3},{2,0},{3,1},{4,6},{5,7},{6,4},{7,5},{8,10},{9,11},{10,... | collective-permute-start | bytes 786440 | tf_op jit(solution)/shard_map/ppermute | solution.py:38
  95.7 15.2 %collective-permute-start.18 = (bf16[128,1024]{1,0:T(8,128)(2,1)S(1)}, bf16[128,1024]{1,0:T(8,128)(2,1)S(1)}, u32[]{:S(2)}, u32[]{:S(2)}) collective-permute-start(bf16[128,1024]{1,0:T(8,128)(2,1)S(1)} %get-tuple-element.39), channel_id=1, source_target_pairs={{0,3},{1,0},{2,1},{3,2},{4,7},{5,4},{6,5},{7,6},{8,11},{9,8},{10,9... | collective-permute-start | bytes 786440 | tf_op jit(solution)/shard_map/ppermute | solution.py:38
  96.5 14.4 %copy-start.2 = (f32[1,128,4096]{2,1,0:T(8,128)S(1)}, f32[1,128,4096]{2,1,0:T(8,128)}, u32[]{:S(2)}) copy-start(f32[1,128,4096]{2,1,0:T(8,128)} %param.7) | copy-start | bytes 6291460
  96.5 14.4 %copy-start.6 = (bf16[128,4096]{1,0:T(8,128)(2,1)S(1)}, bf16[128,4096]{1,0:T(8,128)(2,1)}, u32[]{:S(2)}) copy-start(bf16[128,4096]{1,0:T(8,128)(2,1)} %dynamic-slice_bitcast_fusion.refs_7_) | copy-start | bytes 3145732
  96.5 14.4 %collective-permute-start.17 = (bf16[128,1024]{1,0:T(8,128)(2,1)S(1)}, bf16[128,1024]{1,0:T(8,128)(2,1)S(1)}, u32[]{:S(2)}, u32[]{:S(2)}) collective-permute-start(bf16[128,1024]{1,0:T(8,128)(2,1)S(1)} %get-tuple-element.40), channel_id=1, source_target_pairs={{0,1},{1,2},{2,3},{3,0},{4,5},{5,6},{6,7},{7,4},{8,9},{9,10},{10,1... | collective-permute-start | bytes 786440 | tf_op jit(solution)/shard_map/ppermute | solution.py:38
  98.9 11.9 %collective-permute-start.23 = (f32[1,4096]{1,0:T(1,128)S(1)}, f32[1,4096]{1,0:T(1,128)S(1)}, u32[]{:S(2)}, u32[]{:S(2)}) collective-permute-start(f32[1,4096]{1,0:T(1,128)S(1)} %copy-done.22), channel_id=1, source_target_pairs={{16,0},{32,16},{48,32},{64,48},{80,64},{96,80},{112,96},{0,112},{1... | collective-permute-start | bytes 49160 | tf_op jit(solution)/shard_map/ppermute | solution.py:319
  110.9 21.0 %copy-start.3 = (bf16[1,4096,512]{2,1,0:T(8,128)(2,1)S(1)}, bf16[1,4096,512]{2,1,0:T(8,128)(2,1)}, u32[]{:S(2)}) copy-start(bf16[1,4096,512]{2,1,0:T(8,128)(2,1)} %all-gather.3.cloned.1.call-done) | copy-start | bytes 12582916
  110.9 21.0 %copy-start.9 = (bf16[256,512]{1,0:T(8,128)(2,1)S(1)}, bf16[256,512]{1,0:T(8,128)(2,1)}, u32[]{:S(2)}) copy-start(bf16[256,512]{1,0:T(8,128)(2,1)} %copy-done.8) | copy-start | bytes 786436
  111.0 21.0 %copy-start.11 = (bf16[256,512]{1,0:T(8,128)(2,1)S(1)}, bf16[256,512]{1,0:T(8,128)(2,1)}, u32[]{:S(2)}) copy-start(bf16[256,512]{1,0:T(8,128)(2,1)} %copy-done.10) | copy-start | bytes 786436
  111.0 21.0 %copy-start.13 = (bf16[256,512]{1,0:T(8,128)(2,1)S(1)}, bf16[256,512]{1,0:T(8,128)(2,1)}, u32[]{:S(2)}) copy-start(bf16[256,512]{1,0:T(8,128)(2,1)} %copy-done.12) | copy-start | bytes 786436
  111.0 21.0 %copy-start.15 = (bf16[256,512]{1,0:T(8,128)(2,1)S(1)}, bf16[256,512]{1,0:T(8,128)(2,1)}, u32[]{:S(2)}) copy-start(bf16[256,512]{1,0:T(8,128)(2,1)} %copy-done.14) | copy-start | bytes 786436
  111.0 21.0 %copy-start.17 = (bf16[256,512]{1,0:T(8,128)(2,1)S(1)}, bf16[256,512]{1,0:T(8,128)(2,1)}, u32[]{:S(2)}) copy-start(bf16[256,512]{1,0:T(8,128)(2,1)} %copy-done.16) | copy-start | bytes 786436
  111.0 21.0 %copy-start.21 = (s32[16]{0:T(128)S(1)}, s32[16]{0:T(128)}, u32[]{:S(2)}) copy-start(s32[16]{0:T(128)} %copy-done.20) | copy-start | bytes 196
  117.7 14.2 %collective-permute-start.24 = (bf16[128,4096]{1,0:T(8,128)(2,1)S(1)}, bf16[128,4096]{1,0:T(8,128)(2,1)S(1)}, u32[]{:S(2)}, u32[]{:S(2)}) collective-permute-start(bf16[128,4096]{1,0:T(8,128)(2,1)S(1)} %get-tuple-element.25), channel_id=1, source_target_pairs={{0,16},{16,32},{32,48},{48,64},{64,80},{80,96},{96,112},{112,0},{1... | collective-permute-start | bytes 3145736 | tf_op jit(solution)/shard_map/ppermute | solution.py:338
  131.9 41.5 %collective-permute-start.30 = (f32[128,4096]{1,0:T(8,128)S(1)}, f32[128,4096]{1,0:T(8,128)S(1)}, u32[]{:S(2)}, u32[]{:S(2)}) collective-permute-start(f32[128,4096]{1,0:T(8,128)S(1)} %get-tuple-element.28), channel_id=1, source_target_pairs={{0,16},{16,32},{32,48},{48,64},{64,80},{80,96},{96,112},{112,0},{1... | collective-permute-start | bytes 6291464 | tf_op jit(solution)/shard_map/ppermute | solution.py:340
  136.5 9.6 %collective-permute-start.25 = (bf16[128,1024]{1,0:T(8,128)(2,1)S(1)}, bf16[128,1024]{1,0:T(8,128)(2,1)S(1)}, u32[]{:S(2)}, u32[]{:S(2)}) collective-permute-start(bf16[128,1024]{1,0:T(8,128)(2,1)S(1)} %projection.5.refs_0_), channel_id=1, source_target_pairs={{0,4},{1,5},{2,6},{3,7},{4,8},{5,9},{6,10},{7,11},{8,12},{9,13},{1... | collective-permute-start | bytes 786440 | tf_op jit(solution)/shard_map/ppermute | solution.py:38
  146.1 10.1 %collective-permute-start.26 = (bf16[128,1024]{1,0:T(8,128)(2,1)S(1)}, bf16[128,1024]{1,0:T(8,128)(2,1)S(1)}, u32[]{:S(2)}, u32[]{:S(2)}) collective-permute-start(bf16[128,1024]{1,0:T(8,128)(2,1)S(1)} %collective-permute-done.25.refs_1_), channel_id=1, source_target_pairs={{0,4},{1,5},{2,6},{3,7},{4,8},{5,9},{6,10},{7,11},{8,12},{9,13},{1... | collective-permute-start | bytes 786440 | tf_op jit(solution)/shard_map/ppermute | solution.py:38
  146.1 11.0 %collective-permute-start.33 = (bf16[128,1024]{1,0:T(8,128)(2,1)S(1)}, bf16[128,1024]{1,0:T(8,128)(2,1)S(1)}, u32[]{:S(2)}, u32[]{:S(2)}) collective-permute-start(bf16[128,1024]{1,0:T(8,128)(2,1)S(1)} %collective-permute-done.25.refs_1_), channel_id=1, source_target_pairs={{0,2},{1,3},{2,0},{3,1},{4,6},{5,7},{6,4},{7,5},{8,10},{9,11},{10,... | collective-permute-start | bytes 786440 | tf_op jit(solution)/shard_map/ppermute | solution.py:38
  147.1 12.9 %collective-permute-start.32 = (bf16[128,1024]{1,0:T(8,128)(2,1)S(1)}, bf16[128,1024]{1,0:T(8,128)(2,1)S(1)}, u32[]{:S(2)}, u32[]{:S(2)}) collective-permute-start(bf16[128,1024]{1,0:T(8,128)(2,1)S(1)} %collective-permute-done.25.refs_1_), channel_id=1, source_target_pairs={{0,3},{1,0},{2,1},{3,2},{4,7},{5,4},{6,5},{7,6},{8,11},{9,8},{10,9... | collective-permute-start | bytes 786440 | tf_op jit(solution)/shard_map/ppermute | solution.py:38
  148.3 14.0 %collective-permute-start.31 = (bf16[128,1024]{1,0:T(8,128)(2,1)S(1)}, bf16[128,1024]{1,0:T(8,128)(2,1)S(1)}, u32[]{:S(2)}, u32[]{:S(2)}) collective-permute-start(bf16[128,1024]{1,0:T(8,128)(2,1)S(1)} %collective-permute-done.25.refs_1_), channel_id=1, source_target_pairs={{0,1},{1,2},{2,3},{3,0},{4,5},{5,6},{6,7},{7,4},{8,9},{9,10},{10,1... | collective-permute-start | bytes 786440 | tf_op jit(solution)/shard_map/ppermute | solution.py:38
  156.3 12.5 %collective-permute-start.29 = (bf16[128,1024]{1,0:T(8,128)(2,1)S(1)}, bf16[128,1024]{1,0:T(8,128)(2,1)S(1)}, u32[]{:S(2)}, u32[]{:S(2)}) collective-permute-start(bf16[128,1024]{1,0:T(8,128)(2,1)S(1)} %get-tuple-element.35), channel_id=1, source_target_pairs={{0,2},{1,3},{2,0},{3,1},{4,6},{5,7},{6,4},{7,5},{8,10},{9,11},{10,... | collective-permute-start | bytes 786440 | tf_op jit(solution)/shard_map/ppermute | solution.py:38
  157.1 13.7 %collective-permute-start.28 = (bf16[128,1024]{1,0:T(8,128)(2,1)S(1)}, bf16[128,1024]{1,0:T(8,128)(2,1)S(1)}, u32[]{:S(2)}, u32[]{:S(2)}) collective-permute-start(bf16[128,1024]{1,0:T(8,128)(2,1)S(1)} %get-tuple-element.36), channel_id=1, source_target_pairs={{0,3},{1,0},{2,1},{3,2},{4,7},{5,4},{6,5},{7,6},{8,11},{9,8},{10,9... | collective-permute-start | bytes 786440 | tf_op jit(solution)/shard_map/ppermute | solution.py:38
  160.0 13.5 %collective-permute-start.27 = (bf16[128,1024]{1,0:T(8,128)(2,1)S(1)}, bf16[128,1024]{1,0:T(8,128)(2,1)S(1)}, u32[]{:S(2)}, u32[]{:S(2)}) collective-permute-start(bf16[128,1024]{1,0:T(8,128)(2,1)S(1)} %get-tuple-element.37), channel_id=1, source_target_pairs={{0,1},{1,2},{2,3},{3,0},{4,5},{5,6},{6,7},{7,4},{8,9},{9,10},{10,1... | collective-permute-start | bytes 786440 | tf_op jit(solution)/shard_map/ppermute | solution.py:38
  (12 other events, 31.8 us)
Sparse Core Ops, SparseCore 0:
  9.5 59.3 all-gather.2
